TPU v7x, 32 devices: a whole 2x2x4 slice. The times are simulated.
32 devices in a mesh: fsdp: 2 (over y), dp: 16 (over z, x, core).
Axes of the slice: x: 2, y: 2, z: 4, core: 2. Of those that a mesh axis runs over, the one named last changes fastest.
Arguments:
- doc_tokens: bfloat16 [32, 1024, 1024], P(('fsdp', 'dp')), may hold values from -6 to 6
- query_tokens: bfloat16 [64, 32, 1024], P(('fsdp', 'dp')), may hold values from -6 to 6
- doc_lengths: int32 [32], P(('fsdp', 'dp')), may hold values from 50 to 1024, as said below
- positives: int32 [64], P(('fsdp', 'dp')), may hold values from 0 to 31
- query_weight: bfloat16 [1024, 1024], P(('fsdp', 'dp')), may hold values from -0.1875 to 0.1875
- key_weight: bfloat16 [1024, 1024], P(('fsdp', 'dp')), may hold values from -0.1875 to 0.1875
- value_weight: bfloat16 [1024, 1024], P(('fsdp', 'dp')), may hold values from -0.1875 to 0.1875
- output_weight: bfloat16 [1024, 1024], P(('fsdp', 'dp')), may hold values from -0.75 to 0.75
- query_bias: bfloat16 [1024], P(('fsdp', 'dp')), may hold values from -3 to 3
- key_bias: bfloat16 [1024], P(('fsdp', 'dp')), may hold values from -3 to 3
- value_bias: bfloat16 [1024], P(('fsdp', 'dp')), may hold values from -3 to 3
- output_bias: bfloat16 [1024], P(('fsdp', 'dp')), may hold values from -3 to 3
- attn_gain: bfloat16 [1024], P(('fsdp', 'dp')), may hold values from 0.099609375 to 1.8984375
- attn_shift: bfloat16 [1024], P(('fsdp', 'dp')), may hold values from -3 to 3
- inner_weight: bfloat16 [1024, 4096], P(('fsdp', 'dp')), may hold values from -0.1875 to 0.1875
- inner_bias: bfloat16 [4096], P(('fsdp', 'dp')), may hold values from -3 to 3
- outer_weight: bfloat16 [4096, 1024], P(('fsdp', 'dp')), may hold values from -0.09375 to 0.09375
- outer_bias: bfloat16 [1024], P(('fsdp', 'dp')), may hold values from -3 to 3
- final_gain: bfloat16 [1024], P(('fsdp', 'dp')), may hold values from 0.099609375 to 1.8984375
- final_shift: bfloat16 [1024], P(('fsdp', 'dp')), may hold values from -3 to 3
- proj_weight: bfloat16 [1024, 128], P(('fsdp', 'dp')), may hold values from -0.1875 to 0.1875
Outputs:
- query_loss: float32 [64], P(('fsdp', 'dp'))
- doc_states: bfloat16 [32, 1024, 1024], P(('fsdp', 'dp'))
- query_states: bfloat16 [64, 32, 1024], P(('fsdp', 'dp'))
- doc_tokens_grad: float32 [32, 1024, 1024], P(('fsdp', 'dp'))
- query_tokens_grad: float32 [64, 32, 1024], P(('fsdp', 'dp'))
- query_weight_grad: float32 [1024, 1024], P(('fsdp', 'dp'))
- key_weight_grad: float32 [1024, 1024], P(('fsdp', 'dp'))
- value_weight_grad: float32 [1024, 1024], P(('fsdp', 'dp'))
- output_weight_grad: float32 [1024, 1024], P(('fsdp', 'dp'))
- query_bias_grad: float32 [1024], P(('fsdp', 'dp'))
- key_bias_grad: float32 [1024], P(('fsdp', 'dp'))
- value_bias_grad: float32 [1024], P(('fsdp', 'dp'))
- output_bias_grad: float32 [1024], P(('fsdp', 'dp'))
- attn_gain_grad: float32 [1024], P(('fsdp', 'dp'))
- attn_shift_grad: float32 [1024], P(('fsdp', 'dp'))
- inner_weight_grad: float32 [1024, 4096], P(('fsdp', 'dp'))
- inner_bias_grad: float32 [4096], P(('fsdp', 'dp'))
- outer_weight_grad: float32 [4096, 1024], P(('fsdp', 'dp'))
- outer_bias_grad: float32 [1024], P(('fsdp', 'dp'))
- final_gain_grad: float32 [1024], P(('fsdp', 'dp'))
- final_shift_grad: float32 [1024], P(('fsdp', 'dp'))
- proj_weight_grad: float32 [1024, 128], P(('fsdp', 'dp'))
Inputs may be any that keep to these rules, and one draw needn't show every extreme that they name: `doc_lengths`: tokens of a slot at or beyond its document's length are padding. Some document fills its whole slot of 1024 tokens.
All inputs are finite; a program needn't handle non-finite values.
Results may differ from a plain program's by a relative error of at most 0.04.
Values may be sent and summed in bfloat16 or wider, within the bound.
A program may use at most 256 MiB of HBM per device.

v0:
```python
import math

import jax
import jax.numpy as jnp
from jax import lax
from jax.sharding import PartitionSpec as P

HEADS = 16


norm_eps = 1e-05
unit_eps = 1e-06
sharpness_divisor = 0.0625
loss_scale = 256.0
masked_value = -1e30


def merged(value, axis, combine):
    everything = jax.tree.map(lambda part: lax.all_gather(part, axis), value)
    first = jax.tree.map(lambda part: part[0], everything)

    def turn(k, so_far):
        return combine(so_far, jax.tree.map(lambda part: part[k], everything))

    return lax.fori_loop(1, lax.axis_size(axis), turn, first)


def rotate_half(values):
    first_half, second_half = jnp.split(values, 2, axis=-1)
    return jnp.concatenate([-second_half, first_half], axis=-1)


def rotary_tables(length, head_size):
    position = jnp.arange(length).astype(jnp.float32)[:, None]
    channel = jnp.arange(head_size // 2).astype(jnp.float32)[None, :]
    angles = position * jnp.exp(channel * (-2.0 * math.log(10000.0) / head_size))
    angles = jnp.concatenate([angles, angles], axis=1)
    return (jnp.cos(angles), jnp.sin(angles))


def apply_rotary(values, cosine, sine_table):
    return values * cosine[:, None, :] + rotate_half(values) * sine_table[:, None, :]


def undo_rotary(gradient, cosine, sine_table):
    return gradient * cosine[:, None, :] - rotate_half(gradient * sine_table[:, None, :])


def gelu_value(values):
    return 0.5 * values * (1.0 + lax.erf(values * math.sqrt(0.5)))


def gelu_slope(values):
    return 0.5 * (1.0 + lax.erf(values * math.sqrt(0.5))) + values * jnp.exp(
        -0.5 * values * values
    ) * (1.0 / math.sqrt(2.0 * math.pi))


def dense_apply(operand, matrix):
    return jnp.einsum("bld,de->ble", operand, matrix, preferred_element_type=jnp.float32)


def dense_back(gradient, matrix):
    return jnp.einsum("ble,de->bld", gradient, matrix, preferred_element_type=jnp.float32)


def weight_grad(operand, gradient):
    return jnp.einsum("bld,ble->de", operand, gradient, preferred_element_type=jnp.float32)


def row_sum(values):
    return jnp.sum(values.astype(jnp.float32), axis=(0, 1))


def normalize_rows(values):
    center = jnp.mean(values, axis=-1, keepdims=True)
    centered = values - center
    variance = jnp.mean(centered * centered, axis=-1, keepdims=True)
    inverse_std = lax.rsqrt(variance + norm_eps)
    return (centered * inverse_std, inverse_std)


def norm_back(gradient, normal, inverse_std):
    return inverse_std * (
        gradient
        - jnp.mean(gradient, axis=-1, keepdims=True)
        - normal * jnp.mean(gradient * normal, axis=-1, keepdims=True)
    )


def head_pair(values, pair_start, head_size):
    batch_size, length, model_width = values.shape
    pair_block = lax.dynamic_slice_in_dim(values, pair_start, 2 * head_size, 2)
    return pair_block.reshape(batch_size, length, 2, head_size)


def pair_scores(query_pair, key_pair, key_valid):
    pairwise_dot_products = (
        jnp.einsum("bqhd,bkhd->bhqk", query_pair, key_pair, preferred_element_type=jnp.float32)
        * 0.125
    )
    return jnp.where(key_valid[:, None, None, :], pairwise_dot_products, masked_value)


def restack(stacked, batch_size, length, model_width):
    return jnp.moveaxis(stacked, 0, 2).reshape(batch_size, length, model_width)


def attend_forward(query_rot, key_rot, value_low, key_valid):
    batch_size, length, model_width = query_rot.shape
    head_size = model_width // HEADS

    def one_pair(unused, pair_index):
        pair_start = pair_index * 2 * head_size
        query_pair = head_pair(query_rot, pair_start, head_size)
        key_pair = head_pair(key_rot, pair_start, head_size)
        value_pair = head_pair(value_low, pair_start, head_size)
        pairwise_dot_products = pair_scores(query_pair, key_pair, key_valid)
        row_peak = jnp.max(pairwise_dot_products, axis=-1, keepdims=True)
        exponent = jnp.exp(pairwise_dot_products - row_peak)
        row_mass = jnp.sum(exponent, axis=-1, keepdims=True)
        weights = (exponent / row_mass).astype(jnp.bfloat16)
        mixed_pair = jnp.einsum(
            "bhqk,bkhd->bqhd", weights, value_pair, preferred_element_type=jnp.float32
        )
        log_mass = (row_peak + jnp.log(row_mass))[..., 0]
        return (unused, (mixed_pair.reshape(batch_size, length, 2 * head_size), log_mass))

    unused, (mixed_stack, log_mass) = lax.scan(
        one_pair, jnp.zeros((), jnp.float32), jnp.arange(HEADS // 2)
    )
    mixed_heads = restack(mixed_stack, batch_size, length, model_width)
    return (mixed_heads.astype(jnp.bfloat16), log_mass)


def attend_backward(query_rot, key_rot, value_low, key_valid, log_mass, mixed_grad):
    batch_size, length, model_width = query_rot.shape
    head_size = model_width // HEADS

    def one_pair(unused, inputs):
        pair_index, pair_mass = inputs
        pair_start = pair_index * 2 * head_size
        query_pair = head_pair(query_rot, pair_start, head_size)
        key_pair = head_pair(key_rot, pair_start, head_size)
        value_pair = head_pair(value_low, pair_start, head_size)
        grad_pair = head_pair(mixed_grad, pair_start, head_size)
        pairwise_dot_products = pair_scores(query_pair, key_pair, key_valid)
        normalized_exponential_weight = jnp.exp(pairwise_dot_products - pair_mass[..., None])
        grad_prob = jnp.einsum(
            "bqhd,bkhd->bhqk", grad_pair, value_pair, preferred_element_type=jnp.float32
        )
        row_dot = jnp.sum(normalized_exponential_weight * grad_prob, axis=-1, keepdims=True)
        logits_grad = (normalized_exponential_weight * (grad_prob - row_dot) * 0.125).astype(
            jnp.bfloat16
        )
        query_part = jnp.einsum(
            "bhqk,bkhd->bqhd", logits_grad, key_pair, preferred_element_type=jnp.float32
        )
        key_part = jnp.einsum(
            "bhqk,bqhd->bkhd", logits_grad, query_pair, preferred_element_type=jnp.float32
        )
        value_part = jnp.einsum(
            "bhqk,bqhd->bkhd",
            normalized_exponential_weight.astype(jnp.bfloat16),
            grad_pair,
            preferred_element_type=jnp.float32,
        )
        pair_shape = (batch_size, length, 2 * head_size)
        return (
            unused,
            (
                query_part.reshape(pair_shape),
                key_part.reshape(pair_shape),
                value_part.reshape(pair_shape),
            ),
        )

    unused, (query_stack, key_stack, value_stack) = lax.scan(
        one_pair, jnp.zeros((), jnp.float32), (jnp.arange(HEADS // 2), log_mass)
    )
    return (
        restack(query_stack, batch_size, length, model_width),
        restack(key_stack, batch_size, length, model_width),
        restack(value_stack, batch_size, length, model_width),
    )


def layer_forward(tokens, key_valid, attn_params, ffn_params):
    w_query, w_key, w_value, w_output, b_query, b_key, b_value, b_output, attn_gain, attn_shift = (
        attn_params
    )
    w_inner, b_inner, w_outer, b_outer, final_gain, final_shift, w_proj = ffn_params
    batch_size, length, model_width = tokens.shape
    head_size = model_width // HEADS
    cosine, sine_table = rotary_tables(length, head_size)

    def rotated(weight, bias):
        linear = dense_apply(tokens, weight) + bias.astype(jnp.float32)
        turned = apply_rotary(
            linear.reshape(batch_size, length, HEADS, head_size), cosine, sine_table
        )
        return turned.reshape(batch_size, length, model_width).astype(jnp.bfloat16)

    query_rot = rotated(w_query, b_query)
    key_rot = rotated(w_key, b_key)
    value_low = (dense_apply(tokens, w_value) + b_value.astype(jnp.float32)).astype(jnp.bfloat16)
    mixed_heads, log_mass = attend_forward(query_rot, key_rot, value_low, key_valid)
    attended = dense_apply(mixed_heads, w_output) + b_output.astype(jnp.float32)
    first_normal, first_inverse = normalize_rows(tokens.astype(jnp.float32) + attended)
    normed = first_normal * attn_gain.astype(jnp.float32) + attn_shift.astype(jnp.float32)
    normed_low = normed.astype(jnp.bfloat16)
    hidden = dense_apply(normed_low, w_inner) + b_inner.astype(jnp.float32)
    outer_branch = dense_apply(gelu_value(hidden).astype(jnp.bfloat16), w_outer) + b_outer.astype(
        jnp.float32
    )
    second_normal, second_inverse = normalize_rows(normed + outer_branch)
    states = second_normal * final_gain.astype(jnp.float32) + final_shift.astype(jnp.float32)
    states_low = states.astype(jnp.bfloat16)
    projected = dense_apply(states_low, w_proj)
    inverse_norm = lax.rsqrt(jnp.sum(projected * projected, axis=-1, keepdims=True) + unit_eps)
    encoded_token_arrays = (projected * inverse_norm).astype(jnp.bfloat16)
    kept_values = (
        query_rot,
        key_rot,
        value_low,
        log_mass,
        mixed_heads,
        first_normal,
        first_inverse,
        normed_low,
        hidden,
        second_normal,
        second_inverse,
        states_low,
        projected,
        inverse_norm,
    )
    return (states_low, encoded_token_arrays, kept_values)


def layer_backward(tokens, key_valid, attn_params, ffn_params, kept_values, vector_grad):
    w_query, w_key, w_value, w_output, b_query, b_key, b_value, b_output, attn_gain, attn_shift = (
        attn_params
    )
    w_inner, b_inner, w_outer, b_outer, final_gain, final_shift, w_proj = ffn_params
    (
        query_rot,
        key_rot,
        value_low,
        log_mass,
        mixed_heads,
        first_normal,
        first_inverse,
        normed_low,
        hidden,
        second_normal,
        second_inverse,
        states_low,
        projected,
        inverse_norm,
    ) = kept_values
    batch_size, length, model_width = tokens.shape
    head_size = model_width // HEADS
    cosine, sine_table = rotary_tables(length, head_size)
    radial = jnp.sum(vector_grad * projected, axis=-1, keepdims=True)
    proj_grad = (
        vector_grad * inverse_norm
        - projected * (inverse_norm * inverse_norm * inverse_norm) * radial
    ).astype(jnp.bfloat16)
    proj_weight_grad = weight_grad(states_low, proj_grad)
    states_grad = dense_back(proj_grad, w_proj)
    final_gain_grad = row_sum(states_grad * second_normal)
    final_shift_grad = row_sum(states_grad)
    second_grad = norm_back(
        states_grad * final_gain.astype(jnp.float32), second_normal, second_inverse
    )
    outer_grad = second_grad.astype(jnp.bfloat16)
    activated = gelu_value(hidden).astype(jnp.bfloat16)
    outer_weight_grad = weight_grad(activated, outer_grad)
    outer_bias_grad = row_sum(outer_grad)
    hidden_grad = (dense_back(outer_grad, w_outer) * gelu_slope(hidden)).astype(jnp.bfloat16)
    inner_weight_grad = weight_grad(normed_low, hidden_grad)
    inner_bias_grad = row_sum(hidden_grad)
    normed_grad = second_grad + dense_back(hidden_grad, w_inner)
    attn_gain_grad = row_sum(normed_grad * first_normal)
    attn_shift_grad = row_sum(normed_grad)
    first_grad = norm_back(normed_grad * attn_gain.astype(jnp.float32), first_normal, first_inverse)
    attended_grad = first_grad.astype(jnp.bfloat16)
    output_weight_grad = weight_grad(mixed_heads, attended_grad)
    output_bias_grad = row_sum(attended_grad)
    mixed_grad = dense_back(attended_grad, w_output).astype(jnp.bfloat16)
    query_back, key_back, value_back = attend_backward(
        query_rot, key_rot, value_low, key_valid, log_mass, mixed_grad
    )

    def unturned(gradient):
        reverted = undo_rotary(
            gradient.reshape(batch_size, length, HEADS, head_size), cosine, sine_table
        )
        return reverted.reshape(batch_size, length, model_width).astype(jnp.bfloat16)

    query_grad = unturned(query_back)
    key_grad = unturned(key_back)
    value_grad = value_back.astype(jnp.bfloat16)
    tokens_grad = (
        first_grad
        + dense_back(query_grad, w_query)
        + dense_back(key_grad, w_key)
        + dense_back(value_grad, w_value)
    )
    attn_grads = (
        weight_grad(tokens, query_grad),
        weight_grad(tokens, key_grad),
        weight_grad(tokens, value_grad),
        output_weight_grad,
        row_sum(query_grad),
        row_sum(key_grad),
        row_sum(value_grad),
        output_bias_grad,
        attn_gain_grad,
        attn_shift_grad,
    )
    ffn_grads = (
        inner_weight_grad,
        inner_bias_grad,
        outer_weight_grad,
        outer_bias_grad,
        final_gain_grad,
        final_shift_grad,
        proj_weight_grad,
    )
    return (tokens_grad, attn_grads, ffn_grads)


def local(
    doc_tokens,
    query_tokens,
    doc_lengths,
    positives,
    query_weight,
    key_weight,
    value_weight,
    output_weight,
    query_bias,
    key_bias,
    value_bias,
    output_bias,
    attn_gain,
    attn_shift,
    inner_weight,
    inner_bias,
    outer_weight,
    outer_bias,
    final_gain,
    final_shift,
    proj_weight,
):
    attn_params = (
        lax.all_gather(query_weight, ("fsdp", "dp"), axis=0, tiled=True),
        lax.all_gather(key_weight, ("fsdp", "dp"), axis=0, tiled=True),
        lax.all_gather(value_weight, ("fsdp", "dp"), axis=0, tiled=True),
        lax.all_gather(output_weight, ("fsdp", "dp"), axis=0, tiled=True),
        lax.all_gather(query_bias, ("fsdp", "dp"), axis=0, tiled=True),
        lax.all_gather(key_bias, ("fsdp", "dp"), axis=0, tiled=True),
        lax.all_gather(value_bias, ("fsdp", "dp"), axis=0, tiled=True),
        lax.all_gather(output_bias, ("fsdp", "dp"), axis=0, tiled=True),
        lax.all_gather(attn_gain, ("fsdp", "dp"), axis=0, tiled=True),
        lax.all_gather(attn_shift, ("fsdp", "dp"), axis=0, tiled=True),
    )
    ffn_params = (
        lax.all_gather(inner_weight, ("fsdp", "dp"), axis=0, tiled=True),
        lax.all_gather(inner_bias, ("fsdp", "dp"), axis=0, tiled=True),
        lax.all_gather(outer_weight, ("fsdp", "dp"), axis=0, tiled=True),
        lax.all_gather(outer_bias, ("fsdp", "dp"), axis=0, tiled=True),
        lax.all_gather(final_gain, ("fsdp", "dp"), axis=0, tiled=True),
        lax.all_gather(final_shift, ("fsdp", "dp"), axis=0, tiled=True),
        lax.all_gather(proj_weight, ("fsdp", "dp"), axis=0, tiled=True),
    )
    slot_length = doc_tokens.shape[1]
    local_queries = query_tokens.shape[0]
    query_len = query_tokens.shape[1]
    doc_valid = jnp.arange(slot_length)[None, :] < doc_lengths[:, None]
    query_valid = jnp.ones((local_queries, query_len), dtype=jnp.bool_)
    doc_states, doc_vectors, doc_kept = layer_forward(
        doc_tokens, doc_valid, attn_params, ffn_params
    )
    query_states, query_vectors, query_kept = layer_forward(
        query_tokens, query_valid, attn_params, ffn_params
    )
    vector_width = query_vectors.shape[2]
    all_rows, all_positives = (
        lax.all_gather(
            query_vectors.reshape(local_queries * query_len, vector_width),
            ("fsdp", "dp"),
            axis=0,
            tiled=True,
        ),
        lax.all_gather(positives, ("fsdp", "dp"), axis=0, tiled=True),
    )
    doc_rows = doc_vectors[0]
    key_mask = doc_valid[0]
    block_rows = 32 * query_len
    row_blocks = all_rows.reshape(-1, block_rows, vector_width)

    def block_scores(rows_block):
        pairwise_dot_products = (
            jnp.einsum("qe,ke->qk", rows_block, doc_rows, preferred_element_type=jnp.float32)
            / sharpness_divisor
        )
        return jnp.where(key_mask[None, :], pairwise_dot_products, masked_value)

    def smooth_block(unused, rows_block):
        pairwise_dot_products = block_scores(rows_block)
        row_peak = jnp.max(pairwise_dot_products, axis=1, keepdims=True)
        blurred_line_peaks = sharpness_divisor * (
            row_peak[:, 0] + jnp.log(jnp.sum(jnp.exp(pairwise_dot_products - row_peak), axis=1))
        )
        return (unused, blurred_line_peaks)

    unused, smooth = lax.scan(smooth_block, jnp.zeros((), jnp.float32), row_blocks)
    totals = smooth.reshape(-1, query_len).sum(axis=1)
    doc_index = lax.axis_index(("fsdp", "dp"))
    is_positive = all_positives == doc_index
    target_part = jnp.where(is_positive, totals, 0.0)

    def combine(earlier, later):
        row_peak = jnp.maximum(earlier[0], later[0])
        row_mass = earlier[1] * jnp.exp(earlier[0] - row_peak) + later[1] * jnp.exp(
            later[0] - row_peak
        )
        return (row_peak, row_mass, earlier[2] + later[2])

    peak_all, mass_all, target_all = merged(
        (totals, jnp.ones_like(totals), target_part), ("fsdp", "dp"), combine
    )
    log_total = peak_all + jnp.log(mass_all)
    losses_all = log_total - target_all
    query_loss = lax.dynamic_slice_in_dim(losses_all, doc_index * local_queries, local_queries, 0)
    coefficient = loss_scale * (jnp.exp(totals - log_total) - is_positive.astype(jnp.float32))
    token_coefficient = jnp.broadcast_to(coefficient[:, None], (coefficient.shape[0], query_len))
    token_coefficient = token_coefficient.reshape(row_blocks.shape[0], block_rows)

    def grad_block(doc_grad, inputs):
        rows_block, blurred_line_peaks, coefficient_rows = inputs
        pairwise_dot_products = block_scores(rows_block)
        normalized_exponential_weight = jnp.exp(
            pairwise_dot_products - (blurred_line_peaks / sharpness_divisor)[:, None]
        )
        score_grad = (normalized_exponential_weight * coefficient_rows[:, None]).astype(
            jnp.bfloat16
        )
        row_grad = jnp.einsum("qk,ke->qe", score_grad, doc_rows, preferred_element_type=jnp.float32)
        doc_grad = doc_grad + jnp.einsum(
            "qk,qe->ke", score_grad, rows_block, preferred_element_type=jnp.float32
        )
        return (doc_grad, row_grad)

    doc_vector_grad, row_grads = lax.scan(
        grad_block, jnp.zeros(doc_rows.shape, jnp.float32), (row_blocks, smooth, token_coefficient)
    )
    query_vector_grad = lax.psum_scatter(
        row_grads.reshape(-1, vector_width), ("fsdp", "dp"), scatter_dimension=0, tiled=True
    )
    attn_back = (
        lax.all_gather(query_weight, ("fsdp", "dp"), axis=0, tiled=True),
        lax.all_gather(key_weight, ("fsdp", "dp"), axis=0, tiled=True),
        lax.all_gather(value_weight, ("fsdp", "dp"), axis=0, tiled=True),
        lax.all_gather(output_weight, ("fsdp", "dp"), axis=0, tiled=True),
        lax.all_gather(query_bias, ("fsdp", "dp"), axis=0, tiled=True),
        lax.all_gather(key_bias, ("fsdp", "dp"), axis=0, tiled=True),
        lax.all_gather(value_bias, ("fsdp", "dp"), axis=0, tiled=True),
        lax.all_gather(output_bias, ("fsdp", "dp"), axis=0, tiled=True),
        lax.all_gather(attn_gain, ("fsdp", "dp"), axis=0, tiled=True),
        lax.all_gather(attn_shift, ("fsdp", "dp"), axis=0, tiled=True),
    )
    ffn_back = (
        lax.all_gather(inner_weight, ("fsdp", "dp"), axis=0, tiled=True),
        lax.all_gather(inner_bias, ("fsdp", "dp"), axis=0, tiled=True),
        lax.all_gather(outer_weight, ("fsdp", "dp"), axis=0, tiled=True),
        lax.all_gather(outer_bias, ("fsdp", "dp"), axis=0, tiled=True),
        lax.all_gather(final_gain, ("fsdp", "dp"), axis=0, tiled=True),
        lax.all_gather(final_shift, ("fsdp", "dp"), axis=0, tiled=True),
        lax.all_gather(proj_weight, ("fsdp", "dp"), axis=0, tiled=True),
    )
    doc_tokens_grad, doc_attn, doc_ffn = layer_backward(
        doc_tokens, doc_valid, attn_back, ffn_back, doc_kept, doc_vector_grad[None]
    )
    query_tokens_grad, query_attn, query_ffn = layer_backward(
        query_tokens,
        query_valid,
        attn_back,
        ffn_back,
        query_kept,
        query_vector_grad.reshape(local_queries, query_len, vector_width),
    )
    ffn_summed = jax.tree.map(jnp.add, doc_ffn, query_ffn)
    attn_summed = jax.tree.map(jnp.add, doc_attn, query_attn)
    ffn_shards = (
        lax.psum_scatter(ffn_summed[0], ("fsdp", "dp"), scatter_dimension=0, tiled=True),
        lax.psum_scatter(ffn_summed[1], ("fsdp", "dp"), scatter_dimension=0, tiled=True),
        lax.psum_scatter(ffn_summed[2], ("fsdp", "dp"), scatter_dimension=0, tiled=True),
        lax.psum_scatter(ffn_summed[3], ("fsdp", "dp"), scatter_dimension=0, tiled=True),
        lax.psum_scatter(ffn_summed[4], ("fsdp", "dp"), scatter_dimension=0, tiled=True),
        lax.psum_scatter(ffn_summed[5], ("fsdp", "dp"), scatter_dimension=0, tiled=True),
        lax.psum_scatter(ffn_summed[6], ("fsdp", "dp"), scatter_dimension=0, tiled=True),
    )
    attn_shards = (
        lax.psum_scatter(attn_summed[0], ("fsdp", "dp"), scatter_dimension=0, tiled=True),
        lax.psum_scatter(attn_summed[1], ("fsdp", "dp"), scatter_dimension=0, tiled=True),
        lax.psum_scatter(attn_summed[2], ("fsdp", "dp"), scatter_dimension=0, tiled=True),
        lax.psum_scatter(attn_summed[3], ("fsdp", "dp"), scatter_dimension=0, tiled=True),
        lax.psum_scatter(attn_summed[4], ("fsdp", "dp"), scatter_dimension=0, tiled=True),
        lax.psum_scatter(attn_summed[5], ("fsdp", "dp"), scatter_dimension=0, tiled=True),
        lax.psum_scatter(attn_summed[6], ("fsdp", "dp"), scatter_dimension=0, tiled=True),
        lax.psum_scatter(attn_summed[7], ("fsdp", "dp"), scatter_dimension=0, tiled=True),
        lax.psum_scatter(attn_summed[8], ("fsdp", "dp"), scatter_dimension=0, tiled=True),
        lax.psum_scatter(attn_summed[9], ("fsdp", "dp"), scatter_dimension=0, tiled=True),
    )
    return (
        query_loss,
        doc_states,
        query_states,
        doc_tokens_grad,
        query_tokens_grad,
        attn_shards[0],
        attn_shards[1],
        attn_shards[2],
        attn_shards[3],
        attn_shards[4],
        attn_shards[5],
        attn_shards[6],
        attn_shards[7],
        attn_shards[8],
        attn_shards[9],
        ffn_shards[0],
        ffn_shards[1],
        ffn_shards[2],
        ffn_shards[3],
        ffn_shards[4],
        ffn_shards[5],
        ffn_shards[6],
    )


def solution(mesh):
    in_specs = (
        P(("fsdp", "dp"), None, None),
        P(("fsdp", "dp"), None, None),
        P(("fsdp", "dp")),
        P(("fsdp", "dp")),
        P(("fsdp", "dp"), None),
        P(("fsdp", "dp"), None),
        P(("fsdp", "dp"), None),
        P(("fsdp", "dp"), None),
        P(("fsdp", "dp")),
        P(("fsdp", "dp")),
        P(("fsdp", "dp")),
        P(("fsdp", "dp")),
        P(("fsdp", "dp")),
        P(("fsdp", "dp")),
        P(("fsdp", "dp"), None),
        P(("fsdp", "dp")),
        P(("fsdp", "dp"), None),
        P(("fsdp", "dp")),
        P(("fsdp", "dp")),
        P(("fsdp", "dp")),
        P(("fsdp", "dp"), None),
    )
    out_specs = (
        P(("fsdp", "dp")),
        P(("fsdp", "dp"), None, None),
        P(("fsdp", "dp"), None, None),
        P(("fsdp", "dp"), None, None),
        P(("fsdp", "dp"), None, None),
        P(("fsdp", "dp"), None),
        P(("fsdp", "dp"), None),
        P(("fsdp", "dp"), None),
        P(("fsdp", "dp"), None),
        P(("fsdp", "dp")),
        P(("fsdp", "dp")),
        P(("fsdp", "dp")),
        P(("fsdp", "dp")),
        P(("fsdp", "dp")),
        P(("fsdp", "dp")),
        P(("fsdp", "dp"), None),
        P(("fsdp", "dp")),
        P(("fsdp", "dp"), None),
        P(("fsdp", "dp")),
        P(("fsdp", "dp")),
        P(("fsdp", "dp")),
        P(("fsdp", "dp"), None),
    )
    return jax.shard_map(local, mesh=mesh, in_specs=in_specs, out_specs=out_specs, check_vma=False)
```

profile of v0, /device:TPU:0, one launch (start us, length us, event | category | flops | bytes accessed | tf_op | source)
XLA Modules:
  0.0 2134.6 jit_solution(7582492643211112178)
XLA Ops:
  19.2 42.6 %all-reduce.24 = (bf16[1024]{0:T(1024)(128)(2,1)S(1)}, bf16[1024]{0:T(1024)(128)(2,1)S(1)}, bf16[1024]{0:T(1024)(128)(2,1)S(1)}, bf16[1024]{0:T(1024)(128)(2,1)S...) all-reduce(bf16[1024]{0:T(1024)(128)(2,1)S(1)} %dynamic-update-slic, ...), channel_id=1, replica_groups=mesh['fsdp'=2,'dp'=16] {'fsdp','dp'}, use_global_device_ids=true, to_apply=%add.3 | all-reduce | flops 9216 | bytes 36864
  67.0 40.3 %all-gather.2 = bf16[32,1,128]{2,1,0:T(2,128)(2,1)S(1)} all-gather(bf16[1,1,128]{2,1,0:T(2,128)(2,1)S(1)} %bitcast.618), channel_id=1, replica_groups=mesh['fsdp'=2,'dp'=16] {'fsdp','dp'}, dimensions={0}, use_global_device_ids=true | all-gather | bytes 8448 | tf_op jit(solution)/shard_map/all_gather | solution.py:372
  109.2 40.3 %all_gather.95 = bf16[1024,128]{1,0:T(8,128)(2,1)} all-gather(bf16[32,128]{1,0:T(8,128)(2,1)S(1)} %copy-done.107), channel_id=1, replica_groups=mesh['fsdp'=2,'dp'=16] {'fsdp','dp'}, dimensions={0}, use_global_device_ids=true | all-gather | bytes 270336 | tf_op jit(solution)/shard_map/all_gather | solution.py:377
  150.8 38.6 %all-reduce.10 = s32[64]{0:T(128)} all-reduce(s32[64]{0:T(128)S(1)} %dynamic-update-slice.10), channel_id=1, replica_groups=mesh['fsdp'=2,'dp'=16] {'fsdp','dp'}, use_global_device_ids=true, to_apply=%add.10 | all-reduce | flops 64 | bytes 512
  225.4 21.5 %while.106 = (s32[]{:T(128)}, bf16[8,2,32,128]{3,2,1,0:T(8,128)(2,1)S(1)}, f32[8,2,2,32]{3,2,1,0:T(2,128)}, s32[8]{0:T(128)S(1)}, bf16[2,32,1024]{2,1,0:T(8,128)...) while((s32[]{:T(128)}, ...), condition=%wide.region_3.4_spmd, body=%wide.region_0.3_spmd.sunk | while | flops 1077126 | bytes 415923 | solution.py:129
  267.4 86.4 %while.108 = (s32[]{:T(128)}, bf16[8,1,1024,128]{2,3,1,0:T(8,128)(2,1)S(1)}, f32[8,1,2,1024]{3,2,1,0:T(2,128)}, s32[8]{0:T(128)S(1)}, bf16[1,1024,1024]{1,2,0:T(...) while((s32[]{:T(128)}, ...), condition=%wide.region_12.13_spmd.clone, body=%wide.region_9.12_spmd.clone.sunk | while | flops 562035712 | bytes 28381888 | solution.py:129
  362.2 20.2 multiply_convert_fusion.2
  382.4 19.4 all-gather.20.cloned.1.call-done
  401.8 15.3 fusion.280
  433.2 40.6 %all_gather.96 = bf16[2048,128]{1,0:T(8,128)(2,1)S(1)} all-gather(bf16[64,128]{1,0:T(8,128)(2,1)S(1)} %bitcast.617), channel_id=1, replica_groups=mesh['fsdp'=2,'dp'=16] {'fsdp','dp'}, dimensions={0}, use_global_device_ids=true | all-gather | bytes 540672 | tf_op jit(solution)/shard_map/all_gather | solution.py:392
  479.4 37.2 %all-reduce.23 = (f32[2048]{0:T(1024)S(1)}, f32[2048]{0:T(1024)S(1)}) all-reduce(f32[2048]{0:T(1024)S(1)} %dynamic-update-slice.9, f32[2048]{0:T(1024)S(1)} %fusion.258), channel_id=2, replica_groups=mesh['fsdp'=2,'dp'=16] {'fsdp','dp'}, use_global_device_ids=true, to_apply=%add.9 | all-reduce | flops 4096 | bytes 32768
  553.3 21.4 %convert_reduce_fusion = (f32[4096]{0:T(1024)}, bf16[1024,4096]{1,0:T(8,128)(2,1)}) fusion(f32[1024,4096]{1,0:T(8,128)} %get-tuple-element.1236, f32[4096]{0:T(1024)S(1)} %bitcast.616, bf16[4096,1024]{1,0:T(8,128)(2,1)} %all-gather.20.cloned.1.call-done, f32[1,1024,1024]{1,2,0:T(8,128)S(1)} %get-tuple-element.1157), kind=kOutput, calls=%fused_computation.142 | convolution fusion | flops 8645505024 | bytes 37781504 | tf_op jit(solution)/shard_map/ble,de->bld/dot_general | solution.py:64
  599.0 437.9 %while.110 = (s32[]{:T(128)}, f32[8,1,1024,128]{2,3,1,0:T(8,128)}, f32[8,1,1024,128]{2,3,1,0:T(8,128)}, bf16[8,1,1024,128]{2,3,1,0:T(8,128)(2,1)S(1)}, s32[8]{0:...) while((s32[]{:T(128)}, f32[8,1,1024,128]{2,3,1,0:T(8,128)}, ...), condition=%wide.region_34.35_spmd.clone, body=%wide.region_32.34_spmd.clone.sunk | while | flops 1396710400 | bytes 67154656 | solution.py:178
  615.2 15.2 fusion.435
  630.4 16.2 fusion.434
  670.0 15.2 fusion.435
  685.2 16.1 fusion.434
  724.7 15.2 fusion.435
  739.8 16.1 fusion.434
  794.4 16.1 fusion.434
  849.0 16.1 fusion.434
  903.7 16.1 fusion.434
  958.3 16.1 fusion.434
  997.8 15.2 fusion.435
  1012.9 16.1 fusion.434
  1079.5 154.7 %while.107 = (s32[]{:T(128)}, f32[8,2,32,128]{3,0,2,1:T(8,128)}, f32[8,2,32,128]{3,0,2,1:T(8,128)}, bf16[8,2,32,128]{3,2,1,0:T(8,128)(2,1)}, s32[8]{0:T(128)S(1)...) while((s32[]{:T(128)}, f32[8,2,32,128]{3,0,2,1:T(8,128)}, ...), condition=%wide.region_43.44_spmd, body=%wide.region_41.43_spmd.sunk | while | flops 2675012 | bytes 1067219 | solution.py:178
  1398.8 43.7 %all-reduce.22 = (f32[1024]{0:T(1024)S(1)}, f32[1024]{0:T(1024)S(1)}, f32[1024]{0:T(1024)S(1)}, f32[1024]{0:T(1024)S(1)}, f32[1024]{0:T(1024)S(1)}, /*index=5*/f...) all-reduce(f32[1024]{0:T(1024)S(1)} %add_bitcast_fusion.2, ...), channel_id=9, replica_groups=mesh['fsdp'=2,'dp'=16] {'fsdp','dp'}, use_global_device_ids=true, to_apply=%region_50.51.clone | all-reduce | flops 13312 | bytes 106496
  1454.6 22.2 %reduce-scatter.29.cloned.1.call-done = f32[32,1024]{1,0:T(8,128)} async-done(((f32[1024,1024]{1,0:T(8,128)}), f32[32,1024]{1,0:T(8,128)}) %reduce-scatter.29.cloned.1.call-update) | async-done | bytes 131088
  1476.8 141.6 %reduce-scatter.27.cloned.1.call-done = f32[32,1024]{1,0:T(8,128)} async-done(((f32[1024,1024]{1,0:T(8,128)}), f32[32,1024]{1,0:T(8,128)}) %reduce-scatter.27.cloned.1.call-update) | async-done | bytes 131088
  1618.5 141.9 %reduce-scatter.25.cloned.1.call-done = f32[32,1024]{1,0:T(8,128)} async-done(((f32[1024,1024]{1,0:T(8,128)}), f32[32,1024]{1,0:T(8,128)}) %reduce-scatter.25.cloned.1.call-update) | async-done | bytes 131088
  1760.3 182.7 %reduce-scatter.21.cloned.1.call-done = f32[128,1024]{1,0:T(8,128)} async-done(((f32[4096,1024]{1,0:T(8,128)}), f32[128,1024]{1,0:T(8,128)}) %reduce-scatter.21.cloned.1.call-update) | async-done | bytes 524304 | tf_op jit(solution)/shard_map/reduce_scatter | solution.py:501
  1943.0 184.8 %reduce-scatter.19.cloned.1.call-done = f32[32,4096]{1,0:T(8,128)} async-done(((f32[1024,4096]{1,0:T(8,128)}), f32[32,4096]{1,0:T(8,128)}) %reduce-scatter.19.cloned.1.call-update) | async-done | bytes 524304 | tf_op jit(solution)/shard_map/reduce_scatter | solution.py:499
  (994 shorter events, 887.0 us)
Async XLA Ops:
  7.2 182.2 %all-gather.12.cloned.1.call-start = ((), (), s32[]{:S(2)}) async-start(), calls=%async_computation.9 | async-start | bytes 2162688 | tf_op jit(solution)/shard_map/all_gather | solution.py:359
  7.9 190.5 %all-gather.14.cloned.1.call-start = ((), (), s32[]{:S(2)}) async-start(), calls=%async_computation.10 | async-start | bytes 2162688 | tf_op jit(solution)/shard_map/all_gather | solution.py:360
  8.7 198.1 %all-gather.10.cloned.1.call-start = ((), (), s32[]{:S(2)}) async-start(), calls=%async_computation.8 | async-start | bytes 2162688 | tf_op jit(solution)/shard_map/all_gather | solution.py:361
  9.4 237.6 %all-gather.16.cloned.1.call-start = ((), (), s32[]{:S(2)}) async-start(), calls=%async_computation.11 | async-start | bytes 2162688 | tf_op jit(solution)/shard_map/all_gather | solution.py:362
  10.0 352.2 %all-gather.18.cloned.1.call-start = ((), (), s32[]{:S(2)}) async-start(), calls=%async_computation.12 | async-start | bytes 8650752 | tf_op jit(solution)/shard_map/all_gather | solution.py:371
  10.6 391.2 %all-gather.20.cloned.1.call-start = ((), (), s32[]{:S(2)}) async-start(), calls=%async_computation.13 | async-start | bytes 8650752 | tf_op jit(solution)/shard_map/all_gather | solution.py:373
  11.1 1037.5 %reduce-scatter.15.cloned.1.call-start = ((), (), s32[]{:S(2)}) async-start(), calls=%async_computation.14 | async-start | bytes 1081344 | tf_op jit(solution)/shard_map/reduce_scatter | solution.py:461
  11.5 182.5 %copy-start.8 = (bf16[8,1,1024,128]{2,3,1,0:T(8,128)(2,1)}, bf16[8,1,1024,128]{2,3,1,0:T(8,128)(2,1)S(1)}, u32[]{:S(2)}) copy-start(bf16[8,1,1024,128]{2,3,1,0:T(8,128)(2,1)S(1)} %fusion.276) | copy-start | bytes 6291460
  62.8 194.3 %copy-start.41 = (f32[1024,64]{0,1:T(8,128)}, f32[1024,64]{0,1:T(8,128)S(1)}, u32[]{:S(2)}) copy-start(f32[1024,64]{0,1:T(8,128)S(1)} %get-tuple-element.1215) | copy-start | bytes 786436
  62.8 194.2 %copy-start.52 = (f32[1024,64]{0,1:T(8,128)}, f32[1024,64]{0,1:T(8,128)S(1)}, u32[]{:S(2)}) copy-start(f32[1024,64]{0,1:T(8,128)S(1)} %get-tuple-element.1216) | copy-start | bytes 786436
  62.8 144.0 %copy-start.102 = (f32[1024]{0:T(1024)}, f32[1024]{0:T(1024)S(1)}, u32[]{:S(2)}) copy-start(f32[1024]{0:T(1024)S(1)} %convert_element_type.406) | copy-start | bytes 12292
  62.8 46.3 %copy-start.107 = (bf16[32,128]{1,0:T(8,128)(2,1)S(1)}, bf16[32,128]{1,0:T(8,128)(2,1)}, u32[]{:S(2)}) copy-start(bf16[32,128]{1,0:T(8,128)(2,1)} %param.55) | copy-start | bytes 24580
  62.9 87.8 %copy-start.111 = (s32[2]{0:T(128)S(1)}, s32[2]{0:T(128)}, u32[]{:S(2)}) copy-start(s32[2]{0:T(128)} %param.38) | copy-start | bytes 28
  67.0 359.4 %copy-start.76 = (f32[1024]{0:T(1024)}, f32[1024]{0:T(1024)S(1)}, u32[]{:S(2)}) copy-start(f32[1024]{0:T(1024)S(1)} %convert_element_type.418) | copy-start | bytes 12292
  149.8 73.7 %copy-start.72 = (f32[32,1024]{1,0:T(8,128)}, f32[32,1024]{1,0:T(8,128)S(1)}, u32[]{:S(2)}) copy-start(f32[32,1024]{1,0:T(8,128)S(1)} %mul.849) | copy-start | bytes 393220
  249.8 176.6 %copy-start.21 = (f32[2,32,1024]{2,1,0:T(8,128)}, f32[2,32,1024]{2,1,0:T(8,128)S(1)}, u32[]{:S(2)}) copy-start(f32[2,32,1024]{2,1,0:T(8,128)S(1)} %get-tuple-element.1228) | copy-start | bytes 786436
  249.8 176.6 %copy-start.83 = (f32[2,32]{1,0:T(2,128)}, f32[2,32]{1,0:T(2,128)S(1)}, u32[]{:S(2)}) copy-start(f32[2,32]{1,0:T(2,128)S(1)} %broadcast_multiply_fusion.17) | copy-start | bytes 772
  250.0 176.4 %copy-start.85 = (f32[2,32]{1,0:T(2,128)}, f32[2,32]{1,0:T(2,128)S(1)}, u32[]{:S(2)}) copy-start(f32[2,32]{1,0:T(2,128)S(1)} %add_rsqrt_fusion.5) | copy-start | bytes 772
  359.7 228.5 %copy-start.93 = (f32[1024]{0:T(1024)}, f32[1024]{0:T(1024)S(1)}, u32[]{:S(2)}) copy-start(f32[1024]{0:T(1024)S(1)} %broadcast_multiply_fusion.11) | copy-start | bytes 12292
  362.1 226.0 %copy-start.100 = (f32[1024]{0:T(1024)}, f32[1024]{0:T(1024)S(1)}, u32[]{:S(2)}) copy-start(f32[1024]{0:T(1024)S(1)} %add_rsqrt_fusion.2) | copy-start | bytes 12292
  426.5 47.4 %copy-start.87 = (f32[2,1024]{1,0:T(2,128)S(1)}, f32[2,1024]{1,0:T(2,128)}, u32[]{:S(2)}) copy-start(f32[2,1024]{1,0:T(2,128)} %custom-call.6) | copy-start | bytes 24580
  473.8 45.1 %copy-start.5 = (f32[1024,128]{1,0:T(8,128)S(1)}, f32[1024,128]{1,0:T(8,128)}, u32[]{:S(2)}) copy-start(f32[1024,128]{1,0:T(8,128)} %custom-call.1) | copy-start | bytes 1572868
  547.7 906.9 %reduce-scatter.23.cloned.1.call-start = ((), (), s32[]{:S(2)}) async-start(), calls=%async_computation.18 | async-start | bytes 540672 | tf_op jit(solution)/shard_map/reduce_scatter | solution.py:505
  1055.8 398.8 %reduce-scatter.17.cloned.1.call-start = ((), (), s32[]{:S(2)}) async-start(), calls=%async_computation.15 | async-start | bytes 4325376 | tf_op jit(solution)/shard_map/reduce_scatter | solution.py:511
  1075.7 401.1 %reduce-scatter.29.cloned.1.call-start = ((), (), s32[]{:S(2)}) async-start(), calls=%async_computation.21 | async-start | bytes 4325376
  1244.7 373.8 %reduce-scatter.27.cloned.1.call-start = ((), (), s32[]{:S(2)}) async-start(), calls=%async_computation.20 | async-start | bytes 4325376
  1294.8 465.5 %reduce-scatter.25.cloned.1.call-start = ((), (), s32[]{:S(2)}) async-start(), calls=%async_computation.19 | async-start | bytes 4325376
  1307.9 635.1 %reduce-scatter.21.cloned.1.call-start = ((), (), s32[]{:S(2)}) async-start(), calls=%async_computation.17 | async-start | bytes 17301504 | tf_op jit(solution)/shard_map/reduce_scatter | solution.py:501
  1329.3 798.6 %reduce-scatter.19.cloned.1.call-start = ((), (), s32[]{:S(2)}) async-start(), calls=%async_computation.16 | async-start | bytes 17301504 | tf_op jit(solution)/shard_map/reduce_scatter | solution.py:499
  1389.6 61.1 %copy-start.54 = (f32[2,32,1024]{2,1,0:T(8,128)S(1)}, f32[2,32,1024]{2,1,0:T(8,128)}, u32[]{:S(2)}) copy-start(f32[2,32,1024]{2,1,0:T(8,128)} %copy-done.53) | copy-start | bytes 786436
  1389.6 61.2 %copy-start.68 = (bf16[2,32,1024]{2,1,0:T(8,128)(2,1)S(1)}, bf16[2,32,1024]{2,1,0:T(8,128)(2,1)}, u32[]{:S(2)}) copy-start(bf16[2,32,1024]{2,1,0:T(8,128)(2,1)} %get-tuple-element.1213) | copy-start | bytes 393220
  1389.6 63.5 %copy-start.20 = (bf16[1024,1024]{1,0:T(8,128)(2,1)S(1)}, bf16[1024,1024]{1,0:T(8,128)(2,1)}, u32[]{:S(2)}) copy-start(bf16[1024,1024]{1,0:T(8,128)(2,1)} %all-gather.10.cloned.1.call-done) | copy-start | bytes 6291460
  (96 other events, 837.5 us)
Sparse Core Ops, SparseCore 0:
  10.8 59.4 all-gather.11
  73.1 55.2 all-gather.13
  131.2 55.4 all-gather.9
  189.4 55.0 all-gather.15
  247.2 76.0 all-gather.17
  326.0 75.7 all-gather.19
  547.8 137.7 reduce-scatter.14
  1055.9 137.2 reduce-scatter.22
  1196.1 138.5 reduce-scatter.16
  1337.4 139.3 reduce-scatter.28
  1479.7 138.7 reduce-scatter.26
  1621.2 139.1 reduce-scatter.24
  1763.2 179.7 reduce-scatter.20
  1945.8 182.0 reduce-scatter.18
where the time goes:
time: 2150 us; the launch traced here: 2130 us
  waiting for transfers between devices  696 us (32%)
  matrix products  680 us (32%)
  local copies, waits for them, and re-layouts  293 us (14%)
  blocking collectives  283 us (13%)
  other arithmetic  142 us (7%)
  loops' own time  23.9 us (1%)
    unnamed x17, waiting for transfers between devices  309 us
    reduce_scatter x1, waiting for transfers between devices, local(): lax.psum_scatter(ffn_summed[0], ('fsdp', 'dp'), scatter_dimension=0, tile...  185 us
    reduce_scatter x1, waiting for transfers between devices, local(): lax.psum_scatter(ffn_summed[2], ('fsdp', 'dp'), scatter_dimension=0, tile...  183 us
    unnamed x4, blocking collectives  162 us
    dot_general x16, matrix products, one_pair(): jnp.einsum('bhqk,bqhd->bkhd', logits_grad, query_pair, preferred_element_...  143 us
    dot_general x16, matrix products, one_pair(): jnp.einsum('bhqk,bkhd->bqhd', logits_grad, key_pair, preferred_element_ty...  135 us
    dot_general x14, matrix products, weight_grad(): jnp.einsum('bld,ble->de', operand, gradient, preferred_element_type=jnp.f...  79.7 us
    dot_general x14, matrix products, dense_back(): jnp.einsum('ble,de->bld', gradient, matrix, preferred_element_type=jnp.fl...  77.5 us
  transfers between devices with their start and end apart: 14, of which 6 were waited for; matrix products, arithmetic and copies ran while one was open for 48% of the time, Pallas kernels for 0%

commit v1 on v0

v1 whole, which is shorter than its diff:
```python
import functools
import math

import jax
import jax.numpy as jnp
import numpy as np
from jax import lax
from jax.experimental import pallas as pl
from jax.experimental.pallas import tpu as pltpu
from jax.sharding import PartitionSpec as P

HEADS = 16
HEAD = 64
AXES = ("fsdp", "dp")
MESH = pl.DeviceIdType.MESH
f32 = jnp.float32
bf16 = jnp.bfloat16
norm_eps = 1e-05
unit_eps = 1e-06
sharpness_divisor = 0.0625
loss_scale = 256.0
masked_value = -1e30
score_scale = 0.125 * math.log2(math.e)
vmem_bytes = 62 * 1024 * 1024


def nt(a, b):
    return lax.dot_general(a, b, (((1,), (1,)), ((), ())), preferred_element_type=f32)


def nn(a, b):
    return lax.dot_general(a, b, (((1,), (0,)), ((), ())), preferred_element_type=f32)


def tn(a, b):
    return lax.dot_general(a, b, (((0,), (0,)), ((), ())), preferred_element_type=f32)


def lane_of(shape):
    return lax.broadcasted_iota(jnp.int32, shape, 1)


def row_of(shape):
    return lax.broadcasted_iota(jnp.int32, shape, 0)


def wide(table):
    return jnp.concatenate([table, table], axis=1)


def rope(values, cosine, signed_sine):
    width = values.shape[1]
    turned = jnp.where(
        lane_of(values.shape) % HEAD < HEAD // 2,
        pltpu.roll(values, width - HEAD // 2, 1),
        pltpu.roll(values, HEAD // 2, 1),
    )
    return values * cosine + turned * signed_sine


def rope_back(gradient, cosine, signed_sine):
    width = gradient.shape[1]
    scaled = gradient * signed_sine
    turned = jnp.where(
        lane_of(gradient.shape) % HEAD < HEAD // 2,
        pltpu.roll(scaled, width - HEAD // 2, 1),
        pltpu.roll(scaled, HEAD // 2, 1),
    )
    return gradient * cosine + turned


def heads_apart(values, heads):
    rows = values.shape[0]
    tall = jnp.concatenate([values] * heads, axis=0)
    keep = (row_of(tall.shape) // rows) == (lane_of(tall.shape) // HEAD)
    return jnp.where(keep, tall, jnp.zeros_like(tall))


def heads_joined(values, heads):
    rows = values.shape[0] // heads
    keep = (row_of(values.shape) // rows) == (lane_of(values.shape) // HEAD)
    values = jnp.where(keep, values, 0.0)
    total = values[0:rows]
    for h in range(1, heads):
        total = total + values[h * rows : (h + 1) * rows]
    return total


def question_probs(apart, key, question):
    rows = key.shape[0]
    scores = nt(apart, key) * 0.125
    same = (row_of(scores.shape) % rows) // question == lane_of(scores.shape) // question
    scores = jnp.where(same, scores, masked_value)
    weight = jnp.exp(scores - jnp.max(scores, axis=1, keepdims=True))
    return weight / jnp.sum(weight, axis=1, keepdims=True)


def attend_step(slot, question, length_ref, tokens_ref, wq_ref, wk_ref, wv_ref, bias_ref, cos_ref, sin_ref, q_ref, k_ref, v_ref, mixed_ref, mass_ref):
    tokens = tokens_ref[...]
    cosine = wide(cos_ref[...])
    sine = wide(sin_ref[...])
    q_ref[...] = rope(nn(tokens, wq_ref[...]) + bias_ref[0:1, :].astype(f32), cosine, sine).astype(bf16)
    k_ref[...] = rope(nn(tokens, wk_ref[...]) + bias_ref[1:2, :].astype(f32), cosine, sine).astype(bf16)
    v_ref[...] = (nn(tokens, wv_ref[...]) + bias_ref[2:3, :].astype(f32)).astype(bf16)
    total = tokens.shape[0]
    length = length_ref[0]
    pair = (slot, 2 * HEAD)
    lane = lane_of(pair)
    mask = jnp.where(row_of(pair) < length, 0.0, masked_value).astype(bf16)
    for p in range(2):
        cols = slice(p * 2 * HEAD, (p + 1) * 2 * HEAD)
        query = q_ref[0:slot, cols]
        key = k_ref[0:slot, cols]
        value = v_ref[0:slot, cols]
        parts = []
        masses = []
        for h in range(2):
            mine = (lane // HEAD) == h
            spare = (1 - h) * HEAD
            query_h = jnp.where(mine, query, jnp.where(lane == spare, 1.0, 0.0).astype(bf16))
            key_h = jnp.where(lane == spare, mask, key)
            value_h = jnp.where(mine, value, jnp.ones_like(value))
            scores = nt(query_h, key_h)
            peak = jnp.max(scores, axis=1, keepdims=True)
            weight = jnp.exp2((scores - peak) * score_scale).astype(bf16)
            mixed = nn(weight, value_h)
            parts.append(mixed / pltpu.roll(mixed, HEAD, 1))
            masses.append(peak * score_scale + jnp.log2(mixed))
        mixed_ref[0:slot, cols] = jnp.where(lane < HEAD, parts[0], parts[1]).astype(bf16)
        turned = jnp.where(lane < HEAD, masses[1], masses[0]).T
        mass_ref[0, 2 * p : 2 * p + 1, 0:slot] = turned[HEAD : HEAD + 1, :]
        mass_ref[0, 2 * p + 1 : 2 * p + 2, 0:slot] = turned[0:1, :]
    rest = slice(slot, total)
    weight = question_probs(heads_apart(q_ref[rest, :], 4), k_ref[rest, :], question)
    mixed_ref[rest, :] = heads_joined(nn(weight.astype(bf16), v_ref[rest, :]), 4).astype(bf16)


def group_spec(rows):
    return pl.BlockSpec((rows, 4 * HEAD), lambda i: (0, i))


def whole_spec(shape):
    return pl.BlockSpec(shape, lambda i: (0,) * len(shape))


def mass_spec(total):
    return pl.BlockSpec((1, 8, total), lambda i: (i, 0, 0))


def attend_forward(length, tokens, wq, wk, wv, biases, cosine, sine, slot, question):
    total, width = tokens.shape
    groups = width // (4 * HEAD)
    return pl.pallas_call(
        functools.partial(attend_step, slot, question),
        grid=(groups,),
        in_specs=[
            pl.BlockSpec(memory_space=pltpu.SMEM),
            whole_spec((total, width)),
            group_spec(width),
            group_spec(width),
            group_spec(width),
            group_spec(8),
            whole_spec((total, 2 * HEAD)),
            whole_spec((total, 2 * HEAD)),
        ],
        out_specs=[group_spec(total)] * 4 + [mass_spec(total)],
        out_shape=[jax.ShapeDtypeStruct((total, width), bf16)] * 4
        + [jax.ShapeDtypeStruct((groups, 8, total), f32)],
        compiler_params=pltpu.CompilerParams(vmem_limit_bytes=vmem_bytes),
        name="attend_forward",
    )(length, tokens, wq, wk, wv, biases, cosine, sine)


def attend_back_step(slot, question, length_ref, q_ref, k_ref, v_ref, mixed_ref, grad_ref, mass_ref, cos_ref, sin_ref, dq_ref, dk_ref, dv_ref):
    total = q_ref.shape[0]
    length = length_ref[0]
    pair = (slot, 2 * HEAD)
    lane = lane_of(pair)
    mask = jnp.where(row_of(pair) < length, 0.0, masked_value).astype(bf16)
    cosine = cos_ref[0:slot, :]
    sine = sin_ref[0:slot, :]
    for p in range(2):
        cols = slice(p * 2 * HEAD, (p + 1) * 2 * HEAD)
        query = q_ref[0:slot, cols]
        key = k_ref[0:slot, cols]
        value = v_ref[0:slot, cols]
        grad = grad_ref[0:slot, cols]
        key_turned = key.T
        product = (grad.astype(f32) * mixed_ref[0:slot, cols].astype(f32)).T
        dq = []
        dk = []
        dv = []
        for h in range(2):
            mine = (lane // HEAD) == h
            spare = (1 - h) * HEAD
            query_h = jnp.where(mine, query, jnp.where(lane == spare, 1.0, 0.0).astype(bf16))
            key_h = jnp.where(lane == spare, mask, key)
            value_h = jnp.where(mine, value, jnp.zeros_like(value))
            row_dot = jnp.sum(product[h * HEAD : (h + 1) * HEAD], axis=0, keepdims=True)
            mass = mass_ref[0, 2 * p + h : 2 * p + h + 1, 0:slot]
            probs = jnp.exp2(nt(key_h, query_h) * score_scale - mass)
            slope = (probs * (nt(value_h, grad) - row_dot)).astype(bf16)
            dv.append(nn(probs.astype(bf16), grad))
            dk.append(nn(slope, query))
            dq.append(nn(key_turned[h * HEAD : (h + 1) * HEAD], slope))
        dq_all = jnp.concatenate(dq, axis=0).T * 0.125
        dk_all = jnp.where(lane < HEAD, dk[0], dk[1]) * 0.125
        dq_ref[0:slot, cols] = rope_back(dq_all, cosine, sine).astype(bf16)
        dk_ref[0:slot, cols] = rope_back(dk_all, cosine, sine).astype(bf16)
        dv_ref[0:slot, cols] = jnp.where(lane < HEAD, dv[0], dv[1]).astype(bf16)
    rest = slice(slot, total)
    cosine = wide(cos_ref[rest, :])
    sine = wide(sin_ref[rest, :])
    apart = heads_apart(q_ref[rest, :], 4)
    grad_apart = heads_apart(grad_ref[rest, :], 4)
    key = k_ref[rest, :]
    probs = question_probs(apart, key, question)
    grad_prob = nt(grad_apart, v_ref[rest, :])
    row_dot = jnp.sum(probs * grad_prob, axis=1, keepdims=True)
    slope = (probs * (grad_prob - row_dot) * 0.125).astype(bf16)
    dq_ref[rest, :] = rope_back(heads_joined(nn(slope, key), 4), cosine, sine).astype(bf16)
    dk_ref[rest, :] = rope_back(tn(slope, apart), cosine, sine).astype(bf16)
    dv_ref[rest, :] = tn(probs.astype(bf16), grad_apart).astype(bf16)


def attend_backward(length, q, k, v, mixed, grad, mass, cosine, sine, slot, question):
    total, width = q.shape
    groups = width // (4 * HEAD)
    return pl.pallas_call(
        functools.partial(attend_back_step, slot, question),
        grid=(groups,),
        in_specs=[pl.BlockSpec(memory_space=pltpu.SMEM)]
        + [group_spec(total)] * 5
        + [mass_spec(total), whole_spec((total, 2 * HEAD)), whole_spec((total, 2 * HEAD))],
        out_specs=[group_spec(total)] * 3,
        out_shape=[jax.ShapeDtypeStruct((total, width), bf16)] * 3,
        compiler_params=pltpu.CompilerParams(vmem_limit_bytes=vmem_bytes),
        name="attend_backward",
    )(length, q, k, v, mixed, grad, mass, cosine, sine)


class Place:
    def __init__(self):
        y = lax.axis_index("fsdp")
        d = lax.axis_index("dp")
        z, x, c = d // 4, (d // 2) % 2, d % 2
        self.y, self.z, self.x, self.c = y, z, x, c
        x1, y1 = (1 - c) * (1 - x) + c * x, c * (1 - y) + (1 - c) * y
        x2, y2 = c * (1 - x) + (1 - c) * x, (1 - c) * (1 - y) + c * y
        self.first = (y1, z * 4 + x1 * 2 + c)
        self.second = (y2, z * 4 + x2 * 2 + c)
        self.twin = (y, z * 4 + x * 2 + (1 - c))
        self.along = [(y, ((z + k) % 4) * 4 + x * 2 + c) for k in (1, 2, 3)]
        self.lines = [(y, x), (y1, x1), (y2, x2), (1 - y, 1 - x)]

    def greet(self):
        barrier = pltpu.get_barrier_semaphore()
        peers = [self.first, self.second, self.twin] + self.along
        for peer in peers:
            pl.semaphore_signal(barrier, inc=1, device_id=peer, device_id_type=MESH)
        pl.semaphore_wait(barrier, len(peers))


class Sender:
    def __init__(self):
        self.sent = []

    def go(self, src, dst, send_sem, recv_sem, device):
        copy = pltpu.make_async_remote_copy(
            src_ref=src,
            dst_ref=dst,
            send_sem=send_sem,
            recv_sem=recv_sem,
            device_id=device,
            device_id_type=MESH,
        )
        copy.start()
        self.sent.append(copy)

    def drain(self):
        for copy in self.sent:
            copy.wait_send()


def arrived(ref, sem):
    pltpu.make_async_copy(ref, ref, sem).wait()


class Gather:
    def __init__(self, place, shards, wholes, send_sem, recv_sem, own_sem):
        self.at, self.shards, self.wholes = place, shards, wholes
        self.send_sem, self.recv_sem, self.own_sem = send_sem, recv_sem, own_sem
        self.out = Sender()

    def line(self, t, k, core):
        y, x = self.at.lines[k]
        return self.wholes[t].at[y, :, x, core]

    def own(self, t):
        at = self.at
        return pltpu.make_async_copy(
            self.shards[t], self.wholes[t].at[at.y, at.z, at.x, at.c], self.own_sem.at[t]
        )

    def begin(self, t):
        at = self.at
        for k, peer in enumerate(at.along):
            self.out.go(
                self.shards[t],
                self.wholes[t].at[at.y, at.z, at.x, at.c],
                self.send_sem.at[t, k],
                self.recv_sem.at[t, 0],
                peer,
            )
        self.own(t).start()

    def pass_line(self, t, k, targets):
        line = self.line(t, k, self.at.c)
        for send, recv, peer in targets:
            self.out.go(line, line, self.send_sem.at[t, send], self.recv_sem.at[t, recv], peer)

    def own_line(self, t):
        at = self.at
        arrived(self.wholes[t].at[at.y, 0:3, at.x, at.c], self.recv_sem.at[t, 0])
        self.own(t).wait()
        self.pass_line(t, 0, [(3, 1, at.first), (4, 2, at.second), (5, 4, at.twin)])

    def first_line(self, t):
        at = self.at
        arrived(self.line(t, 1, at.c), self.recv_sem.at[t, 1])
        self.pass_line(t, 1, [(6, 3, at.second), (7, 5, at.twin)])

    def second_line(self, t):
        arrived(self.line(t, 2, self.at.c), self.recv_sem.at[t, 2])
        self.pass_line(t, 2, [(8, 6, self.at.twin)])

    def far_line(self, t):
        arrived(self.line(t, 3, self.at.c), self.recv_sem.at[t, 3])
        self.pass_line(t, 3, [(9, 7, self.at.twin)])

    def twin_lines(self, t):
        for k in range(4):
            arrived(self.line(t, k, 1 - self.at.c), self.recv_sem.at[t, 4 + k])


def gather_body(count, *refs):
    shards, wholes = refs[:count], refs[count : 2 * count]
    place = Place()
    place.greet()
    run = Gather(place, shards, wholes, *refs[2 * count :])
    for t in range(count):
        run.begin(t)
    for s in range(count + 2):
        if s < count:
            run.own_line(s)
        if 0 <= s - 1 < count:
            run.first_line(s - 1)
            run.second_line(s - 1)
        if 0 <= s - 2 < count:
            run.far_line(s - 2)
    for t in range(count):
        run.twin_lines(t)
    run.out.drain()


def gather(shards, collective_id):
    count = len(shards)
    wholes = pl.pallas_call(
        functools.partial(gather_body, count),
        in_specs=[pl.BlockSpec(memory_space=pltpu.VMEM)] * count,
        out_specs=[pl.BlockSpec(memory_space=pl.ANY)] * count,
        out_shape=[jax.ShapeDtypeStruct((2, 4, 2, 2) + a.shape, a.dtype) for a in shards],
        scratch_shapes=[
            pltpu.SemaphoreType.DMA((count, 10)),
            pltpu.SemaphoreType.DMA((count, 8)),
            pltpu.SemaphoreType.DMA((count,)),
        ],
        compiler_params=pltpu.CompilerParams(
            collective_id=collective_id, has_side_effects=True, vmem_limit_bytes=vmem_bytes
        ),
        name="gather",
    )(*shards)
    return [w.reshape((32 * a.shape[0],) + a.shape[1:]) for w, a in zip(wholes, shards)]


class Scatter:
    twin_slot = (0, 2, 1, 3)

    def __init__(self, place, parts, outs, buffers, send_sem, recv_sem, own_sem):
        self.at, self.parts, self.outs, self.buffers = place, parts, outs, buffers
        self.send_sem, self.recv_sem, self.own_sem = send_sem, recv_sem, own_sem
        self.out = Sender()

    def own(self, t, k):
        y, x = self.at.lines[k]
        return pltpu.make_async_copy(
            self.parts[t].at[y, :, x, self.at.c], self.buffers[t][0].at[k], self.own_sem.at[t, k]
        )

    def begin(self, t):
        at = self.at
        for k in (3, 2, 1, 0):
            y, x = at.lines[k]
            slot = self.twin_slot[k]
            self.out.go(
                self.parts[t].at[y, :, x, 1 - at.c],
                self.buffers[t][1].at[slot],
                self.send_sem.at[t, k],
                self.recv_sem.at[t, slot],
                at.twin,
            )
            self.own(t, k).start()

    def join_twin(self, t, k):
        total, twin = self.buffers[t][:2]
        self.own(t, k).wait()
        arrived(twin.at[k], self.recv_sem.at[t, k])
        total[k] = total[k] + twin[k]

    def to_second(self, t):
        total, second = self.buffers[t][0], self.buffers[t][2]
        self.join_twin(t, 3)
        self.out.go(total.at[3], second.at[1], self.send_sem.at[t, 4], self.recv_sem.at[t, 5], self.at.second)
        self.join_twin(t, 2)
        self.out.go(total.at[2], second.at[0], self.send_sem.at[t, 5], self.recv_sem.at[t, 4], self.at.second)
        self.join_twin(t, 1)
        self.join_twin(t, 0)

    def to_first(self, t):
        total, second, first = self.buffers[t][0], self.buffers[t][2], self.buffers[t][3]
        arrived(second.at[1], self.recv_sem.at[t, 5])
        total[1] = total[1] + second[1]
        self.out.go(total.at[1], first, self.send_sem.at[t, 6], self.recv_sem.at[t, 6], self.at.first)
        arrived(second.at[0], self.recv_sem.at[t, 4])
        total[0] = total[0] + second[0]

    def to_line(self, t):
        total, first, last = self.buffers[t][0], self.buffers[t][3], self.buffers[t][4]
        arrived(first, self.recv_sem.at[t, 6])
        total[0] = total[0] + first[...]
        for k, peer in enumerate(self.at.along):
            self.out.go(
                total.at[0, (self.at.z + k + 1) % 4],
                last.at[k],
                self.send_sem.at[t, 7 + k],
                self.recv_sem.at[t, 7 + k],
                peer,
            )

    def finish(self, t):
        total, last = self.buffers[t][0], self.buffers[t][4]
        for k in range(3):
            arrived(last.at[k], self.recv_sem.at[t, 7 + k])
        self.outs[t][...] = (total[0, self.at.z].astype(f32) + last[0].astype(f32)) + (
            last[1].astype(f32) + last[2].astype(f32)
        )


def scatter_buffers(shape, dtype):
    return [
        pltpu.VMEM((4, 4) + shape, dtype),
        pltpu.VMEM((4, 4) + shape, dtype),
        pltpu.VMEM((2, 4) + shape, dtype),
        pltpu.VMEM((4,) + shape, dtype),
        pltpu.VMEM((3,) + shape, dtype),
    ]


def scatter_body(count, *refs):
    parts, outs = refs[:count], refs[count : 2 * count]
    flat = refs[2 * count : 7 * count]
    buffers = [flat[5 * t : 5 * t + 5] for t in range(count)]
    place = Place()
    place.greet()
    run = Scatter(place, parts, outs, buffers, *refs[7 * count :])
    for t in range(count):
        run.begin(t)
    for s in range(count + 3):
        if s < count:
            run.to_second(s)
        if 0 <= s - 1 < count:
            run.to_first(s - 1)
        if 0 <= s - 2 < count:
            run.to_line(s - 2)
        if 0 <= s - 3 < count:
            run.finish(s - 3)
    run.out.drain()


def scatter(parts, collective_id):
    count = len(parts)
    shapes = [(p.shape[0] // 32, p.shape[1]) for p in parts]
    scratch = []
    for p, shape in zip(parts, shapes):
        scratch += scatter_buffers(shape, p.dtype)
    return pl.pallas_call(
        functools.partial(scatter_body, count),
        in_specs=[pl.BlockSpec(memory_space=pl.ANY)] * count,
        out_specs=[pl.BlockSpec(memory_space=pltpu.VMEM)] * count,
        out_shape=[jax.ShapeDtypeStruct(shape, f32) for shape in shapes],
        scratch_shapes=scratch
        + [
            pltpu.SemaphoreType.DMA((count, 10)),
            pltpu.SemaphoreType.DMA((count, 10)),
            pltpu.SemaphoreType.DMA((count, 4)),
        ],
        compiler_params=pltpu.CompilerParams(
            collective_id=collective_id, has_side_effects=True, vmem_limit_bytes=vmem_bytes
        ),
        name="scatter",
    )(*[p.reshape((2, 4, 2, 2) + shape) for p, shape in zip(parts, shapes)])


def rotary_tables(slot, question, count):
    place = np.concatenate([np.arange(slot)] + [np.arange(question)] * count)
    channel = np.arange(HEAD // 2, dtype=np.float32)[None, :]
    rate = np.exp(channel * np.float32(-2.0 * math.log(10000.0) / HEAD))
    angle = place.astype(np.float32)[:, None] * rate
    cosine, sine = np.cos(angle), np.sin(angle)
    return (
        jnp.asarray(np.concatenate([cosine] * 4, axis=1)),
        jnp.asarray(np.concatenate([-sine, sine] * 2, axis=1)),
    )


def dense(operand, matrix):
    return jnp.einsum("ld,de->le", operand, matrix, preferred_element_type=f32)


def dense_back(gradient, matrix):
    return jnp.einsum("le,de->ld", gradient, matrix, preferred_element_type=f32)


def weight_grad(operand, gradient):
    return jnp.einsum("ld,le->de", operand, gradient, preferred_element_type=f32).astype(bf16)


def row_sum(values):
    return jnp.sum(values.astype(f32), axis=0)


def normalize_rows(values):
    center = jnp.mean(values, axis=-1, keepdims=True)
    centered = values - center
    variance = jnp.mean(centered * centered, axis=-1, keepdims=True)
    inverse_std = lax.rsqrt(variance + norm_eps)
    return (centered * inverse_std, inverse_std)


def norm_back(gradient, normal, inverse_std):
    return inverse_std * (
        gradient
        - jnp.mean(gradient, axis=-1, keepdims=True)
        - normal * jnp.mean(gradient * normal, axis=-1, keepdims=True)
    )


def gelu_both(values):
    half = 0.5 * (1.0 + lax.erf(values * math.sqrt(0.5)))
    bell = jnp.exp(-0.5 * values * values) * (1.0 / math.sqrt(2.0 * math.pi))
    return (values * half, half + values * bell)


def padded(rows, lanes):
    return jnp.pad(rows, ((0, 0), (0, lanes - rows.shape[1])))


class Close:
    def weights(self, matrices, vectors, wide_vector, positives):
        lanes = wide_vector.shape[0]
        rows = jnp.concatenate(
            [wide_vector[None], padded(jnp.stack(vectors), lanes), padded(positives.astype(bf16)[None], lanes)]
        )
        pack = jnp.pad(rows, ((0, 16 - rows.shape[0]), (0, 0)))
        *wholes, packs = gather(list(matrices) + [pack], 0)
        packs = packs.reshape(32, 16, lanes)
        count, size = len(vectors), vectors[0].shape[0]
        small = packs[:, 1 : 1 + count, :size].transpose(1, 0, 2).reshape(count, 32 * size)
        chosen = packs[:, 1 + count, : positives.shape[0]].reshape(-1).astype(jnp.int32)
        return wholes, small, packs[:, 0].reshape(-1), chosen

    def rows(self, rows):
        return gather([rows], 1)[0]

    def totals(self, totals):
        block = jnp.broadcast_to(padded(totals[None], 128), (8, 128))
        return gather([block], 2)[0].reshape(32, 8, 128)[:, 0, : totals.shape[0]]

    def row_grads(self, grads):
        return scatter([grads], 3)[0]

    def grads(self, matrices, vectors, wide_vector):
        count, size = len(vectors), vectors[0].shape[0] // 32
        lanes = wide_vector.shape[0] // 32
        small = jnp.stack(vectors).reshape(count, 32, size).transpose(1, 0, 2)
        small = jnp.pad(small, ((0, 0), (0, 15 - count), (0, lanes - size)))
        pack = jnp.concatenate([wide_vector.reshape(32, 1, lanes), small], axis=1)
        *shards, packed = scatter(list(matrices) + [pack.reshape(32 * 16, lanes)], 4)
        return shards, [packed[1 + i, :size] for i in range(count)], packed[0]


class Far:
    def one(self, value):
        return lax.all_gather(value, AXES, axis=0, tiled=True)

    def back(self, value):
        return lax.psum_scatter(value.astype(f32), AXES, scatter_dimension=0, tiled=True)

    def weights(self, matrices, vectors, wide_vector, positives):
        return (
            [self.one(m) for m in matrices],
            jnp.stack([self.one(v) for v in vectors]),
            self.one(wide_vector),
            self.one(positives),
        )

    def rows(self, rows):
        return self.one(rows)

    def totals(self, totals):
        return self.one(totals[None])

    def row_grads(self, grads):
        return self.back(grads)

    def grads(self, matrices, vectors, wide_vector):
        return [self.back(m) for m in matrices], [self.back(v) for v in vectors], self.back(wide_vector)


def local(
    link,
    doc_tokens,
    query_tokens,
    doc_lengths,
    positives,
    query_weight,
    key_weight,
    value_weight,
    output_weight,
    query_bias,
    key_bias,
    value_bias,
    output_bias,
    attn_gain,
    attn_shift,
    inner_weight,
    inner_bias,
    outer_weight,
    outer_bias,
    final_gain,
    final_shift,
    proj_weight,
):
    slot, width = doc_tokens.shape[1:]
    count, question = query_tokens.shape[:2]
    tokens = jnp.concatenate([doc_tokens[0], query_tokens.reshape(count * question, width)])
    cosine, sine = rotary_tables(slot, question, count)

    matrices, vectors, b_inner, chosen = link.weights(
        [query_weight, key_weight, value_weight, output_weight, inner_weight, outer_weight, proj_weight],
        [
            query_bias,
            key_bias,
            value_bias,
            output_bias,
            attn_gain,
            attn_shift,
            outer_bias,
            final_gain,
            final_shift,
        ],
        inner_bias,
        positives,
    )
    w_query, w_key, w_value, w_output, w_inner, w_outer, w_proj = matrices
    b_output, g_attn, s_attn, b_outer, g_final, s_final = [vectors[i].astype(f32) for i in range(3, 9)]

    query_rot, key_rot, value_low, mixed, mass = attend_forward(
        doc_lengths, tokens, w_query, w_key, w_value, vectors[0:8], cosine, sine, slot, question
    )
    attended = dense(mixed, w_output) + b_output
    first_normal, first_inverse = normalize_rows(tokens.astype(f32) + attended)
    normed = first_normal * g_attn + s_attn
    normed_low = normed.astype(bf16)
    activated, slope = gelu_both(dense(normed_low, w_inner) + b_inner.astype(f32))
    activated = activated.astype(bf16)
    slope = slope.astype(bf16)
    outer_branch = dense(activated, w_outer) + b_outer
    second_normal, second_inverse = normalize_rows(normed + outer_branch)
    states_low = (second_normal * g_final + s_final).astype(bf16)
    projected = dense(states_low, w_proj)
    inverse_norm = lax.rsqrt(jnp.sum(projected * projected, axis=-1, keepdims=True) + unit_eps)
    encoded = (projected * inverse_norm).astype(bf16)

    doc_rows = encoded[:slot]
    all_rows = link.rows(encoded[slot:])
    key_mask = jnp.arange(slot)[None, :] < doc_lengths[0]
    vector_width = encoded.shape[1]
    block_rows = 32 * question
    row_blocks = all_rows.reshape(-1, block_rows, vector_width)

    def block_scores(rows_block):
        scores = jnp.einsum("qe,ke->qk", rows_block, doc_rows, preferred_element_type=f32)
        return jnp.where(key_mask, scores / sharpness_divisor, masked_value)

    def smooth_block(unused, rows_block):
        scores = block_scores(rows_block)
        peak = jnp.max(scores, axis=1, keepdims=True)
        return unused, sharpness_divisor * (
            peak[:, 0] + jnp.log(jnp.sum(jnp.exp(scores - peak), axis=1))
        )

    unused, smooth = lax.scan(smooth_block, jnp.zeros((), f32), row_blocks)
    totals = smooth.reshape(-1, question).sum(axis=1)
    doc_index = lax.axis_index(AXES)
    all_totals = link.totals(totals)
    peak = jnp.max(all_totals, axis=0)
    log_total = peak + jnp.log(jnp.sum(jnp.exp(all_totals - peak), axis=0))
    hit = jnp.arange(all_totals.shape[0])[:, None] == chosen[None, :]
    losses = log_total - jnp.sum(jnp.where(hit, all_totals, 0.0), axis=0)
    query_loss = lax.dynamic_slice_in_dim(losses, doc_index * count, count, 0)
    coefficient = loss_scale * (jnp.exp(totals - log_total) - (chosen == doc_index).astype(f32))
    token_coefficient = jnp.broadcast_to(coefficient[:, None], (coefficient.shape[0], question))
    token_coefficient = token_coefficient.reshape(row_blocks.shape[0], block_rows)

    def grad_block(doc_grad, inputs):
        rows_block, smooth_rows, coefficient_rows = inputs
        weight = jnp.exp(block_scores(rows_block) - (smooth_rows / sharpness_divisor)[:, None])
        score_grad = (weight * coefficient_rows[:, None]).astype(bf16)
        row_grad = jnp.einsum("qk,ke->qe", score_grad, doc_rows, preferred_element_type=f32)
        doc_grad = doc_grad + jnp.einsum("qk,qe->ke", score_grad, rows_block, preferred_element_type=f32)
        return doc_grad, row_grad

    doc_vector_grad, row_grads = lax.scan(
        grad_block, jnp.zeros(doc_rows.shape, f32), (row_blocks, smooth, token_coefficient)
    )
    query_vector_grad = link.row_grads(row_grads.reshape(-1, vector_width))
    vector_grad = jnp.concatenate([doc_vector_grad, query_vector_grad])

    radial = jnp.sum(vector_grad * projected, axis=-1, keepdims=True)
    proj_grad = (
        vector_grad * inverse_norm - projected * (inverse_norm * inverse_norm * inverse_norm) * radial
    ).astype(bf16)
    proj_weight_grad = weight_grad(states_low, proj_grad)
    states_grad = dense_back(proj_grad, w_proj)
    final_gain_grad = row_sum(states_grad * second_normal)
    final_shift_grad = row_sum(states_grad)
    second_grad = norm_back(states_grad * g_final, second_normal, second_inverse)
    outer_grad = second_grad.astype(bf16)
    outer_weight_grad = weight_grad(activated, outer_grad)
    outer_bias_grad = row_sum(outer_grad)
    hidden_grad = (dense_back(outer_grad, w_outer) * slope.astype(f32)).astype(bf16)
    inner_weight_grad = weight_grad(normed_low, hidden_grad)
    inner_bias_grad = row_sum(hidden_grad)
    normed_grad = second_grad + dense_back(hidden_grad, w_inner)
    attn_gain_grad = row_sum(normed_grad * first_normal)
    attn_shift_grad = row_sum(normed_grad)
    first_grad = norm_back(normed_grad * g_attn, first_normal, first_inverse)
    attended_grad = first_grad.astype(bf16)
    output_weight_grad = weight_grad(mixed, attended_grad)
    output_bias_grad = row_sum(attended_grad)
    mixed_grad = dense_back(attended_grad, w_output).astype(bf16)
    query_grad, key_grad, value_grad = attend_backward(
        doc_lengths, query_rot, key_rot, value_low, mixed, mixed_grad, mass, cosine, sine, slot, question
    )
    tokens_grad = (
        first_grad
        + dense_back(query_grad, w_query)
        + dense_back(key_grad, w_key)
        + dense_back(value_grad, w_value)
    )
    shards, small, inner_bias_shard = link.grads(
        [
            outer_weight_grad,
            inner_weight_grad,
            proj_weight_grad,
            output_weight_grad,
            weight_grad(tokens, query_grad),
            weight_grad(tokens, key_grad),
            weight_grad(tokens, value_grad),
        ],
        [
            row_sum(query_grad),
            row_sum(key_grad),
            row_sum(value_grad),
            output_bias_grad,
            attn_gain_grad,
            attn_shift_grad,
            outer_bias_grad,
            final_gain_grad,
            final_shift_grad,
        ],
        inner_bias_grad,
    )
    outer_shard, inner_shard, proj_shard, output_shard, query_shard, key_shard, value_shard = shards
    return (
        query_loss,
        states_low[None, :slot],
        states_low[slot:].reshape(count, question, width),
        tokens_grad[None, :slot],
        tokens_grad[slot:].reshape(count, question, width),
        query_shard,
        key_shard,
        value_shard,
        output_shard,
        *small[:6],
        inner_shard,
        inner_bias_shard,
        outer_shard,
        *small[6:],
        proj_shard,
    )


def solution(mesh):
    row = P(AXES)
    flat = P(AXES, None)
    deep = P(AXES, None, None)
    in_specs = (deep, deep, row, row) + (flat,) * 4 + (row,) * 6 + (flat, row, flat, row, row, row, flat)
    out_specs = (row, deep, deep, deep, deep) + (flat,) * 4 + (row,) * 6 + (flat, row, flat, row, row, row, flat)
    link = Close() if (mesh.shape["fsdp"], mesh.shape["dp"]) == (2, 16) else Far()
    return jax.shard_map(
        functools.partial(local, link), mesh=mesh, in_specs=in_specs, out_specs=out_specs, check_vma=False
    )
```

time: 2150 us -> 665 us (0.31)
  waiting for transfers between devices: 696 us -> 0 us
  matrix products: 680 us -> 160 us
  Pallas kernels: 0 us -> 425 us
  blocking collectives: 283 us -> 0 us
  local copies, waits for them, and re-layouts: 293 us -> 28.3 us
  other arithmetic: 142 us -> 36.8 us
  loops' own time: 23.9 us -> 0.57 us
    dot_general x162 -> x26, matrix products: 680 us -> 160 us  [the longest x7 57 us: dense_back(): return jnp.einsum('le,de->ld', gradient, matrix, preferred_element_type=f32)]
    pallas_call x0 -> x7, Pallas kernels: none -> 425 us  [the longest x3 170 us: gather(): pl.pallas_call(functools.partial(gather_body, count), in_specs=[pl.BlockS...]
    reduce_scatter x5 -> x0, waiting for transfers between devices: 368 us -> none  [the longest x1 185 us: local(): lax.psum_scatter(ffn_summed[0], ('fsdp', 'dp'), scatter_dimension=0, tile...]
    unnamed x17 -> x0, waiting for transfers between devices: 309 us -> none
    unnamed x4 -> x0, blocking collectives: 162 us -> none
    all_gather x3 -> x0, blocking collectives: 121 us -> none  [the longest x1 40.6 us: local(): lax.all_gather(query_vectors.reshape(local_queries * query_len, vector_wi...]
    dynamic_slice x121 -> x1, local copies, waits for them, and re-layouts: 80.2 us -> 1.24 us  [local(): query_loss = lax.dynamic_slice_in_dim(losses, doc_index * count, count, 0)]
    unnamed x269 -> x74, local copies, waits for them, and re-layouts: 66.9 us -> 11 us
  transfers between devices with their start and end apart: 14 -> 0, of which waited for: 6 -> 0; matrix products, arithmetic and copies ran while one was open for 48% -> 0% of each run, Pallas kernels for 0% -> 0%
where the time goes in v1:
time: 665 us; the launch traced here: 654 us
  Pallas kernels  425 us (64%)
  matrix products  160 us (24%)
  other arithmetic  36.8 us (6%)
  local copies, waits for them, and re-layouts  28.3 us (4%)
    pallas_call x3, Pallas kernels, gather(): pl.pallas_call(functools.partial(gather_body, count), in_specs=[pl.BlockS...  170 us
    pallas_call x2, Pallas kernels, scatter(): pl.pallas_call(functools.partial(scatter_body, count), in_specs=[pl.Block...  169 us
    dot_general x7, matrix products, dense_back(): return jnp.einsum('le,de->ld', gradient, matrix, preferred_element_type=f32)  57 us
    pallas_call x1, Pallas kernels, attend_backward(): pl.pallas_call(functools.partial(attend_back_step, slot, question), grid=...  50.3 us
    dot_general x7, matrix products, weight_grad(): jnp.einsum('ld,le->de', operand, gradient, preferred_element_type=f32)  50.3 us
    dot_general x4, matrix products, dense(): return jnp.einsum('ld,de->le', operand, matrix, preferred_element_type=f32)  44.9 us
    pallas_call x1, Pallas kernels, attend_forward(): pl.pallas_call(functools.partial(attend_step, slot, question), grid=(grou...  36.1 us

profile of v1, /device:TPU:0, one launch (start us, length us, event | category | flops | bytes accessed | tf_op | source)
XLA Modules:
  0.0 653.7 jit_solution(2581050058069731442)
XLA Ops:
  4.1 135.8 %gather.3 = (bf16[2,4,2,2,32,1024]{5,4,3,2,1,0:T(8,128)(2,1)}, bf16[2,4,2,2,32,1024]{5,4,3,2,1,0:T(8,128)(2,1)}, bf16[2,4,2,2,32,1024]{5,4,3,2,1,0:T(8,128)(2,1)...) custom-call(bf16[32,1024]{1,0:T(8,128)(2,1)} %refs_0_.1, ...), custom_call_target="tpu_custom_call" | custom-call | tf_op jit(solution)/shard_map/gather/pallas_call | solution.py:368
  141.6 3.2 pad_maximum_fusion.tokens_ref
  145.5 36.1 %attend_forward.1 = (bf16[1088,1024]{1,0:T(8,128)(2,1)}, bf16[1088,1024]{1,0:T(8,128)(2,1)}, bf16[1088,1024]{1,0:T(8,128)(2,1)}, bf16[1088,1024]{1,0:T(8,128)(2,1)}, f32[4,8,1088]{2,1,0:T(8,128)}) custom-call(s32[1]{0:T(128)S(6)} %copy.80.length_ref, bf16[1088,1024]{1,0:T(8,128)(2,1)} %pad_maximum_fusion.tokens_ref, bf16[1024,1024]{1,0:T(8,128)(2,1)} %bitcast.158, ...), custom_call_target="tpu_custom_call" | custom-call | tf_op jit(solution)/shard_map/attend_forward/pallas_call | solution.py:153
  181.6 7.6 %fusion.37 = (f32[1088]{0:T(1024)S(1)}, f32[1088,1024]{1,0:T(8,128)}) fusion(f32[1024]{0:T(1024)S(1)} %reshape.337, bf16[1088,1024]{1,0:T(8,128)(2,1)} %get-tuple-element.120.mixed_ref, bf16[1024,1024]{1,0:T(8,128)(2,1)} %bitcast.210, bf16[64,1024]{1,0:T(8,128)(2,1)S(1)} %bitcast.183, bf16[1024,1024]{1,0:T(8,128)(2,1)} %bitcast.165), kind=kOutput, calls=%fused_computation.133 | convolution fusion | flops 2289499136 | bytes 11018496 | tf_op jit(solution)/shard_map/ld,de->le/dot_general | solution.py:527
  189.3 2.9 multiply_reduce_fusion.5
  193.1 19.1 %multiply_convert_fusion.1 = (bf16[1088,4096]{1,0:T(8,128)(2,1)}, f32[1088,4096]{1,0:T(8,128)}) fusion(f32[4096]{0:T(1024)S(1)} %bitcast.192, bf16[1024,4096]{1,0:T(8,128)(2,1)} %bitcast.204, f32[1088,1024]{1,0:T(8,128)} %get-tuple-element.252, f32[1024]{0:T(1024)S(1)} %reshape.339, f32[1024]{0:T(1024)S(1)} %reshape.338, f32[1088]{0:T(1024)S(1)} %add_rsqrt_fusion.2, ...), kind=kOutput, calls=%fused_computation.33 | convolution fusion | flops 9159114752 | bytes 39617024 | tf_op jit(solution)/shard_map/ld,de->le/dot_general | solution.py:527
  212.3 17.3 %fusion.38 = (f32[1088]{0:T(1024)S(1)}, f32[1088,1024]{1,0:T(8,128)}) fusion(f32[1024]{0:T(1024)S(1)} %reshape.341, bf16[1088,4096]{1,0:T(8,128)(2,1)} %get-tuple-element.253, bf16[4096,1024]{1,0:T(8,128)(2,1)} %bitcast.206, f32[1024]{0:T(1024)S(1)} %reshape.339, f32[1024]{0:T(1024)S(1)} %reshape.338, f32[1088]{0:T(1024)S(1)} %add_rsqrt_fusion.2, ...), kind=kOutput, calls=%fused_computation.134 | convolution fusion | flops 9134603264 | bytes 26239744 | tf_op jit(solution)/shard_map/ld,de->le/dot_general | solution.py:527
  229.6 2.9 multiply_reduce_fusion.4
  232.6 3.0 add_convert_fusion
  239.3 20.7 %gather.4 = bf16[2,4,2,2,64,128]{5,4,3,2,1,0:T(8,128)(2,1)S(1)} custom-call(bf16[64,128]{1,0:T(8,128)(2,1)} %slice.127.refs_0_), custom_call_target="tpu_custom_call" | custom-call | tf_op jit(solution)/shard_map/gather/pallas_call | solution.py:368
  260.0 4.8 while.24
  265.6 13.5 %gather.5 = f32[2,4,2,2,8,128]{5,4,3,2,1,0:T(8,128)} custom-call(f32[8,128]{1,0:T(8,128)} %broadcast_in_dim.104.refs_0_), custom_call_target="tpu_custom_call" | custom-call | tf_op jit(solution)/shard_map/gather/pallas_call | solution.py:368
  282.1 8.7 %while.25 = (s32[]{:T(128)}, f32[1024,128]{1,0:T(8,128)S(1)}, f32[2,1024,128]{2,1,0:T(8,128)}, bf16[2,1024,128]{2,1,0:T(8,128)(2,1)S(1)}, bf16[1024,128]{1,0:T(8...) while((s32[]{:T(128)}, f32[1024,128]{1,0:T(8,128)S(1)}, ...), condition=%wide.region_14.15_spmd.clone, body=%wide.region_13.14_spmd.clone.sunk | while | flops 810813440 | bytes 8940159 | solution.py:734
  290.8 16.7 %scatter.2 = f32[64,128]{1,0:T(8,128)} custom-call(f32[2,4,2,2,64,128]{5,4,3,2,1,0:T(8,128)} %bitcast.31.refs_0_), custom_call_target="tpu_custom_call" | custom-call | tf_op jit(solution)/shard_map/scatter/pallas_call | solution.py:496
  310.3 4.4 multiply_reduce_fusion
  314.7 3.2 convert_reduce_fusion.1
  318.2 20.0 %convert_reduce_fusion = (f32[4096]{0:T(1024)S(1)}, bf16[1088,4096]{1,0:T(8,128)(2,1)}) fusion(f32[1088,4096]{1,0:T(8,128)} %get-tuple-element.254, bf16[4096,1024]{1,0:T(8,128)(2,1)S(1)} %bitcast.209, f32[1088,1024]{1,0:T(8,128)S(1)} %get-tuple-element.223), kind=kOutput, calls=%fused_computation.32 | convolution fusion | flops 9190305792 | bytes 39600128 | tf_op jit(solution)/shard_map/le,de->ld/dot_general | solution.py:531
  338.2 17.5 %multiply_reduce_fusion.1 = (f32[1024]{0:T(1024)S(1)}, f32[1088]{0:T(1024)S(1)}, f32[1088]{0:T(1024)S(1)}, f32[1024]{0:T(1024)S(1)}, f32[1088,1024]{1,0:T(8,128)S(1)}) fusion(f32[1088,1024]{1,0:T(8,128)} %get-tuple-element.252, f32[1088]{0:T(1024)S(1)} %add_rsqrt_fusion.2, f32[1088]{0:T(1024)S(1)} %broadcast_multiply_fusion.5, f32[1024]{0:T(1024)S(1)} %reshape.338, ...), kind=kOutput, calls=%fused_computation.48 | convolution fusion | flops 9137942528 | bytes 30700544 | tf_op jit(solution)/shard_map/le,de->ld/dot_general | solution.py:531
  355.7 3.2 convert_reduce_fusion.2
  361.0 3.9 convolution_convert_fusion.2.grad_ref
  364.9 50.3 %attend_backward.1 = (bf16[1088,1024]{1,0:T(8,128)(2,1)}, bf16[1088,1024]{1,0:T(8,128)(2,1)}, bf16[1088,1024]{1,0:T(8,128)(2,1)}) custom-call(s32[1]{0:T(128)S(6)} %copy.80.length_ref, bf16[1088,1024]{1,0:T(8,128)(2,1)} %get-tuple-element.128.q_ref, bf16[1088,1024]{1,0:T(8,128)(2,1)} %get-tuple-element.129.k_ref, ...), custom_call_target="tpu_custom_call" | custom-call | tf_op jit(solution)/shard_map/attend_backward/pallas_call | solution.py:229
  424.8 18.7 %convolution_convert_fusion = bf16[1024,4096]{1,0:T(8,128)(2,1)} fusion(bf16[1088,4096]{1,0:T(8,128)(2,1)} %get-tuple-element.262, f32[1088,1024]{1,0:T(8,128)} %get-tuple-element.252, f32[1024]{0:T(1024)S(1)} %reshape.339, f32[1024]{0:T(1024)S(1)} %reshape.338, f32[1088]{0:T(1024)S(1)} %add_rsqrt_fusion.2, f32[1088]{0:T(1024)S(1)} %broadcast_multiply_fusion.5), kind=kOutput, calls=%fused_computation.36 | convolution fusion | flops 9136570368 | bytes 21774848 | tf_op jit(solution)/shard_map/ld,le->de/dot_general | solution.py:535
  443.4 4.1 convolution_convert_fusion.6
  447.6 13.5 %convolution_convert_fusion.1 = bf16[4096,1024]{1,0:T(8,128)(2,1)} fusion(bf16[1088,4096]{1,0:T(8,128)(2,1)S(1)} %bitcast.213, f32[1088,1024]{1,0:T(8,128)S(1)} %bitcast.153), kind=kOutput, calls=%fused_computation.37 | convolution fusion | flops 9132113920 | bytes 21757952 | tf_op jit(solution)/shard_map/ld,le->de/dot_general | solution.py:535
  461.1 4.1 convolution_convert_fusion.5
  465.3 4.1 convolution_convert_fusion.4
  469.3 4.3 convolution_convert_fusion.3
  473.6 152.4 %scatter.3 = (f32[128,1024]{1,0:T(8,128)}, f32[32,4096]{1,0:T(8,128)}, f32[32,128]{1,0:T(8,128)}, f32[32,1024]{1,0:T(8,128)}, f32[32,1024]{1,0:T(8,128)}, /*inde...) custom-call(bf16[2,4,2,2,128,1024]{5,4,3,2,1,0:T(8,128)(2,1)} %bitcast.149, ...), custom_call_target="tpu_custom_call" | custom-call | tf_op jit(solution)/shard_map/scatter/pallas_call | solution.py:496
  628.7 6.2 convolution_add_fusion.6
  635.0 2.5 convolution_add_fusion.5
  637.5 2.5 convolution_add_fusion.4
  640.1 2.6 slice_bitcast_fusion
  (168 shorter events, 54.8 us)
Async XLA Ops:
  145.5 36.2 %copy-start.18 = (bf16[2,32,1024]{2,1,0:T(8,128)(2,1)S(1)}, bf16[2,32,1024]{2,1,0:T(8,128)(2,1)}, u32[]{:S(2)}) copy-start(bf16[2,32,1024]{2,1,0:T(8,128)(2,1)} %param.28) | copy-start | bytes 393220
  232.5 4.6 copy-start.17
  235.7 1.4 copy-start
  310.3 7.7 %slice-start.4 = ((s8[8388608]{0:T(1024)(128)(4,1)}), s8[4194304]{0:T(1024)(128)(4,1)S(1)}, s32[]{:S(2)}) async-start(s8[8388608]{0:T(1024)(128)(4,1)} %bitcast.207), calls=%async_computation.4 | async-start | bytes 8388608
  314.7 3.5 slice-start.5
  317.9 20.3 %copy-start.5 = (f32[1088,1024]{1,0:T(8,128)}, f32[1088,1024]{1,0:T(8,128)S(1)}, u32[]{:S(2)}) copy-start(f32[1088,1024]{1,0:T(8,128)S(1)} %get-tuple-element.223) | copy-start | bytes 13369348
  355.7 5.3 copy-start.23
  358.9 2.0 copy-start.4
  415.2 8.0 %copy-start.1 = (bf16[1088,1024]{1,0:T(8,128)(2,1)S(1)}, bf16[1088,1024]{1,0:T(8,128)(2,1)}, u32[]{:S(2)}) copy-start(bf16[1088,1024]{1,0:T(8,128)(2,1)} %copy-done) | copy-start | bytes 6684676
  422.4 25.1 %slice-start.6 = ((s8[8912896]{0:T(1024)(128)(4,1)}), s8[4194304]{0:T(1024)(128)(4,1)S(1)}, s32[]{:S(2)}) async-start(s8[8912896]{0:T(1024)(128)(4,1)} %bitcast.212), calls=%async_computation.6 | async-start | bytes 8388608
  423.2 20.2 %slice-start = ((s8[4456448]{0:T(1024)(128)(4,1)}), s8[4194304]{0:T(1024)(128)(4,1)S(1)}, s32[]{:S(2)}) async-start(s8[4456448]{0:T(1024)(128)(4,1)} %bitcast.150), calls=%async_computation | async-start | bytes 8388608
  423.2 24.4 %slice-start.2 = ((s8[4456448]{0:T(1024)(128)(4,1)}), s8[4194304]{0:T(1024)(128)(4,1)S(1)}, s32[]{:S(2)}) async-start(s8[4456448]{0:T(1024)(128)(4,1)} %bitcast.152), calls=%async_computation.2 | async-start | bytes 8388608
  424.7 18.7 %slice-start.1 = ((s8[4456448]{0:T(1024)(128)(4,1)}), s8[262144]{0:T(1024)(128)(4,1)S(1)}, s32[]{:S(2)}) async-start(s8[4456448]{0:T(1024)(128)(4,1)} %bitcast.150), calls=%async_computation.1 | async-start | bytes 524288
  424.7 18.7 %copy-start.6 = (bf16[1088,1024]{1,0:T(8,128)(2,1)S(1)}, bf16[1088,1024]{1,0:T(8,128)(2,1)}, u32[]{:S(2)}) copy-start(bf16[1088,1024]{1,0:T(8,128)(2,1)} %get-tuple-element.120.mixed_ref) | copy-start | bytes 6684676
  424.7 22.8 %slice-start.3 = ((s8[4456448]{0:T(1024)(128)(4,1)}), s8[262144]{0:T(1024)(128)(4,1)S(1)}, s32[]{:S(2)}) async-start(s8[4456448]{0:T(1024)(128)(4,1)} %bitcast.152), calls=%async_computation.3 | async-start | bytes 524288
  424.7 22.8 %slice-start.7 = ((s8[8912896]{0:T(1024)(128)(4,1)}), s8[4194304]{0:T(1024)(128)(4,1)S(1)}, s32[]{:S(2)}) async-start(s8[8912896]{0:T(1024)(128)(4,1)} %bitcast.212), calls=%async_computation.7 | async-start | bytes 8388608
  424.7 22.8 %slice-start.8 = ((s8[8912896]{0:T(1024)(128)(4,1)}), s8[524288]{0:T(1024)(128)(4,1)S(1)}, s32[]{:S(2)}) async-start(s8[8912896]{0:T(1024)(128)(4,1)} %bitcast.212), calls=%async_computation.8 | async-start | bytes 1048576
  447.6 13.5 %copy-start.11 = (bf16[1088,1024]{1,0:T(8,128)(2,1)S(1)}, bf16[1088,1024]{1,0:T(8,128)(2,1)}, u32[]{:S(2)}) copy-start(bf16[1088,1024]{1,0:T(8,128)(2,1)} %get-tuple-element.132) | copy-start | bytes 6684676
  447.6 13.5 %copy-start.14 = (bf16[1,1024,1024]{2,1,0:T(8,128)(2,1)S(1)}, bf16[1,1024,1024]{2,1,0:T(8,128)(2,1)}, u32[]{:S(2)}) copy-start(bf16[1,1024,1024]{2,1,0:T(8,128)(2,1)} %param.27) | copy-start | bytes 6291460
  447.6 13.5 %copy-start.19 = (bf16[2,32,1024]{2,1,0:T(8,128)(2,1)S(1)}, bf16[2,32,1024]{2,1,0:T(8,128)(2,1)}, u32[]{:S(2)}) copy-start(bf16[2,32,1024]{2,1,0:T(8,128)(2,1)} %param.28) | copy-start | bytes 393220
  461.1 4.1 copy-start.9
  465.3 4.1 copy-start.7
  628.7 6.2 copy-start.10
  628.7 6.3 copy-start.13
  635.0 2.5 copy-start.8
  635.0 2.5 copy-start.12
  640.1 3.4 copy-start.2
  642.7 7.3 %copy-start.21 = (f32[32,1024]{1,0:T(8,128)S(1)}, f32[32,1024]{1,0:T(8,128)}, u32[]{:S(2)}) copy-start(f32[32,1024]{1,0:T(8,128)} %get-tuple-element.433) | copy-start | bytes 393220
  642.7 7.9 %copy-start.20 = (f32[32,1024]{1,0:T(8,128)S(1)}, f32[32,1024]{1,0:T(8,128)}, u32[]{:S(2)}) copy-start(f32[32,1024]{1,0:T(8,128)} %get-tuple-element.434) | copy-start | bytes 393220
  642.7 8.6 %copy-start.16 = (f32[32,4096]{1,0:T(8,128)S(1)}, f32[32,4096]{1,0:T(8,128)}, u32[]{:S(2)}) copy-start(f32[32,4096]{1,0:T(8,128)} %get-tuple-element.441) | copy-start | bytes 1572868
  642.7 9.4 %copy-start.15 = (f32[128,1024]{1,0:T(8,128)S(1)}, f32[128,1024]{1,0:T(8,128)}, u32[]{:S(2)}) copy-start(f32[128,1024]{1,0:T(8,128)} %get-tuple-element.443) | copy-start | bytes 1572868
  642.7 10.2 %copy-start.22 = (f32[32,128]{1,0:T(8,128)S(1)}, f32[32,128]{1,0:T(8,128)}, u32[]{:S(2)}) copy-start(f32[32,128]{1,0:T(8,128)} %get-tuple-element.447) | copy-start | bytes 49156
  (1 other events, 0.8 us)

commit v2 on v1

--- a/solution.py
+++ b/solution.py
@@ -95,13 +95,14 @@
     return weight / jnp.sum(weight, axis=1, keepdims=True)
 
 
-def attend_step(slot, question, length_ref, tokens_ref, wq_ref, wk_ref, wv_ref, bias_ref, cos_ref, sin_ref, q_ref, k_ref, v_ref, mixed_ref, mass_ref):
+def attend_step(slot, question, length_ref, tokens_ref, wq_ref, wk_ref, wv_ref, bias_ref, cos_ref, sin_ref, q_ref, k_ref, v_ref, mixed_ref, mass_ref, go=lambda part: None):
     tokens = tokens_ref[...]
     cosine = wide(cos_ref[...])
     sine = wide(sin_ref[...])
     q_ref[...] = rope(nn(tokens, wq_ref[...]) + bias_ref[0:1, :].astype(f32), cosine, sine).astype(bf16)
     k_ref[...] = rope(nn(tokens, wk_ref[...]) + bias_ref[1:2, :].astype(f32), cosine, sine).astype(bf16)
     v_ref[...] = (nn(tokens, wv_ref[...]) + bias_ref[2:3, :].astype(f32)).astype(bf16)
+    go(0)
     total = tokens.shape[0]
     length = length_ref[0]
     pair = (slot, 2 * HEAD)
@@ -130,9 +131,12 @@
         turned = jnp.where(lane < HEAD, masses[1], masses[0]).T
         mass_ref[0, 2 * p : 2 * p + 1, 0:slot] = turned[HEAD : HEAD + 1, :]
         mass_ref[0, 2 * p + 1 : 2 * p + 2, 0:slot] = turned[0:1, :]
+        if p == 0:
+            go(1)
     rest = slice(slot, total)
     weight = question_probs(heads_apart(q_ref[rest, :], 4), k_ref[rest, :], question)
     mixed_ref[rest, :] = heads_joined(nn(weight.astype(bf16), v_ref[rest, :]), 4).astype(bf16)
+    go(2)
 
 
 def group_spec(rows):
@@ -171,74 +175,6 @@
     )(length, tokens, wq, wk, wv, biases, cosine, sine)
 
 
-def attend_back_step(slot, question, length_ref, q_ref, k_ref, v_ref, mixed_ref, grad_ref, mass_ref, cos_ref, sin_ref, dq_ref, dk_ref, dv_ref):
-    total = q_ref.shape[0]
-    length = length_ref[0]
-    pair = (slot, 2 * HEAD)
-    lane = lane_of(pair)
-    mask = jnp.where(row_of(pair) < length, 0.0, masked_value).astype(bf16)
-    cosine = cos_ref[0:slot, :]
-    sine = sin_ref[0:slot, :]
-    for p in range(2):
-        cols = slice(p * 2 * HEAD, (p + 1) * 2 * HEAD)
-        query = q_ref[0:slot, cols]
-        key = k_ref[0:slot, cols]
-        value = v_ref[0:slot, cols]
-        grad = grad_ref[0:slot, cols]
-        key_turned = key.T
-        product = (grad.astype(f32) * mixed_ref[0:slot, cols].astype(f32)).T
-        dq = []
-        dk = []
-        dv = []
-        for h in range(2):
-            mine = (lane // HEAD) == h
-            spare = (1 - h) * HEAD
-            query_h = jnp.where(mine, query, jnp.where(lane == spare, 1.0, 0.0).astype(bf16))
-            key_h = jnp.where(lane == spare, mask, key)
-            value_h = jnp.where(mine, value, jnp.zeros_like(value))
-            row_dot = jnp.sum(product[h * HEAD : (h + 1) * HEAD], axis=0, keepdims=True)
-            mass = mass_ref[0, 2 * p + h : 2 * p + h + 1, 0:slot]
-            probs = jnp.exp2(nt(key_h, query_h) * score_scale - mass)
-            slope = (probs * (nt(value_h, grad) - row_dot)).astype(bf16)
-            dv.append(nn(probs.astype(bf16), grad))
-            dk.append(nn(slope, query))
-            dq.append(nn(key_turned[h * HEAD : (h + 1) * HEAD], slope))
-        dq_all = jnp.concatenate(dq, axis=0).T * 0.125
-        dk_all = jnp.where(lane < HEAD, dk[0], dk[1]) * 0.125
-        dq_ref[0:slot, cols] = rope_back(dq_all, cosine, sine).astype(bf16)
-        dk_ref[0:slot, cols] = rope_back(dk_all, cosine, sine).astype(bf16)
-        dv_ref[0:slot, cols] = jnp.where(lane < HEAD, dv[0], dv[1]).astype(bf16)
-    rest = slice(slot, total)
-    cosine = wide(cos_ref[rest, :])
-    sine = wide(sin_ref[rest, :])
-    apart = heads_apart(q_ref[rest, :], 4)
-    grad_apart = heads_apart(grad_ref[rest, :], 4)
-    key = k_ref[rest, :]
-    probs = question_probs(apart, key, question)
-    grad_prob = nt(grad_apart, v_ref[rest, :])
-    row_dot = jnp.sum(probs * grad_prob, axis=1, keepdims=True)
-    slope = (probs * (grad_prob - row_dot) * 0.125).astype(bf16)
-    dq_ref[rest, :] = rope_back(heads_joined(nn(slope, key), 4), cosine, sine).astype(bf16)
-    dk_ref[rest, :] = rope_back(tn(slope, apart), cosine, sine).astype(bf16)
-    dv_ref[rest, :] = tn(probs.astype(bf16), grad_apart).astype(bf16)
-
-
-def attend_backward(length, q, k, v, mixed, grad, mass, cosine, sine, slot, question):
-    total, width = q.shape
-    groups = width // (4 * HEAD)
-    return pl.pallas_call(
-        functools.partial(attend_back_step, slot, question),
-        grid=(groups,),
-        in_specs=[pl.BlockSpec(memory_space=pltpu.SMEM)]
-        + [group_spec(total)] * 5
-        + [mass_spec(total), whole_spec((total, 2 * HEAD)), whole_spec((total, 2 * HEAD))],
-        out_specs=[group_spec(total)] * 3,
-        out_shape=[jax.ShapeDtypeStruct((total, width), bf16)] * 3,
-        compiler_params=pltpu.CompilerParams(vmem_limit_bytes=vmem_bytes),
-        name="attend_backward",
-    )(length, q, k, v, mixed, grad, mass, cosine, sine)
-
-
 class Place:
     def __init__(self):
         y = lax.axis_index("fsdp")
@@ -252,6 +188,8 @@
         self.twin = (y, z * 4 + x * 2 + (1 - c))
         self.along = [(y, ((z + k) % 4) * 4 + x * 2 + c) for k in (1, 2, 3)]
         self.lines = [(y, x), (y1, x1), (y2, x2), (1 - y, 1 - x)]
+        self.ahead = [(z + k) % 4 for k in (1, 2, 3)]
+        self.other = 1 - c
 
     def greet(self):
         barrier = pltpu.get_barrier_semaphore()
@@ -286,42 +224,71 @@
     pltpu.make_async_copy(ref, ref, sem).wait()
 
 
+class LateSender:
+    def __init__(self):
+        self.sent = []
+
+    def copy(self, parts):
+        src, dst, send_sem, recv_sem, device = parts()
+        return pltpu.make_async_remote_copy(
+            src_ref=src, dst_ref=dst, send_sem=send_sem, recv_sem=recv_sem, device_id=device, device_id_type=MESH
+        )
+
+    def go(self, parts):
+        self.copy(parts).start()
+        self.sent.append(parts)
+
+    def drain(self):
+        for parts in self.sent:
+            self.copy(parts).wait_send()
+
+
 class Gather:
     def __init__(self, place, shards, wholes, send_sem, recv_sem, own_sem):
-        self.at, self.shards, self.wholes = place, shards, wholes
+        self.at, self.shards = place, shards
+        self.wholes = [w if isinstance(w, tuple) else (w, ()) for w in wholes]
         self.send_sem, self.recv_sem, self.own_sem = send_sem, recv_sem, own_sem
-        self.out = Sender()
+        self.out = LateSender()
+
+    def block(self, t, *where):
+        whole, tail = self.wholes[t]
+        return whole.at[where + tail]
 
     def line(self, t, k, core):
         y, x = self.at.lines[k]
-        return self.wholes[t].at[y, :, x, core]
+        return self.block(t, y, slice(None), x, core)
+
+    def mine(self, t):
+        at = self.at
+        return self.block(t, at.y, at.z, at.x, at.c)
 
     def own(self, t):
-        at = self.at
-        return pltpu.make_async_copy(
-            self.shards[t], self.wholes[t].at[at.y, at.z, at.x, at.c], self.own_sem.at[t]
-        )
+        return pltpu.make_async_copy(self.shards[t], self.mine(t), self.own_sem.at[t])
 
     def begin(self, t):
-        at = self.at
-        for k, peer in enumerate(at.along):
+        for k, peer in enumerate(self.at.along):
             self.out.go(
-                self.shards[t],
-                self.wholes[t].at[at.y, at.z, at.x, at.c],
-                self.send_sem.at[t, k],
-                self.recv_sem.at[t, 0],
-                peer,
+                lambda k=k, peer=peer: (
+                    self.shards[t], self.mine(t), self.send_sem.at[t, k], self.recv_sem.at[t, 0], peer,
+                )
             )
         self.own(t).start()
 
     def pass_line(self, t, k, targets):
-        line = self.line(t, k, self.at.c)
         for send, recv, peer in targets:
-            self.out.go(line, line, self.send_sem.at[t, send], self.recv_sem.at[t, recv], peer)
+            self.out.go(
+                lambda send=send, recv=recv, peer=peer: (
+                    self.line(t, k, self.at.c),
+                    self.line(t, k, self.at.c),
+                    self.send_sem.at[t, send],
+                    self.recv_sem.at[t, recv],
+                    peer,
+                )
+            )
 
     def own_line(self, t):
         at = self.at
-        arrived(self.wholes[t].at[at.y, 0:3, at.x, at.c], self.recv_sem.at[t, 0])
+        arrived(self.block(t, at.y, slice(0, 3), at.x, at.c), self.recv_sem.at[t, 0])
         self.own(t).wait()
         self.pass_line(t, 0, [(3, 1, at.first), (4, 2, at.second), (5, 4, at.twin)])
 
@@ -340,7 +307,32 @@
 
     def twin_lines(self, t):
         for k in range(4):
-            arrived(self.line(t, k, 1 - self.at.c), self.recv_sem.at[t, 4 + k])
+            arrived(self.line(t, k, self.at.other), self.recv_sem.at[t, 4 + k])
+
+    def perform(self, names):
+        moves = {
+            "B": self.begin, "O": self.own_line, "F": self.first_line, "S": self.second_line,
+            "R": self.far_line, "T": self.twin_lines,
+        }
+        for some in names:
+            for name in some.split():
+                moves[name[0]](int(name[1:]))
+
+
+def gather_sems(count):
+    return [
+        pltpu.SemaphoreType.DMA((count, 10)),
+        pltpu.SemaphoreType.DMA((count, 8)),
+        pltpu.SemaphoreType.DMA((count,)),
+    ]
+
+
+def spread_shape(shard):
+    return jax.ShapeDtypeStruct((2, 4, 2, 2) + shard.shape, shard.dtype)
+
+
+def joined_shards(whole):
+    return whole.reshape((32 * whole.shape[4],) + whole.shape[5:])
 
 
 def gather_body(count, *refs):
@@ -369,18 +361,202 @@
         functools.partial(gather_body, count),
         in_specs=[pl.BlockSpec(memory_space=pltpu.VMEM)] * count,
         out_specs=[pl.BlockSpec(memory_space=pl.ANY)] * count,
-        out_shape=[jax.ShapeDtypeStruct((2, 4, 2, 2) + a.shape, a.dtype) for a in shards],
-        scratch_shapes=[
-            pltpu.SemaphoreType.DMA((count, 10)),
-            pltpu.SemaphoreType.DMA((count, 8)),
-            pltpu.SemaphoreType.DMA((count,)),
-        ],
+        out_shape=[spread_shape(a) for a in shards],
+        scratch_shapes=gather_sems(count),
         compiler_params=pltpu.CompilerParams(
             collective_id=collective_id, has_side_effects=True, vmem_limit_bytes=vmem_bytes
         ),
         name="gather",
     )(*shards)
-    return [w.reshape((32 * a.shape[0],) + a.shape[1:]) for w, a in zip(wholes, shards)]
+    return [joined_shards(w) for w in wholes]
+
+
+attend_plan = {
+    (0, 2): ["O0"],
+    (1, 1): ["O1 F0 S0"],
+    (2, 0): ["O2 F1 S1 R0"],
+    (2, 2): ["O3 F2 S2 R1"],
+    (3, 1): ["R2"],
+    (3, 2): ["O4 F3 S3"],
+    (3, 3): ["F4 S4 R3 R4"],
+}
+
+
+def pump(run, step, plan, steps):
+    def go(part):
+        for g in range(steps):
+            if (g, part) in plan:
+
+                @pl.when(step == g)
+                def _():
+                    run.perform(plan[g, part])
+
+    return go
+
+
+def attend_gather_body(slot, question, *refs):
+    ins, shards = refs[:8], refs[8:10]
+    outs, wholes = refs[10:15], refs[15:17]
+    step = pl.program_id(0)
+    place = Place()
+    width = shards[1].shape[1] // 4
+    cuts = [slice(j * width, (j + 1) * width) for j in range(4)]
+    units = [shards[0]] + [shards[1].at[:, cut] for cut in cuts]
+    places = [wholes[0]] + [(wholes[1], (slice(None), cut)) for cut in cuts]
+    run = Gather(place, units, places, *refs[17:])
+
+    @pl.when(step == 0)
+    def _():
+        place.greet()
+        for t in range(len(units)):
+            run.begin(t)
+
+    go = pump(run, step, attend_plan, 4)
+    attend_step(slot, question, *ins, *outs, go=go)
+
+    @pl.when(step == 3)
+    def _():
+        run.perform(attend_plan[3, 3])
+        for t in range(len(units)):
+            run.twin_lines(t)
+        run.out.drain()
+
+
+def attend_gather(length, tokens, wq, wk, wv, biases, cosine, sine, slot, question, shards):
+    total, width = tokens.shape
+    groups = width // (4 * HEAD)
+    once = pl.Buffered(1)
+
+    def kept(shape):
+        return pl.BlockSpec(shape, lambda i: (0,) * len(shape), pipeline_mode=once)
+
+    *outs, first, second = pl.pallas_call(
+        functools.partial(attend_gather_body, slot, question),
+        grid=(groups,),
+        in_specs=[
+            pl.BlockSpec(memory_space=pltpu.SMEM),
+            kept((total, width)),
+            group_spec(width),
+            group_spec(width),
+            group_spec(width),
+            group_spec(8),
+            kept((total, 2 * HEAD)),
+            kept((total, 2 * HEAD)),
+        ]
+        + [kept(a.shape) for a in shards],
+        out_specs=[group_spec(total)] * 4 + [mass_spec(total)] + [pl.BlockSpec(memory_space=pl.ANY)] * 2,
+        out_shape=[jax.ShapeDtypeStruct((total, width), bf16)] * 4
+        + [jax.ShapeDtypeStruct((groups, 8, total), f32)]
+        + [spread_shape(a) for a in shards],
+        scratch_shapes=gather_sems(5),
+        compiler_params=pltpu.CompilerParams(collective_id=5, has_side_effects=True, vmem_limit_bytes=vmem_bytes),
+        name="attend_forward",
+    )(length, tokens, wq, wk, wv, biases, cosine, sine, *shards)
+    return outs, [joined_shards(first), joined_shards(second)]
+
+
+inner_plan = {
+    (0, 3): ["O0"],
+    (2, 0): ["O1 F0 S0"],
+    (4, 0): ["F1 S1 R0"],
+    (5, 0): ["O2"],
+    (6, 0): ["R1"],
+    (7, 0): ["O3 F2 S2 O4"],
+    (8, 0): ["R2"],
+    (8, 1): ["F3 S3 F4 S4", "R3 R4"],
+}
+
+
+def inner_body(refs):
+    (tokens_ref, mixed_ref, wo_ref, wi_ref, vec_ref, bias_ref, outer_ref, proj_ref) = refs[:8]
+    (normal_ref, inverse_ref, low_ref, act_ref, slope_ref, outer_whole, proj_whole) = refs[8:15]
+    step = pl.program_id(0)
+    place = Place()
+    rows = outer_ref.shape[0] // 4
+    cuts = [slice(j * rows, (j + 1) * rows) for j in range(4)]
+    units = [outer_ref.at[cut] for cut in cuts] + [proj_ref]
+    places = [(outer_whole, (cut,)) for cut in cuts] + [proj_whole]
+    run = Gather(place, units, places, *refs[15:])
+    total = tokens_ref.shape[0]
+
+    @pl.when(step == 0)
+    def _():
+        place.greet()
+        for t in range(len(units)):
+            run.begin(t)
+        part = total // 4
+        for j in range(4):
+            these = slice(j * part, (j + 1) * part)
+            attended = nn(mixed_ref[these, :], wo_ref[...]) + vec_ref[0:1, :]
+            normal, inverse = normalize_rows(tokens_ref[these, :].astype(f32) + attended)
+            normal_ref[these, :] = normal
+            inverse_ref[these, :] = jnp.broadcast_to(inverse, (part, inverse_ref.shape[1]))
+            low_ref[these, :] = (normal * vec_ref[1:2, :] + vec_ref[2:3, :]).astype(bf16)
+            if (0, j) in inner_plan:
+                run.perform(inner_plan[0, j])
+
+    @pl.when(step > 0)
+    def _():
+        part = total // 4
+
+        def some(j, carry):
+            these = pl.ds(pl.multiple_of(j * part, 16), part)
+            hidden = nn(low_ref[these, :], wi_ref[...]) + bias_ref[...].astype(f32)
+            activated, slope = gelu_both(hidden)
+            act_ref[these, :] = activated.astype(bf16)
+            slope_ref[these, :] = slope.astype(bf16)
+            return carry
+
+        lax.fori_loop(0, 4, some, 0)
+
+    for g in range(1, 9):
+        if (g, 0) in inner_plan:
+
+            @pl.when(step == g)
+            def _():
+                run.perform(inner_plan[g, 0])
+
+    @pl.when(step == 8)
+    def _():
+        run.perform(inner_plan[8, 1])
+        for t in range(len(units)):
+            run.twin_lines(t)
+        run.out.drain()
+
+
+def inner_forward(tokens, mixed, wo, wi, vectors, bias, shards):
+    total, width = tokens.shape
+    hidden = wi.shape[1]
+    chunk = hidden // 8
+    once = pl.Buffered(1)
+
+    def kept(shape):
+        return pl.BlockSpec(shape, lambda i: (0,) * len(shape), pipeline_mode=once)
+
+    def chunked(rows):
+        return pl.BlockSpec((rows, chunk), lambda i: (0, jnp.maximum(i - 1, 0)))
+
+    *outs, outer, proj = pl.pallas_call(
+        lambda *refs: inner_body(refs),
+        grid=(9,),
+        in_specs=[kept((total, width)), kept((total, width)), kept((width, width)), chunked(width), kept(vectors.shape)]
+        + [chunked(1)]
+        + [kept(a.shape) for a in shards],
+        out_specs=[kept((total, width)), kept((total, 128)), kept((total, width)), chunked(total), chunked(total)]
+        + [pl.BlockSpec(memory_space=pl.ANY)] * 2,
+        out_shape=[
+            jax.ShapeDtypeStruct((total, width), f32),
+            jax.ShapeDtypeStruct((total, 128), f32),
+            jax.ShapeDtypeStruct((total, width), bf16),
+            jax.ShapeDtypeStruct((total, hidden), bf16),
+            jax.ShapeDtypeStruct((total, hidden), bf16),
+        ]
+        + [spread_shape(a) for a in shards],
+        scratch_shapes=gather_sems(5),
+        compiler_params=pltpu.CompilerParams(collective_id=6, has_side_effects=True, vmem_limit_bytes=vmem_bytes),
+        name="inner_forward",
+    )(tokens, mixed, wo, wi, vectors, bias, *shards)
+    return outs, [joined_shards(outer), joined_shards(proj)]
 
 
 class Scatter:
@@ -511,6 +687,407 @@
     )(*[p.reshape((2, 4, 2, 2) + shape) for p, shape in zip(parts, shapes)])
 
 
+class Unit:
+    twin_slot = (0, 2, 1, 3)
+
+    def __init__(self, place, out, mine, twins, buffers, send_sem, recv_sem, own_sem=None):
+        self.at, self.out, self.mine, self.twins = place, out, mine, twins
+        self.total, self.twin, self.second, self.first, self.last = buffers
+        self.send_sem, self.recv_sem, self.own_sem = send_sem, recv_sem, own_sem
+        self.sender = LateSender()
+
+    def to_twin(self, k):
+        slot = self.twin_slot[k]
+        return lambda: (self.twins(k), self.twin.at[slot], self.send_sem.at[k], self.recv_sem.at[slot], self.at.twin)
+
+    def begin(self):
+        for k in (3, 2, 1, 0):
+            self.sender.copy(self.to_twin(k)).start()
+            if self.own_sem is not None:
+                self.own(k).start()
+
+    def own(self, k):
+        return pltpu.make_async_copy(self.mine(k), self.total.at[k], self.own_sem.at[k])
+
+    def join_twin(self, k):
+        if self.own_sem is not None:
+            self.own(k).wait()
+        arrived(self.twin.at[k], self.recv_sem.at[k])
+        if self.own_sem is not None:
+            self.total[k] = self.total[k] + self.twin[k]
+        else:
+            self.total[k] = self.mine(k)[...] + self.twin[k]
+
+    def to_second(self):
+        self.join_twin(3)
+        self.sender.go(lambda: (self.total.at[3], self.second.at[1], self.send_sem.at[4], self.recv_sem.at[5], self.at.second))
+        self.join_twin(2)
+        self.sender.go(lambda: (self.total.at[2], self.second.at[0], self.send_sem.at[5], self.recv_sem.at[4], self.at.second))
+        self.join_twin(1)
+        self.join_twin(0)
+
+    def to_first(self):
+        arrived(self.second.at[1], self.recv_sem.at[5])
+        self.total[1] = self.total[1] + self.second[1]
+        self.sender.go(lambda: (self.total.at[1], self.first, self.send_sem.at[6], self.recv_sem.at[6], self.at.first))
+        arrived(self.second.at[0], self.recv_sem.at[4])
+        self.total[0] = self.total[0] + self.second[0]
+
+    def to_line(self):
+        arrived(self.first, self.recv_sem.at[6])
+        self.total[0] = self.total[0] + self.first[...]
+        for k, peer in enumerate(self.at.along):
+            self.sender.go(lambda k=k, peer=peer: (self.total.at[0, self.at.ahead[k]], self.last.at[k], self.send_sem.at[7 + k], self.recv_sem.at[7 + k], peer))
+
+    def finish(self):
+        for k in range(3):
+            arrived(self.last.at[k], self.recv_sem.at[7 + k])
+        self.out(
+            (self.total[0, self.at.z].astype(f32) + self.last[0].astype(f32))
+            + (self.last[1].astype(f32) + self.last[2].astype(f32))
+        )
+
+    def drain_twin(self):
+        for k in range(4):
+            self.sender.copy(self.to_twin(k)).wait_send()
+
+    def drain(self):
+        self.sender.drain()
+
+
+class VectorSum:
+    def __init__(self, place, value, sums, heard, out, send_sem, recv_sem):
+        self.at, self.value, self.sums, self.heard, self.out = place, value, sums, heard, out
+        self.send_sem, self.recv_sem = send_sem, recv_sem
+        self.sender = LateSender()
+
+    def tell(self, source, slot, peer):
+        self.sender.go(lambda: (source(), self.heard.at[slot], self.send_sem.at[slot], self.recv_sem.at[slot], peer))
+
+    def hear(self, slot):
+        arrived(self.heard.at[slot], self.recv_sem.at[slot])
+        return self.heard[slot]
+
+    def twin(self):
+        self.tell(lambda: self.value, 0, self.at.twin)
+
+    def second(self):
+        self.sums[0] = self.value[...] + self.hear(0)
+        self.tell(lambda: self.sums.at[0], 1, self.at.second)
+
+    def first(self):
+        self.sums[1] = self.sums[0] + self.hear(1)
+        self.tell(lambda: self.sums.at[1], 2, self.at.first)
+
+    def line(self):
+        self.sums[2] = self.sums[1] + self.hear(2)
+        for k, peer in enumerate(self.at.along):
+            self.tell(lambda: self.sums.at[2], 3 + k, peer)
+
+    def finish(self):
+        self.out[...] = (self.sums[2] + self.hear(3)) + (self.hear(4) + self.hear(5))
+
+
+def back_pair(slot, p, length, q_ref, k_ref, v_ref, mixed_ref, grad_ref, mass_ref, cos_ref, sin_ref, dq_ref, dk_ref, dv_ref):
+    pair = (slot, 2 * HEAD)
+    lane = lane_of(pair)
+    mask = jnp.where(row_of(pair) < length, 0.0, masked_value).astype(bf16)
+    cosine = cos_ref[0:slot, :]
+    sine = sin_ref[0:slot, :]
+    cols = slice(p * 2 * HEAD, (p + 1) * 2 * HEAD)
+    query = q_ref[0:slot, cols]
+    key = k_ref[0:slot, cols]
+    value = v_ref[0:slot, cols]
+    grad = grad_ref[0:slot, cols]
+    key_turned = key.T
+    product = (grad.astype(f32) * mixed_ref[0:slot, cols].astype(f32)).T
+    dq = []
+    dk = []
+    dv = []
+    for h in range(2):
+        mine = (lane // HEAD) == h
+        spare = (1 - h) * HEAD
+        query_h = jnp.where(mine, query, jnp.where(lane == spare, 1.0, 0.0).astype(bf16))
+        key_h = jnp.where(lane == spare, mask, key)
+        value_h = jnp.where(mine, value, jnp.zeros_like(value))
+        row_dot = jnp.sum(product[h * HEAD : (h + 1) * HEAD], axis=0, keepdims=True)
+        mass = mass_ref[0, 2 * p + h : 2 * p + h + 1, 0:slot]
+        probs = jnp.exp2(nt(key_h, query_h) * score_scale - mass)
+        slope = (probs * (nt(value_h, grad) - row_dot)).astype(bf16)
+        dv.append(nn(probs.astype(bf16), grad))
+        dk.append(nn(slope, query))
+        dq.append(nn(key_turned[h * HEAD : (h + 1) * HEAD], slope))
+    dq_all = jnp.concatenate(dq, axis=0).T * 0.125
+    dk_all = jnp.where(lane < HEAD, dk[0], dk[1]) * 0.125
+    dq_ref[0:slot, cols] = rope_back(dq_all, cosine, sine).astype(bf16)
+    dk_ref[0:slot, cols] = rope_back(dk_all, cosine, sine).astype(bf16)
+    dv_ref[0:slot, cols] = jnp.where(lane < HEAD, dv[0], dv[1]).astype(bf16)
+
+
+def back_questions(slot, question, q_ref, k_ref, v_ref, grad_ref, cos_ref, sin_ref, dq_ref, dk_ref, dv_ref):
+    rest = slice(slot, q_ref.shape[0])
+    cosine = wide(cos_ref[rest, :])
+    sine = wide(sin_ref[rest, :])
+    apart = heads_apart(q_ref[rest, :], 4)
+    grad_apart = heads_apart(grad_ref[rest, :], 4)
+    key = k_ref[rest, :]
+    probs = question_probs(apart, key, question)
+    grad_prob = nt(grad_apart, v_ref[rest, :])
+    row_dot = jnp.sum(probs * grad_prob, axis=1, keepdims=True)
+    slope = (probs * (grad_prob - row_dot) * 0.125).astype(bf16)
+    dq_ref[rest, :] = rope_back(heads_joined(nn(slope, key), 4), cosine, sine).astype(bf16)
+    dk_ref[rest, :] = rope_back(tn(slope, apart), cosine, sine).astype(bf16)
+    dv_ref[rest, :] = tn(probs.astype(bf16), grad_apart).astype(bf16)
+
+
+def attend_back_step(slot, question, length_ref, q_ref, k_ref, v_ref, mixed_ref, grad_ref, mass_ref, cos_ref, sin_ref, dq_ref, dk_ref, dv_ref):
+    ins = (q_ref, k_ref, v_ref, mixed_ref, grad_ref, mass_ref, cos_ref, sin_ref)
+    for p in range(2):
+        back_pair(slot, p, length_ref[0], *ins, dq_ref, dk_ref, dv_ref)
+    back_questions(slot, question, q_ref, k_ref, v_ref, grad_ref, cos_ref, sin_ref, dq_ref, dk_ref, dv_ref)
+
+
+def attend_backward(length, q, k, v, mixed, grad, mass, cosine, sine, slot, question):
+    total, width = q.shape
+    groups = width // (4 * HEAD)
+    return pl.pallas_call(
+        functools.partial(attend_back_step, slot, question),
+        grid=(groups,),
+        in_specs=[pl.BlockSpec(memory_space=pltpu.SMEM)]
+        + [group_spec(total)] * 5
+        + [mass_spec(total), whole_spec((total, 2 * HEAD)), whole_spec((total, 2 * HEAD))],
+        out_specs=[group_spec(total)] * 3,
+        out_shape=[jax.ShapeDtypeStruct((total, width), bf16)] * 3,
+        compiler_params=pltpu.CompilerParams(vmem_limit_bytes=vmem_bytes),
+        name="attend_backward",
+    )(length, q, k, v, mixed, grad, mass, cosine, sine)
+
+
+back_plan = {
+    (0, 0): ["B0 B1 B2 B3", "B4 B5 B6 B7", "B8 B9 S0"],
+    (0, 1): ["S1 S2 S3"],
+    (0, 2): ["S4 S5"],
+    (0, 3): ["B10 S6 S7 F0"],
+    (1, 1): ["S8 S9 S10 F1"],
+    (1, 2): ["F2 L0"],
+    (1, 3): ["B11 F3 L1"],
+    (2, 1): ["S11 F4 L2"],
+    (2, 2): ["F5 L3 E0"],
+    (2, 3): ["B12 F6 L4 E1"],
+    (3, 1): ["S12 F7 L5 E2"],
+    (3, 2): ["F8 F9 F10 L6", "E3"],
+    (3, 3): ["B13 Vt F11 L7", "S13 L8 L9 F12", "L10 Vs E4 E5", "L11 Vf F13 E6", "E7 L12 E8 E9", "Vl E10 E11 L13", "E12 Ve E13"],
+}
+
+
+def back_body(slot, question, *refs):
+    (length_ref, q_ref, k_ref, v_ref, mixed_ref, grad_ref, mass_ref, cos_ref, sin_ref) = refs[:9]
+    (wq_ref, wk_ref, wv_ref, turned_ref, vec_ref, first_ref, outer_ref, inner_ref, output_ref, proj_ref) = refs[9:19]
+    (doc_ref, query_ref, outer_out, inner_out, output_out, proj_out, dwq_out, dwk_out, dwv_out, vec_out) = refs[19:29]
+    (grads, token_grad, stage, value, sums, heard) = refs[29:35]
+    flat = refs[35 : 35 + 14 * 5]
+    send_sem, recv_sem, own_sem, vec_send, vec_recv, copy_sem = refs[35 + 14 * 5 :]
+    step = pl.program_id(0)
+    place = Place()
+    group = 4 * HEAD
+
+    def lines(ref, core, *tail):
+        return lambda k: ref.at[(place.lines[k][0], slice(None), place.lines[k][1], core) + tail]
+
+    def matrix(u, ref, out, *tail):
+        return Unit(
+            place,
+            out,
+            lines(ref, place.c, *tail),
+            lines(ref, place.other, *tail),
+            flat[5 * u : 5 * u + 5],
+            send_sem.at[u],
+            recv_sem.at[u],
+            own_sem.at[u],
+        )
+
+    def into(ref, *where):
+        def put(block):
+            ref[where] = block
+
+        return put
+
+    everything = slice(None)
+    units = []
+    rows = outer_out.shape[0] // 4
+    for j in range(4):
+        part = slice(j * rows, (j + 1) * rows)
+        units.append(matrix(j, outer_ref, into(outer_out, part, everything), part))
+    columns = inner_out.shape[1] // 4
+    for j in range(4):
+        part = slice(j * columns, (j + 1) * columns)
+        units.append(matrix(4 + j, inner_ref, into(inner_out, everything, part), everything, part))
+    units.append(matrix(8, output_ref, into(output_out, everything, everything)))
+    units.append(matrix(9, proj_ref, into(proj_out, everything, everything)))
+
+    def heads_out(g):
+        part = slice(g * group, (g + 1) * group)
+
+        def put(block):
+            for i, ref in enumerate((dwq_out, dwk_out, dwv_out)):
+                ref[:, part] = block[:, i * group : (i + 1) * group]
+
+        return put
+
+    for g in range(4):
+        here = stage.at[g % 2]
+        u = 10 + g
+        units.append(
+            Unit(
+                place,
+                heads_out(g),
+                lines(here, place.c),
+                lines(here, place.other),
+                flat[5 * u : 5 * u + 5],
+                send_sem.at[u],
+                recv_sem.at[u],
+            )
+        )
+    vectors = VectorSum(place, value, sums, heard, vec_out, vec_send, vec_recv)
+    moves = {"B": "begin", "S": "to_second", "F": "to_first", "L": "to_line", "E": "finish"}
+    tells = {"t": "twin", "s": "second", "f": "first", "l": "line", "e": "finish"}
+
+    def pump(spot):
+        for g in range(4):
+            todo = [name for some in back_plan.get((g, spot), []) for name in some.split()]
+            if todo:
+
+                @pl.when(step == g)
+                def _():
+                    for name in todo:
+                        if name[0] == "V":
+                            getattr(vectors, tells[name[1]])()
+                        else:
+                            getattr(units[int(name[1:])], moves[name[0]])()
+
+    seed = pltpu.make_async_copy(first_ref, token_grad, copy_sem.at[0])
+
+    @pl.when(step == 0)
+    def _():
+        place.greet()
+        seed.start()
+        value[...] = vec_ref[...]
+
+    ins = (q_ref, k_ref, v_ref, mixed_ref, grad_ref, mass_ref, cos_ref, sin_ref)
+    dq, dk, dv = [grads.at[:, i * group : (i + 1) * group] for i in range(3)]
+    pump(0)
+    for p in range(2):
+        back_pair(slot, p, length_ref[0], *ins, dq, dk, dv)
+        pump(1 + p)
+    back_questions(slot, question, q_ref, k_ref, v_ref, grad_ref, cos_ref, sin_ref, dq, dk, dv)
+    for g in range(2, 4):
+
+        @pl.when(step == g)
+        def _():
+            units[8 + g].drain_twin()
+
+    weight = nn(turned_ref[...], grads[...]).astype(bf16)
+    stage[lax.rem(step, 2)] = weight.reshape(stage.shape[1:])
+    column_sums = jnp.sum(grads[...].astype(f32), axis=0, keepdims=True)
+    for g in range(4):
+
+        @pl.when(step == g)
+        def _():
+            for i in range(3):
+                value[10 + i : 11 + i, g * group : (g + 1) * group] = column_sums[:, i * group : (i + 1) * group]
+
+    @pl.when(step == 0)
+    def _():
+        seed.wait()
+
+    token_grad[...] += nt(dq[...], wq_ref[...]) + nt(dk[...], wk_ref[...]) + nt(dv[...], wv_ref[...])
+    docs = pltpu.make_async_copy(token_grad.at[0:slot], doc_ref, copy_sem.at[1])
+    asked = pltpu.make_async_copy(token_grad.at[slot:], query_ref, copy_sem.at[2])
+
+    @pl.when(step == 3)
+    def _():
+        docs.start()
+        asked.start()
+
+    pump(3)
+
+    @pl.when(step == 3)
+    def _():
+        for u in range(14):
+            if u not in (10, 11):
+                units[u].drain_twin()
+            units[u].drain()
+        vectors.sender.drain()
+        docs.wait()
+        asked.wait()
+
+
+def unit_buffers(shape, dtype):
+    return [
+        pltpu.VMEM((4, 4) + shape, dtype),
+        pltpu.VMEM((4, 4) + shape, dtype),
+        pltpu.VMEM((2, 4) + shape, dtype),
+        pltpu.VMEM((4,) + shape, dtype),
+        pltpu.VMEM((3,) + shape, dtype),
+    ]
+
+
+def back_close(length, q, k, v, mixed, grad, mass, cosine, sine, slot, question, tokens, weights, vectors, first_grad, parts):
+    total, width = q.shape
+    group = 4 * HEAD
+    shapes = [(p.shape[0] // 32, p.shape[1]) for p in parts]
+    outer, inner, output, proj = shapes
+    unit_shapes = [(outer[0] // 4, outer[1])] * 4 + [(inner[0], inner[1] // 4)] * 4 + [output, proj]
+    unit_shapes += [(width // 32, 3 * group)] * 4
+    scratch = []
+    for shape in unit_shapes:
+        scratch += unit_buffers(shape, bf16)
+    once = pl.Buffered(1)
+    hbm = pl.BlockSpec(memory_space=pl.ANY)
+
+    def kept(shape):
+        return pl.BlockSpec(shape, lambda i: (0,) * len(shape), pipeline_mode=once)
+
+    shard = (width // 32, width)
+    outs = [outer, inner, output, proj, shard, shard, shard, vectors.shape]
+    return pl.pallas_call(
+        functools.partial(back_body, slot, question),
+        grid=(width // group,),
+        in_specs=[pl.BlockSpec(memory_space=pltpu.SMEM)]
+        + [group_spec(total)] * 3
+        + [pl.BlockSpec((total, group), lambda i: (0, i), pipeline_mode=once)] * 2
+        + [mass_spec(total), kept((total, 2 * HEAD)), kept((total, 2 * HEAD))]
+        + [pl.BlockSpec((width, group), lambda i: (0, i), pipeline_mode=once)] * 3
+        + [kept((width, total)), kept(vectors.shape)]
+        + [hbm] * 5,
+        out_specs=[hbm, hbm] + [kept(shape) for shape in outs],
+        out_shape=[jax.ShapeDtypeStruct((slot, width), f32), jax.ShapeDtypeStruct((total - slot, width), f32)]
+        + [jax.ShapeDtypeStruct(shape, f32) for shape in outs],
+        scratch_shapes=[
+            pltpu.VMEM((total, 3 * group), bf16),
+            pltpu.VMEM((total, width), f32),
+            pltpu.VMEM((2, 2, 4, 2, 2, width // 32, 3 * group), bf16),
+            pltpu.VMEM(vectors.shape, f32),
+            pltpu.VMEM((3,) + vectors.shape, f32),
+            pltpu.VMEM((6,) + vectors.shape, f32),
+        ]
+        + scratch
+        + [
+            pltpu.SemaphoreType.DMA((14, 10)),
+            pltpu.SemaphoreType.DMA((14, 10)),
+            pltpu.SemaphoreType.DMA((14, 4)),
+            pltpu.SemaphoreType.DMA((6,)),
+            pltpu.SemaphoreType.DMA((6,)),
+            pltpu.SemaphoreType.DMA((3,)),
+        ],
+        compiler_params=pltpu.CompilerParams(collective_id=4, has_side_effects=True, vmem_limit_bytes=67043328),
+        name="back",
+    )(
+        length, q, k, v, mixed, grad, mass, cosine, sine, *weights, tokens.T, vectors, first_grad,
+        *[p.reshape((2, 4, 2, 2) + shape) for p, shape in zip(parts, shapes)],
+    )
+
+
 def rotary_tables(slot, question, count):
     place = np.concatenate([np.arange(slot)] + [np.arange(question)] * count)
     channel = np.arange(HEAD // 2, dtype=np.float32)[None, :]
@@ -579,6 +1156,16 @@
         chosen = packs[:, 1 + count, : positives.shape[0]].reshape(-1).astype(jnp.int32)
         return wholes, small, packs[:, 0].reshape(-1), chosen
 
+    def forward(self, attend, shards, row_vectors, inner_bias):
+        tokens = attend[1]
+        output_shard, inner_shard, outer_shard, proj_shard = shards
+        outs, (w_output, w_inner) = attend_gather(*attend, [output_shard, inner_shard])
+        mixed = outs[3]
+        (normal, inverse, low, activated, slope), (w_outer, w_proj) = inner_forward(
+            tokens, mixed, w_output, w_inner, jnp.stack(row_vectors), inner_bias[None], [outer_shard, proj_shard]
+        )
+        return outs, normal, inverse[:, :1], low, activated, slope, (w_output, w_inner, w_outer, w_proj)
+
     def rows(self, rows):
         return gather([rows], 1)[0]
 
@@ -589,22 +1176,21 @@
     def row_grads(self, grads):
         return scatter([grads], 3)[0]
 
-    def grads(self, matrices, vectors, wide_vector):
-        count, size = len(vectors), vectors[0].shape[0] // 32
-        lanes = wide_vector.shape[0] // 32
-        small = jnp.stack(vectors).reshape(count, 32, size).transpose(1, 0, 2)
-        small = jnp.pad(small, ((0, 0), (0, 15 - count), (0, lanes - size)))
-        pack = jnp.concatenate([wide_vector.reshape(32, 1, lanes), small], axis=1)
-        *shards, packed = scatter(list(matrices) + [pack.reshape(32 * 16, lanes)], 4)
-        return shards, [packed[1 + i, :size] for i in range(count)], packed[0]
+    def back(self, attend, tokens, weights, vectors, inner_bias_grad, first_grad, parts):
+        width = tokens.shape[1]
+        slot = attend[-2]
+        rows = jnp.concatenate([inner_bias_grad.reshape(4, width), jnp.stack(vectors)])
+        rows = jnp.pad(rows, ((0, 16 - rows.shape[0]), (0, 0)))
+        docs, asked, *shards, sums = back_close(*attend, tokens, weights, rows, first_grad, parts)
+        index = lax.axis_index(AXES)
+        small = lax.dynamic_slice_in_dim(sums[4:13], index * (width // 32), width // 32, 1)
+        inner_bias_shard = lax.dynamic_slice_in_dim(sums[:4].reshape(-1), index * (width // 8), width // 8, 0)
+        return docs, asked, shards, [small[i] for i in range(9)], inner_bias_shard
 
 
 class Far:
     def one(self, value):
         return lax.all_gather(value, AXES, axis=0, tiled=True)
-
-    def back(self, value):
-        return lax.psum_scatter(value.astype(f32), AXES, scatter_dimension=0, tiled=True)
 
     def weights(self, matrices, vectors, wide_vector, positives):
         return (
@@ -614,6 +1200,16 @@
             self.one(positives),
         )
 
+    def forward(self, attend, shards, row_vectors, inner_bias):
+        tokens = attend[1]
+        weights = [self.one(m) for m in shards]
+        outs = attend_forward(*attend)
+        bias, gain, shift = row_vectors
+        normal, inverse = normalize_rows(tokens.astype(f32) + dense(outs[3], weights[0]) + bias)
+        low = (normal * gain + shift).astype(bf16)
+        activated, slope = gelu_both(dense(low, weights[1]) + inner_bias.astype(f32))
+        return outs, normal, inverse, low, activated.astype(bf16), slope.astype(bf16), weights
+
     def rows(self, rows):
         return self.one(rows)
 
@@ -621,10 +1217,26 @@
         return self.one(totals[None])
 
     def row_grads(self, grads):
-        return self.back(grads)
-
-    def grads(self, matrices, vectors, wide_vector):
-        return [self.back(m) for m in matrices], [self.back(v) for v in vectors], self.back(wide_vector)
+        return self.spread(grads)
+
+    def spread(self, value):
+        return lax.psum_scatter(value.astype(f32), AXES, scatter_dimension=0, tiled=True)
+
+    def back(self, attend, tokens, weights, vectors, inner_bias_grad, first_grad, parts):
+        slot = attend[-2]
+        grads = attend_backward(*attend)
+        total = first_grad
+        for grad, weight in zip(grads, weights):
+            total = total + dense_back(grad, weight)
+        parts = list(parts) + [weight_grad(tokens, grad) for grad in grads]
+        vectors = list(vectors) + [row_sum(grad) for grad in grads]
+        return (
+            total[:slot],
+            total[slot:],
+            [self.spread(part) for part in parts],
+            [self.spread(vector) for vector in vectors],
+            self.spread(inner_bias_grad),
+        )
 
 
 def local(
@@ -657,7 +1269,7 @@
     cosine, sine = rotary_tables(slot, question, count)
 
     matrices, vectors, b_inner, chosen = link.weights(
-        [query_weight, key_weight, value_weight, output_weight, inner_weight, outer_weight, proj_weight],
+        [query_weight, key_weight, value_weight],
         [
             query_bias,
             key_bias,
@@ -672,19 +1284,18 @@
         inner_bias,
         positives,
     )
-    w_query, w_key, w_value, w_output, w_inner, w_outer, w_proj = matrices
+    w_query, w_key, w_value = matrices
     b_output, g_attn, s_attn, b_outer, g_final, s_final = [vectors[i].astype(f32) for i in range(3, 9)]
 
-    query_rot, key_rot, value_low, mixed, mass = attend_forward(
-        doc_lengths, tokens, w_query, w_key, w_value, vectors[0:8], cosine, sine, slot, question
+    outs, first_normal, first_inverse, normed_low, activated, slope, matrices = link.forward(
+        (doc_lengths, tokens, w_query, w_key, w_value, vectors[0:8], cosine, sine, slot, question),
+        [output_weight, inner_weight, outer_weight, proj_weight],
+        [b_output, g_attn, s_attn],
+        b_inner,
     )
-    attended = dense(mixed, w_output) + b_output
-    first_normal, first_inverse = normalize_rows(tokens.astype(f32) + attended)
+    query_rot, key_rot, value_low, mixed, mass = outs
+    w_output, w_inner, w_outer, w_proj = matrices
     normed = first_normal * g_attn + s_attn
-    normed_low = normed.astype(bf16)
-    activated, slope = gelu_both(dense(normed_low, w_inner) + b_inner.astype(f32))
-    activated = activated.astype(bf16)
-    slope = slope.astype(bf16)
     outer_branch = dense(activated, w_outer) + b_outer
     second_normal, second_inverse = normalize_rows(normed + outer_branch)
     states_low = (second_normal * g_final + s_final).astype(bf16)
@@ -760,54 +1371,40 @@
     output_weight_grad = weight_grad(mixed, attended_grad)
     output_bias_grad = row_sum(attended_grad)
     mixed_grad = dense_back(attended_grad, w_output).astype(bf16)
-    query_grad, key_grad, value_grad = attend_backward(
-        doc_lengths, query_rot, key_rot, value_low, mixed, mixed_grad, mass, cosine, sine, slot, question
+    attend = (
+        doc_lengths, query_rot, key_rot, value_low, mixed, mixed_grad, mass, cosine, sine, slot, question,
     )
-    tokens_grad = (
-        first_grad
-        + dense_back(query_grad, w_query)
-        + dense_back(key_grad, w_key)
-        + dense_back(value_grad, w_value)
+    docs_grad, asked_grad, shards, small, inner_bias_shard = link.back(
+        attend,
+        tokens,
+        (w_query, w_key, w_value),
+        [outer_bias_grad, final_gain_grad, final_shift_grad, attn_gain_grad, attn_shift_grad, output_bias_grad],
+        inner_bias_grad,
+        first_grad,
+        [outer_weight_grad, inner_weight_grad, output_weight_grad, proj_weight_grad],
     )
-    shards, small, inner_bias_shard = link.grads(
-        [
-            outer_weight_grad,
-            inner_weight_grad,
-            proj_weight_grad,
-            output_weight_grad,
-            weight_grad(tokens, query_grad),
-            weight_grad(tokens, key_grad),
-            weight_grad(tokens, value_grad),
-        ],
-        [
-            row_sum(query_grad),
-            row_sum(key_grad),
-            row_sum(value_grad),
-            output_bias_grad,
-            attn_gain_grad,
-            attn_shift_grad,
-            outer_bias_grad,
-            final_gain_grad,
-            final_shift_grad,
-        ],
-        inner_bias_grad,
-    )
-    outer_shard, inner_shard, proj_shard, output_shard, query_shard, key_shard, value_shard = shards
+    outer_shard, inner_shard, output_shard, proj_shard, query_shard, key_shard, value_shard = shards
+    b_outer_shard, gain_shard, shift_shard, attn_gain_shard, attn_shift_shard, b_output_shard, *b_heads = small
     return (
         query_loss,
         states_low[None, :slot],
         states_low[slot:].reshape(count, question, width),
-        tokens_grad[None, :slot],
-        tokens_grad[slot:].reshape(count, question, width),
+        docs_grad[None],
+        asked_grad.reshape(count, question, width),
         query_shard,
         key_shard,
         value_shard,
         output_shard,
-        *small[:6],
+        *b_heads,
+        b_output_shard,
+        attn_gain_shard,
+        attn_shift_shard,
         inner_shard,
         inner_bias_shard,
         outer_shard,
-        *small[6:],
+        b_outer_shard,
+        gain_shard,
+        shift_shard,
         proj_shard,
     )
 

time: 665 us -> 542 us (0.82); the launches traced: 654 us -> 539 us
  Pallas kernels: 425 us -> 366 us
  matrix products: 160 us -> 105 us
  local copies, waits for them, and re-layouts: 28.3 us -> 40.2 us
  other arithmetic: 36.8 us -> 24.9 us
    pallas_call x2 -> x3, Pallas kernels: 86.4 us -> 277 us  [the longest x1 139 us: back_close(): pl.pallas_call(functools.partial(back_body, slot, question), grid=(width...]
    pallas_call x2 -> x1, Pallas kernels: 169 us -> 14.4 us  [scatter(): pl.pallas_call(functools.partial(scatter_body, count), in_specs=[pl.Block...]
    pallas_call x3, Pallas kernels: 170 us -> 74.9 us  [gather(): pl.pallas_call(functools.partial(gather_body, count), in_specs=[pl.BlockS...]
    dot_general x4 -> x2, matrix products: 44.9 us -> 17.4 us  [dense(): return jnp.einsum('ld,de->le', operand, matrix, preferred_element_type=f32)]
    dot_general x7 -> x4, matrix products: 57 us -> 42.8 us  [dense_back(): return jnp.einsum('le,de->ld', gradient, matrix, preferred_element_type=f32)]
    dot_general x7 -> x4, matrix products: 50.3 us -> 38.2 us  [weight_grad(): jnp.einsum('ld,le->de', operand, gradient, preferred_element_type=f32)]
    unnamed x74 -> x63, local copies, waits for them, and re-layouts: 11 us -> 16.7 us
where the time goes in v2:
time: 542 us; the launch traced here: 539 us
  Pallas kernels  366 us (68%)
  matrix products  105 us (19%)
  local copies, waits for them, and re-layouts  40.2 us (7%)
  other arithmetic  24.9 us (5%)
    pallas_call x1, Pallas kernels, back_close(): pl.pallas_call(functools.partial(back_body, slot, question), grid=(width...  139 us
    pallas_call x1, Pallas kernels, attend_gather(): pl.pallas_call(functools.partial(attend_gather_body, slot, question), gri...  75.7 us
    pallas_call x3, Pallas kernels, gather(): pl.pallas_call(functools.partial(gather_body, count), in_specs=[pl.BlockS...  74.9 us
    pallas_call x1, Pallas kernels, inner_forward(): pl.pallas_call(lambda *refs: inner_body(refs), grid=(9,), in_specs=[kept(...  61.7 us
    dot_general x4, matrix products, dense_back(): return jnp.einsum('le,de->ld', gradient, matrix, preferred_element_type=f32)  42.8 us
    dot_general x4, matrix products, weight_grad(): jnp.einsum('ld,le->de', operand, gradient, preferred_element_type=f32)  38.2 us
    dot_general x2, matrix products, dense(): return jnp.einsum('ld,de->le', operand, matrix, preferred_element_type=f32)  17.4 us
    unnamed x63, local copies, waits for them, and re-layouts  16.7 us

profile of v2, /device:TPU:0, one launch (start us, length us, event | category | flops | bytes accessed | tf_op | source)
XLA Modules:
  0.0 538.7 jit_solution(1214168494029892643)
XLA Ops:
  2.0 1.5 stack.65
  5.8 3.9 copy.52
  9.7 4.1 fusion.28
  13.9 4.3 copy.57.refs_1_.refs_0_
  18.1 43.6 %gather.3 = (bf16[2,4,2,2,32,1024]{5,4,3,2,1,0:T(8,128)(2,1)}, bf16[2,4,2,2,32,1024]{5,4,3,2,1,0:T(8,128)(2,1)}, bf16[2,4,2,2,32,1024]{5,4,3,2,1,0:T(8,128)(2,1)}, bf16[2,4,2,2,16,128]{5,4,3,2,1,0:T(8,128)(2,1)}) custom-call(bf16[32,1024]{1,0:T(8,128)(2,1)} %refs_0_.3, bf16[32,1024]{1,0:T(8,128)(2,1)} %refs_1_.1, bf16[32,1024]{1,0:T(8,128)(2,1)} %refs_2_.1, ...), custom_call_target="tpu_custom_call" | custom-call | tf_op jit(solution)/shard_map/gather/pallas_call | solution.py:360
  62.8 1.5 slice_bitcast_fusion.1.refs_5_
  67.2 75.7 %attend_forward.1 = (bf16[1088,1024]{1,0:T(8,128)(2,1)}, bf16[1088,1024]{1,0:T(8,128)(2,1)}, bf16[1088,1024]{1,0:T(8,128)(2,1)}, bf16[1088,1024]{1,0:T(8,128)(2,...) custom-call(s32[1]{0:T(128)S(6)} %copy.96.refs_0_, ...), custom_call_target="tpu_custom_call" | custom-call | tf_op jit(solution)/shard_map/attend_forward/pallas_call | solution.py:433
  142.9 61.7 %inner_forward.1 = (f32[1088,1024]{1,0:T(8,128)}, f32[1088,128]{1,0:T(8,128)}, bf16[1088,1024]{1,0:T(8,128)(2,1)}, bf16[1088,4096]{1,0:T(8,128)(2,1)}, bf16[1088...) custom-call(bf16[1088,1024]{1,0:T(8,128)(2,1)} %copy.57.refs_1_.refs_0_, ...), custom_call_target="tpu_custom_call" | custom-call | tf_op jit(solution)/shard_map/inner_forward/pallas_call | solution.py:539
  204.6 1.3 slice_reduce_fusion
  205.9 16.5 %fusion.29 = (f32[1088]{0:T(1024)S(1)}, f32[1088,1024]{1,0:T(8,128)S(1)}) fusion(f32[1024]{0:T(1024)S(1)} %reshape.314, bf16[1088,4096]{1,0:T(8,128)(2,1)} %get-tuple-element.128, bf16[4096,1024]{1,0:T(8,128)(2,1)} %bitcast.196, f32[1024]{0:T(1024)S(1)} %reshape.313, f32[1088,1024]{1,0:T(8,128)} %get-tuple-element.127, f32[1024]{0:T(1024)S(1)} %reshape.312), kind=kOutput, calls=%fused_computation.108 | convolution fusion | flops 9132375040 | bytes 26231040 | tf_op jit(solution)/shard_map/ld,de->le/dot_general | solution.py:1104
  227.6 16.1 %gather.4 = bf16[2,4,2,2,64,128]{5,4,3,2,1,0:T(8,128)(2,1)S(1)} custom-call(bf16[64,128]{1,0:T(8,128)(2,1)} %slice.127.refs_0_), custom_call_target="tpu_custom_call" | custom-call | tf_op jit(solution)/shard_map/gather/pallas_call | solution.py:360
  243.8 5.2 while.24
  249.8 15.2 %gather.5 = f32[2,4,2,2,8,128]{5,4,3,2,1,0:T(8,128)} custom-call(f32[8,128]{1,0:T(8,128)} %broadcast_in_dim.100.refs_0_), custom_call_target="tpu_custom_call" | custom-call | tf_op jit(solution)/shard_map/gather/pallas_call | solution.py:360
  266.9 9.6 %while.25 = (s32[]{:T(128)}, f32[1024,128]{1,0:T(8,128)S(1)}, f32[2,1024,128]{2,1,0:T(8,128)}, bf16[2,1024,128]{2,1,0:T(8,128)(2,1)S(1)}, bf16[1024,128]{1,0:T(8...) while((s32[]{:T(128)}, f32[1024,128]{1,0:T(8,128)S(1)}, ...), condition=%wide.region_12.13_spmd.clone, body=%wide.region_11.12_spmd.clone.sunk | while | flops 810813440 | bytes 17328324 | solution.py:1345
  267.6 1.1 multiply_convert_fusion.3
  272.4 1.1 multiply_convert_fusion.3
  276.5 14.4 %scatter.1 = f32[64,128]{1,0:T(8,128)} custom-call(f32[2,4,2,2,64,128]{5,4,3,2,1,0:T(8,128)} %bitcast.161), custom_call_target="tpu_custom_call" | custom-call | tf_op jit(solution)/shard_map/scatter/pallas_call | solution.py:672
  290.9 1.2 multiply_reduce_fusion.7
  292.1 1.8 subtract_convert_fusion
  293.9 3.2 convolution_convert_fusion.4
  297.1 1.5 slice_bitcast_fusion
  298.6 1.9 multiply_reduce_fusion.1
  300.5 2.8 convert_reduce_fusion.2
  303.3 17.3 %convert_reduce_fusion = (f32[4096]{0:T(1024)S(1)}, bf16[1088,4096]{1,0:T(8,128)(2,1)}) fusion(bf16[1088,4096]{1,0:T(8,128)(2,1)} %get-tuple-element.138, bf16[4096,1024]{1,0:T(8,128)(2,1)} %bitcast.197, f32[1088,1024]{1,0:T(8,128)} %get-tuple-element.233), kind=kOutput, calls=%fused_computation.25 | convolution fusion | flops 9150197760 | bytes 30687232 | tf_op jit(solution)/shard_map/le,de->ld/dot_general | solution.py:1108
  320.6 17.7 %convolution_convert_fusion.1 = bf16[4096,1024]{1,0:T(8,128)(2,1)} fusion(bf16[1088,4096]{1,0:T(8,128)(2,1)} %get-tuple-element.128, f32[1088,1024]{1,0:T(8,128)} %get-tuple-element.233), kind=kOutput, calls=%fused_computation.28 | convolution fusion | flops 9132113920 | bytes 21757952 | tf_op jit(solution)/shard_map/ld,le->de/dot_general | solution.py:1112
  338.3 17.4 %multiply_reduce_fusion = (f32[1024]{0:T(1024)S(1)}, f32[1088]{0:T(1024)S(1)}, f32[1088]{0:T(1024)S(1)}, f32[1024]{0:T(1024)S(1)}, f32[1088,1024]{1,0:T(8,128)}) fusion(f32[1088,1024]{1,0:T(8,128)S(1)} %bitcast.156, f32[1024]{0:T(1024)S(1)} %reshape.312, f32[1088,1024]{1,0:T(8,128)S(1)} %copy-done.5, bf16[1088,4096]{1,0:T(8,128)(2,1)} %get-tuple-element.270, ...), kind=kOutput, calls=%fused_computation.33 | convolution fusion | flops 9135714304 | bytes 30691840 | tf_op jit(solution)/shard_map/le,de->ld/dot_general | solution.py:1108
  355.7 5.8 %convert_reduce_fusion.1 = (f32[1024]{0:T(1024)S(1)}, f32[1088,1024]{1,0:T(8,128)}) fusion(f32[1088,1024]{1,0:T(8,128)} %get-tuple-element.127, f32[1088]{0:T(1024)S(1)} %broadcast_multiply_fusion, f32[1088]{0:T(1024)S(1)} %broadcast_multiply_fusion.1, f32[1088,1024]{1,0:T(8,128)} %get-tuple-element.268, f32[1024]{0:T(1024)S(1)} %reshape.312, ...), kind=kLoop, calls=%fused_computation.32 | loop fusion | flops 8911872 | bytes 13390592 | tf_op jit(solution)/shard_map/reduce_sum | solution.py:1116
  362.3 6.3 %convolution_convert_fusion.2.refs_5_ = bf16[1088,1024]{1,0:T(8,128)(2,1)} fusion(bf16[1024,1024]{1,0:T(8,128)(2,1)S(1)} %bitcast.159, f32[1088,1024]{1,0:T(8,128)} %get-tuple-element.231.refs_14_), kind=kOutput, calls=%fused_computation.45 | convolution fusion | flops 2283929600 | bytes 8781824 | tf_op jit(solution)/shard_map/le,de->ld/dot_general | solution.py:1108
  368.6 4.1 convolution_convert_fusion.3
  372.7 13.1 %convolution_convert_fusion = bf16[1024,4096]{1,0:T(8,128)(2,1)} fusion(bf16[1088,1024]{1,0:T(8,128)(2,1)S(1)} %copy-done.19, bf16[1088,4096]{1,0:T(8,128)(2,1)S(1)} %bitcast.199), kind=kOutput, calls=%fused_computation.27 | convolution fusion | flops 9130999808 | bytes 19529728 | tf_op jit(solution)/shard_map/ld,le->de/dot_general | solution.py:1112
  385.9 139.3 %back.1 = (f32[1024,1024]{1,0:T(8,128)}, f32[64,1024]{1,0:T(8,128)}, f32[128,1024]{1,0:T(8,128)}, f32[32,4096]{1,0:T(8,128)}, f32[32,1024]{1,0:T(8,128)}, /*inde...) custom-call(s32[1]{0:T(128)S(6)} %copy.96.refs_0_, ...), custom_call_target="tpu_custom_call" | custom-call | tf_op jit(solution)/shard_map/back/pallas_call | solution.py:1053
  528.1 4.9 copy.97
  (146 shorter events, 36.0 us)
Async XLA Ops:
  222.4 2.1 copy-start
  223.0 2.9 copy-start.12
  224.5 1.4 copy-start.1
  268.7 1.2 copy-start.7
  270.7 1.1 copy-start.8
  273.5 1.2 copy-start.7
  275.4 1.1 copy-start.8
  290.9 6.2 %copy-start.2 = (bf16[1088,1024]{1,0:T(8,128)(2,1)S(1)}, bf16[1088,1024]{1,0:T(8,128)(2,1)}, u32[]{:S(2)}) copy-start(bf16[1088,1024]{1,0:T(8,128)(2,1)} %copy-done.1) | copy-start | bytes 6684676
  290.9 7.7 %slice-start = ((s8[4456448]{0:T(1024)(128)(4,1)}), s8[4194304]{0:T(1024)(128)(4,1)S(1)}, s32[]{:S(2)}) async-start(s8[4456448]{0:T(1024)(128)(4,1)} %bitcast.141), calls=%async_computation | async-start | bytes 8388608
  293.9 4.8 slice-start.1
  293.9 4.7 copy-start.13
  303.3 35.0 %slice-start.2 = ((s8[4456448]{0:T(1024)(128)(4,1)}), s8[262144]{0:T(1024)(128)(4,1)S(1)}, s32[]{:S(2)}) async-start(s8[4456448]{0:T(1024)(128)(4,1)} %bitcast.155), calls=%async_computation.2 | async-start | bytes 524288
  320.6 17.7 %slice-start.3 = ((s8[4456448]{0:T(1024)(128)(4,1)}), s8[4194304]{0:T(1024)(128)(4,1)S(1)}, s32[]{:S(2)}) async-start(s8[4456448]{0:T(1024)(128)(4,1)} %bitcast.155), calls=%async_computation.3 | async-start | bytes 8388608
  320.6 17.7 %copy-start.5 = (f32[1088,1024]{1,0:T(8,128)S(1)}, f32[1088,1024]{1,0:T(8,128)}, u32[]{:S(2)}) copy-start(f32[1088,1024]{1,0:T(8,128)} %get-tuple-element.233) | copy-start | bytes 13369348
  355.7 6.5 %copy-start.6 = (bf16[2,4,2,2,32,1024]{5,4,3,2,1,0:T(8,128)(2,1)S(1)}, bf16[2,4,2,2,32,1024]{5,4,3,2,1,0:T(8,128)(2,1)}, u32[]{:S(2)}) copy-start(bf16[2,4,2,2,32,1024]{5,4,3,2,1,0:T(8,128)(2,1)} %get-tuple-element.125) | copy-start | bytes 6291460
  362.3 6.3 %copy-start.3 = (f32[1088,1024]{1,0:T(8,128)S(1)}, f32[1088,1024]{1,0:T(8,128)}, u32[]{:S(2)}) copy-start(f32[1088,1024]{1,0:T(8,128)} %get-tuple-element.231.refs_14_) | copy-start | bytes 13369348
  362.3 6.3 %copy-start.4 = (bf16[1088,1024]{1,0:T(8,128)(2,1)S(1)}, bf16[1088,1024]{1,0:T(8,128)(2,1)}, u32[]{:S(2)}) copy-start(bf16[1088,1024]{1,0:T(8,128)(2,1)} %get-tuple-element.124.refs_1_.refs_4_) | copy-start | bytes 6684676
  362.3 10.5 %slice-start.4 = ((s8[8912896]{0:T(1024)(128)(4,1)}), s8[4194304]{0:T(1024)(128)(4,1)S(1)}, s32[]{:S(2)}) async-start(s8[8912896]{0:T(1024)(128)(4,1)} %bitcast.198), calls=%async_computation.4 | async-start | bytes 8388608
  362.3 10.5 %slice-start.5 = ((s8[8912896]{0:T(1024)(128)(4,1)}), s8[4194304]{0:T(1024)(128)(4,1)S(1)}, s32[]{:S(2)}) async-start(s8[8912896]{0:T(1024)(128)(4,1)} %bitcast.198), calls=%async_computation.5 | async-start | bytes 8388608
  368.6 4.2 copy-start.19
  368.6 4.2 slice-start.6
  525.2 7.8 %copy-start.11 = (f32[64,1024]{1,0:T(8,128)S(1)}, f32[64,1024]{1,0:T(8,128)}, u32[]{:S(2)}) copy-start(f32[64,1024]{1,0:T(8,128)} %get-tuple-element.142) | copy-start | bytes 786436
  528.0 5.7 %copy-start.17 = (f32[32,1024]{1,0:T(8,128)S(1)}, f32[32,1024]{1,0:T(8,128)}, u32[]{:S(2)}) copy-start(f32[32,1024]{1,0:T(8,128)} %get-tuple-element.439) | copy-start | bytes 393220
  528.0 6.3 %copy-start.16 = (f32[32,1024]{1,0:T(8,128)S(1)}, f32[32,1024]{1,0:T(8,128)}, u32[]{:S(2)}) copy-start(f32[32,1024]{1,0:T(8,128)} %get-tuple-element.440) | copy-start | bytes 393220
  528.0 7.0 %copy-start.15 = (f32[32,1024]{1,0:T(8,128)S(1)}, f32[32,1024]{1,0:T(8,128)}, u32[]{:S(2)}) copy-start(f32[32,1024]{1,0:T(8,128)} %get-tuple-element.441) | copy-start | bytes 393220
  528.0 7.6 %copy-start.14 = (f32[32,1024]{1,0:T(8,128)S(1)}, f32[32,1024]{1,0:T(8,128)}, u32[]{:S(2)}) copy-start(f32[32,1024]{1,0:T(8,128)} %get-tuple-element.442) | copy-start | bytes 393220
  528.0 8.3 %copy-start.10 = (f32[32,4096]{1,0:T(8,128)S(1)}, f32[32,4096]{1,0:T(8,128)}, u32[]{:S(2)}) copy-start(f32[32,4096]{1,0:T(8,128)} %get-tuple-element.449) | copy-start | bytes 1572868
  528.0 9.1 %copy-start.9 = (f32[128,1024]{1,0:T(8,128)S(1)}, f32[128,1024]{1,0:T(8,128)}, u32[]{:S(2)}) copy-start(f32[128,1024]{1,0:T(8,128)} %get-tuple-element.451) | copy-start | bytes 1572868
  528.0 9.8 %copy-start.18 = (f32[32,128]{1,0:T(8,128)S(1)}, f32[32,128]{1,0:T(8,128)}, u32[]{:S(2)}) copy-start(f32[32,128]{1,0:T(8,128)} %get-tuple-element.455) | copy-start | bytes 49156

commit v3 on v2

--- a/solution.py
+++ b/solution.py
@@ -266,10 +266,13 @@
         return pltpu.make_async_copy(self.shards[t], self.mine(t), self.own_sem.at[t])
 
     def begin(self, t):
-        for k, peer in enumerate(self.at.along):
+        at = self.at
+        targets = [(k, 0, peer) for k, peer in enumerate(at.along)]
+        targets += [(3, 1, at.first), (4, 2, at.second), (5, 4, at.twin)]
+        for send, recv, peer in targets:
             self.out.go(
-                lambda k=k, peer=peer: (
-                    self.shards[t], self.mine(t), self.send_sem.at[t, k], self.recv_sem.at[t, 0], peer,
+                lambda send=send, recv=recv, peer=peer: (
+                    self.shards[t], self.mine(t), self.send_sem.at[t, send], self.recv_sem.at[t, recv], peer,
                 )
             )
         self.own(t).start()
@@ -289,8 +292,17 @@
     def own_line(self, t):
         at = self.at
         arrived(self.block(t, at.y, slice(0, 3), at.x, at.c), self.recv_sem.at[t, 0])
-        self.own(t).wait()
-        self.pass_line(t, 0, [(3, 1, at.first), (4, 2, at.second), (5, 4, at.twin)])
+        for j, (recv, peer) in enumerate([(1, at.first), (2, at.second), (4, at.twin)]):
+            for k in range(3):
+                self.out.go(
+                    lambda send=10 + 3 * j + k, recv=recv, peer=peer, z=at.ahead[k]: (
+                        self.block(t, at.y, z, at.x, at.c),
+                        self.block(t, at.y, z, at.x, at.c),
+                        self.send_sem.at[t, send],
+                        self.recv_sem.at[t, recv],
+                        peer,
+                    )
+                )
 
     def first_line(self, t):
         at = self.at
@@ -306,6 +318,7 @@
         self.pass_line(t, 3, [(9, 7, self.at.twin)])
 
     def twin_lines(self, t):
+        self.own(t).wait()
         for k in range(4):
             arrived(self.line(t, k, self.at.other), self.recv_sem.at[t, 4 + k])
 
@@ -321,7 +334,7 @@
 
 def gather_sems(count):
     return [
-        pltpu.SemaphoreType.DMA((count, 10)),
+        pltpu.SemaphoreType.DMA((count, 19)),
         pltpu.SemaphoreType.DMA((count, 8)),
         pltpu.SemaphoreType.DMA((count,)),
     ]
@@ -373,11 +386,14 @@
 
 attend_plan = {
     (0, 2): ["O0"],
-    (1, 1): ["O1 F0 S0"],
-    (2, 0): ["O2 F1 S1 R0"],
-    (2, 2): ["O3 F2 S2 R1"],
-    (3, 1): ["R2"],
-    (3, 2): ["O4 F3 S3"],
+    (1, 1): ["O1"],
+    (1, 2): ["F0 S0"],
+    (2, 0): ["O2"],
+    (2, 1): ["F1 S1"],
+    (2, 2): ["R0 O3"],
+    (3, 0): ["F2 S2"],
+    (3, 1): ["R1 O4"],
+    (3, 2): ["F3 S3 R2"],
     (3, 3): ["F4 S4 R3 R4"],
 }
 
@@ -396,14 +412,14 @@
 
 def attend_gather_body(slot, question, *refs):
     ins, shards = refs[:8], refs[8:10]
-    outs, wholes = refs[10:15], refs[15:17]
+    outs, turned_ref, wholes = refs[10:15], refs[15], refs[16:18]
     step = pl.program_id(0)
     place = Place()
     width = shards[1].shape[1] // 4
     cuts = [slice(j * width, (j + 1) * width) for j in range(4)]
     units = [shards[0]] + [shards[1].at[:, cut] for cut in cuts]
     places = [wholes[0]] + [(wholes[1], (slice(None), cut)) for cut in cuts]
-    run = Gather(place, units, places, *refs[17:])
+    run = Gather(place, units, places, *refs[18:])
 
     @pl.when(step == 0)
     def _():
@@ -411,6 +427,9 @@
         for t in range(len(units)):
             run.begin(t)
 
+    columns = pl.ds(pl.multiple_of(step * 4 * HEAD, 4 * HEAD), 4 * HEAD)
+    turned_ref[:, 0:slot] = ins[1][0:slot, columns].T
+    turned_ref[:, slot:] = ins[1][slot:, columns].T
     go = pump(run, step, attend_plan, 4)
     attend_step(slot, question, *ins, *outs, go=go)
 
@@ -430,7 +449,7 @@
     def kept(shape):
         return pl.BlockSpec(shape, lambda i: (0,) * len(shape), pipeline_mode=once)
 
-    *outs, first, second = pl.pallas_call(
+    *outs, turned, first, second = pl.pallas_call(
         functools.partial(attend_gather_body, slot, question),
         grid=(groups,),
         in_specs=[
@@ -444,15 +463,17 @@
             kept((total, 2 * HEAD)),
         ]
         + [kept(a.shape) for a in shards],
-        out_specs=[group_spec(total)] * 4 + [mass_spec(total)] + [pl.BlockSpec(memory_space=pl.ANY)] * 2,
+        out_specs=[group_spec(total)] * 4
+        + [mass_spec(total), pl.BlockSpec((4 * HEAD, total), lambda i: (i, 0))]
+        + [pl.BlockSpec(memory_space=pl.ANY)] * 2,
         out_shape=[jax.ShapeDtypeStruct((total, width), bf16)] * 4
-        + [jax.ShapeDtypeStruct((groups, 8, total), f32)]
+        + [jax.ShapeDtypeStruct((groups, 8, total), f32), jax.ShapeDtypeStruct((width, total), bf16)]
         + [spread_shape(a) for a in shards],
         scratch_shapes=gather_sems(5),
         compiler_params=pltpu.CompilerParams(collective_id=5, has_side_effects=True, vmem_limit_bytes=vmem_bytes),
         name="attend_forward",
     )(length, tokens, wq, wk, wv, biases, cosine, sine, *shards)
-    return outs, [joined_shards(first), joined_shards(second)]
+    return outs, turned, [joined_shards(first), joined_shards(second)]
 
 
 inner_plan = {
@@ -467,16 +488,16 @@
 }
 
 
-def inner_body(refs):
+def inner_body(slot, refs):
     (tokens_ref, mixed_ref, wo_ref, wi_ref, vec_ref, bias_ref, outer_ref, proj_ref) = refs[:8]
-    (normal_ref, inverse_ref, low_ref, act_ref, slope_ref, outer_whole, proj_whole) = refs[8:15]
+    (normal_ref, inverse_ref, low_ref, act_ref, slope_ref, turned_ref, outer_whole, proj_whole) = refs[8:16]
     step = pl.program_id(0)
     place = Place()
     rows = outer_ref.shape[0] // 4
     cuts = [slice(j * rows, (j + 1) * rows) for j in range(4)]
     units = [outer_ref.at[cut] for cut in cuts] + [proj_ref]
     places = [(outer_whole, (cut,)) for cut in cuts] + [proj_whole]
-    run = Gather(place, units, places, *refs[15:])
+    run = Gather(place, units, places, *refs[16:])
     total = tokens_ref.shape[0]
 
     @pl.when(step == 0)
@@ -508,6 +529,10 @@
             return carry
 
         lax.fori_loop(0, 4, some, 0)
+        slab = turned_ref.shape[0]
+        columns = pl.ds(pl.multiple_of((step - 1) * slab, slab), slab)
+        turned_ref[:, 0:slot] = low_ref[0:slot, columns].T
+        turned_ref[:, slot:] = low_ref[slot:, columns].T
 
     for g in range(1, 9):
         if (g, 0) in inner_plan:
@@ -524,7 +549,7 @@
         run.out.drain()
 
 
-def inner_forward(tokens, mixed, wo, wi, vectors, bias, shards):
+def inner_forward(tokens, mixed, wo, wi, vectors, bias, slot, shards):
     total, width = tokens.shape
     hidden = wi.shape[1]
     chunk = hidden // 8
@@ -537,12 +562,13 @@
         return pl.BlockSpec((rows, chunk), lambda i: (0, jnp.maximum(i - 1, 0)))
 
     *outs, outer, proj = pl.pallas_call(
-        lambda *refs: inner_body(refs),
+        lambda *refs: inner_body(slot, refs),
         grid=(9,),
         in_specs=[kept((total, width)), kept((total, width)), kept((width, width)), chunked(width), kept(vectors.shape)]
         + [chunked(1)]
         + [kept(a.shape) for a in shards],
         out_specs=[kept((total, width)), kept((total, 128)), kept((total, width)), chunked(total), chunked(total)]
+        + [pl.BlockSpec((width // 8, total), lambda i: (jnp.maximum(i - 1, 0), 0))]
         + [pl.BlockSpec(memory_space=pl.ANY)] * 2,
         out_shape=[
             jax.ShapeDtypeStruct((total, width), f32),
@@ -550,6 +576,7 @@
             jax.ShapeDtypeStruct((total, width), bf16),
             jax.ShapeDtypeStruct((total, hidden), bf16),
             jax.ShapeDtypeStruct((total, hidden), bf16),
+            jax.ShapeDtypeStruct((width, total), bf16),
         ]
         + [spread_shape(a) for a in shards],
         scratch_shapes=gather_sems(5),
@@ -687,6 +714,14 @@
     )(*[p.reshape((2, 4, 2, 2) + shape) for p, shape in zip(parts, shapes)])
 
 
+def add_blocks(out, left, right):
+    def one(z, carry):
+        out[z] = left[z] + right[z]
+        return carry
+
+    lax.fori_loop(0, out.shape[0], one, 0)
+
+
 class Unit:
     twin_slot = (0, 2, 1, 3)
 
@@ -713,10 +748,8 @@
         if self.own_sem is not None:
             self.own(k).wait()
         arrived(self.twin.at[k], self.recv_sem.at[k])
-        if self.own_sem is not None:
-            self.total[k] = self.total[k] + self.twin[k]
-        else:
-            self.total[k] = self.mine(k)[...] + self.twin[k]
+        base = self.total.at[k] if self.own_sem is not None else self.mine(k)
+        add_blocks(self.total.at[k], base, self.twin.at[k])
 
     def to_second(self):
         self.join_twin(3)
@@ -728,14 +761,14 @@
 
     def to_first(self):
         arrived(self.second.at[1], self.recv_sem.at[5])
-        self.total[1] = self.total[1] + self.second[1]
+        add_blocks(self.total.at[1], self.total.at[1], self.second.at[1])
         self.sender.go(lambda: (self.total.at[1], self.first, self.send_sem.at[6], self.recv_sem.at[6], self.at.first))
         arrived(self.second.at[0], self.recv_sem.at[4])
-        self.total[0] = self.total[0] + self.second[0]
+        add_blocks(self.total.at[0], self.total.at[0], self.second.at[0])
 
     def to_line(self):
         arrived(self.first, self.recv_sem.at[6])
-        self.total[0] = self.total[0] + self.first[...]
+        add_blocks(self.total.at[0], self.total.at[0], self.first)
         for k, peer in enumerate(self.at.along):
             self.sender.go(lambda k=k, peer=peer: (self.total.at[0, self.at.ahead[k]], self.last.at[k], self.send_sem.at[7 + k], self.recv_sem.at[7 + k], peer))
 
@@ -863,30 +896,182 @@
     )(length, q, k, v, mixed, grad, mass, cosine, sine)
 
 
+middle_plan = {
+    (1, 0): ["S0"],
+    (2, 0): ["S1"],
+    (2, 1): ["F0"],
+    (3, 0): ["S2 L0"],
+    (3, 1): ["F1"],
+    (4, 0): ["S3 L1"],
+    (4, 1): ["F2"],
+    (5, 0): ["E0 L2"],
+    (5, 1): ["F3"],
+    (6, 0): ["E1"],
+    (6, 1): ["L3"],
+    (7, 0): ["E2"],
+    (7, 1): ["E3"],
+}
+scatter_moves = {"B": "begin", "S": "to_second", "F": "to_first", "L": "to_line", "E": "finish"}
+
+
+def middle_body(refs):
+    (grad_ref, second_ref, turned_ref, wo_ref, wi_ref, slope_ref, part_ref) = refs[:7]
+    (normed_ref, inner_ref, bias_ref, out_ref) = refs[7:11]
+    hidden_ref, seed_ref = refs[11:13]
+    flat = refs[13:33]
+    send_sem, recv_sem, own_sem, seed_sem = refs[33:]
+    step = pl.program_id(0)
+    place = Place()
+    rows = out_ref.shape[0] // 4
+
+    def lines(core, part):
+        return lambda k: part_ref.at[place.lines[k][0], :, place.lines[k][1], core, part]
+
+    def put(part):
+        def write(block):
+            out_ref[part, :] = block
+
+        return write
+
+    units = []
+    for u in range(4):
+        part = slice(u * rows, (u + 1) * rows)
+        units.append(
+            Unit(
+                place,
+                put(part),
+                lines(place.c, part),
+                lines(place.other, part),
+                flat[5 * u : 5 * u + 5],
+                send_sem.at[u],
+                recv_sem.at[u],
+                own_sem.at[u],
+            )
+        )
+
+    def go(part):
+        for g in range(8):
+            if (g, part) in middle_plan:
+
+                @pl.when(step == g)
+                def _():
+                    for some in middle_plan[g, part]:
+                        for name in some.split():
+                            getattr(units[int(name[1:])], scatter_moves[name[0]])()
+
+    @pl.when(step == 0)
+    def _():
+        place.greet()
+        for unit in units:
+            unit.begin()
+        pltpu.make_async_copy(second_ref, seed_ref, seed_sem.at[0]).start()
+        normed_ref[...] = jnp.zeros_like(normed_ref)
+
+    half = grad_ref.shape[0] // 2
+
+    def some_rows(j, sums):
+        these = pl.ds(pl.multiple_of(j * half, 16), half)
+        hidden = (nt(grad_ref[these, :], wo_ref[...]) * slope_ref[these, :].astype(f32)).astype(bf16)
+        hidden_ref[these, :] = hidden
+        normed_ref[these, :] += nt(hidden, wi_ref[...])
+        return sums + jnp.sum(hidden.astype(f32), axis=0, keepdims=True)
+
+    sums = lax.fori_loop(0, 2, some_rows, jnp.zeros((1, hidden_ref.shape[1]), f32))
+    bias_ref[...] = jnp.broadcast_to(sums, bias_ref.shape)
+    go(0)
+    quarter = turned_ref.shape[0] // 2
+
+    def some_columns(j, carry):
+        these = pl.ds(pl.multiple_of(j * quarter, 16), quarter)
+        inner_ref[these, :] = nn(turned_ref[these, :], hidden_ref[...]).astype(bf16)
+        return carry
+
+    lax.fori_loop(0, 2, some_columns, 0)
+    go(1)
+
+    @pl.when(step == 7)
+    def _():
+        pltpu.make_async_copy(second_ref, seed_ref, seed_sem.at[0]).wait()
+        normed_ref[...] += seed_ref[...]
+        for unit in units:
+            unit.drain_twin()
+            unit.drain()
+
+
+def middle_back(grad, second, turned, wo, wi, slope, part):
+    total, width = grad.shape
+    hidden = wi.shape[1]
+    chunk = hidden // 8
+    shard = part.shape[0] // 32
+    once = pl.Buffered(1)
+
+    def kept(shape):
+        return pl.BlockSpec(shape, lambda i: (0,) * len(shape), pipeline_mode=once)
+
+    def chunked(rows):
+        return pl.BlockSpec((rows, chunk), lambda i: (0, i))
+
+    scratch = [pltpu.VMEM((total, chunk), bf16), pltpu.VMEM((total, width), f32)]
+    for u in range(4):
+        scratch += unit_buffers((shard // 4, width), bf16)
+    return pl.pallas_call(
+        lambda *refs: middle_body(refs),
+        grid=(8,),
+        in_specs=[
+            kept((total, width)),
+            pl.BlockSpec(memory_space=pl.ANY),
+            kept((width, total)),
+            pl.BlockSpec((chunk, width), lambda i: (i, 0)),
+            chunked(width),
+            chunked(total),
+            pl.BlockSpec(memory_space=pl.ANY),
+        ],
+        out_specs=[kept((total, width)), chunked(width), chunked(8), kept((shard, width))],
+        out_shape=[
+            jax.ShapeDtypeStruct((total, width), f32),
+            jax.ShapeDtypeStruct((width, hidden), bf16),
+            jax.ShapeDtypeStruct((8, hidden), f32),
+            jax.ShapeDtypeStruct((shard, width), f32),
+        ],
+        scratch_shapes=scratch
+        + [
+            pltpu.SemaphoreType.DMA((4, 10)),
+            pltpu.SemaphoreType.DMA((4, 10)),
+            pltpu.SemaphoreType.DMA((4, 4)),
+            pltpu.SemaphoreType.DMA((1,)),
+        ],
+        compiler_params=pltpu.CompilerParams(collective_id=7, has_side_effects=True, vmem_limit_bytes=vmem_bytes),
+        name="middle",
+    )(grad, second, turned, wo, wi, slope, part.reshape((2, 4, 2, 2, shard, width)))
+
+
 back_plan = {
-    (0, 0): ["B0 B1 B2 B3", "B4 B5 B6 B7", "B8 B9 S0"],
-    (0, 1): ["S1 S2 S3"],
-    (0, 2): ["S4 S5"],
-    (0, 3): ["B10 S6 S7 F0"],
-    (1, 1): ["S8 S9 S10 F1"],
-    (1, 2): ["F2 L0"],
-    (1, 3): ["B11 F3 L1"],
-    (2, 1): ["S11 F4 L2"],
-    (2, 2): ["F5 L3 E0"],
-    (2, 3): ["B12 F6 L4 E1"],
-    (3, 1): ["S12 F7 L5 E2"],
-    (3, 2): ["F8 F9 F10 L6", "E3"],
-    (3, 3): ["B13 Vt F11 L7", "S13 L8 L9 F12", "L10 Vs E4 E5", "L11 Vf F13 E6", "E7 L12 E8 E9", "Vl E10 E11 L13", "E12 Ve E13"],
+    (0, 0): ["B0 B1 B2 B3", "B4 B5"],
+    (0, 2): ["S0"],
+    (0, 3): ["S1"],
+    (0, 4): ["B6"],
+    (1, 1): ["S2 F0"],
+    (1, 2): ["S3 F1 L0"],
+    (1, 3): ["S4 S5 F2 L1"],
+    (1, 4): ["B7"],
+    (2, 1): ["S6 F3 L2 E0"],
+    (2, 2): ["S7 F4 F5 L3", "E1"],
+    (2, 3): ["F6 L4 L5 E2"],
+    (2, 4): ["B8"],
+    (3, 1): ["S8 F7 L6 E3"],
+    (3, 2): ["F8 L7 E4 E5"],
+    (3, 3): ["S9 Vt L8 E6", "F9 Vs E7 L9", "Vf E8 Vl E9", "Ve"],
+    (3, 4): ["B9"],
 }
 
 
 def back_body(slot, question, *refs):
     (length_ref, q_ref, k_ref, v_ref, mixed_ref, grad_ref, mass_ref, cos_ref, sin_ref) = refs[:9]
-    (wq_ref, wk_ref, wv_ref, turned_ref, vec_ref, first_ref, outer_ref, inner_ref, output_ref, proj_ref) = refs[9:19]
-    (doc_ref, query_ref, outer_out, inner_out, output_out, proj_out, dwq_out, dwk_out, dwv_out, vec_out) = refs[19:29]
-    (grads, token_grad, stage, value, sums, heard) = refs[29:35]
-    flat = refs[35 : 35 + 14 * 5]
-    send_sem, recv_sem, own_sem, vec_send, vec_recv, copy_sem = refs[35 + 14 * 5 :]
+    (wq_ref, wk_ref, wv_ref, turned_ref, vec_ref, first_ref, inner_ref, output_ref, proj_ref) = refs[9:18]
+    (doc_ref, query_ref, inner_out, output_out, proj_out, dwq_out, dwk_out, dwv_out, vec_out) = refs[18:27]
+    (grads, token_grad, stage, value, sums, heard) = refs[27:33]
+    flat = refs[33 : 33 + 10 * 5]
+    send_sem, recv_sem, own_sem, vec_send, vec_recv, copy_sem = refs[33 + 10 * 5 :]
     step = pl.program_id(0)
     place = Place()
     group = 4 * HEAD
@@ -914,16 +1099,12 @@
 
     everything = slice(None)
     units = []
-    rows = outer_out.shape[0] // 4
-    for j in range(4):
-        part = slice(j * rows, (j + 1) * rows)
-        units.append(matrix(j, outer_ref, into(outer_out, part, everything), part))
     columns = inner_out.shape[1] // 4
     for j in range(4):
         part = slice(j * columns, (j + 1) * columns)
-        units.append(matrix(4 + j, inner_ref, into(inner_out, everything, part), everything, part))
-    units.append(matrix(8, output_ref, into(output_out, everything, everything)))
-    units.append(matrix(9, proj_ref, into(proj_out, everything, everything)))
+        units.append(matrix(j, inner_ref, into(inner_out, everything, part), everything, part))
+    units.append(matrix(4, output_ref, into(output_out, everything, everything)))
+    units.append(matrix(5, proj_ref, into(proj_out, everything, everything)))
 
     def heads_out(g):
         part = slice(g * group, (g + 1) * group)
@@ -936,7 +1117,7 @@
 
     for g in range(4):
         here = stage.at[g % 2]
-        u = 10 + g
+        u = 6 + g
         units.append(
             Unit(
                 place,
@@ -949,7 +1130,6 @@
             )
         )
     vectors = VectorSum(place, value, sums, heard, vec_out, vec_send, vec_recv)
-    moves = {"B": "begin", "S": "to_second", "F": "to_first", "L": "to_line", "E": "finish"}
     tells = {"t": "twin", "s": "second", "f": "first", "l": "line", "e": "finish"}
 
     def pump(spot):
@@ -963,7 +1143,7 @@
                         if name[0] == "V":
                             getattr(vectors, tells[name[1]])()
                         else:
-                            getattr(units[int(name[1:])], moves[name[0]])()
+                            getattr(units[int(name[1:])], scatter_moves[name[0]])()
 
     seed = pltpu.make_async_copy(first_ref, token_grad, copy_sem.at[0])
 
@@ -984,7 +1164,7 @@
 
         @pl.when(step == g)
         def _():
-            units[8 + g].drain_twin()
+            units[4 + g].drain_twin()
 
     weight = nn(turned_ref[...], grads[...]).astype(bf16)
     stage[lax.rem(step, 2)] = weight.reshape(stage.shape[1:])
@@ -996,6 +1176,8 @@
             for i in range(3):
                 value[10 + i : 11 + i, g * group : (g + 1) * group] = column_sums[:, i * group : (i + 1) * group]
 
+    pump(4)
+
     @pl.when(step == 0)
     def _():
         seed.wait()
@@ -1013,8 +1195,8 @@
 
     @pl.when(step == 3)
     def _():
-        for u in range(14):
-            if u not in (10, 11):
+        for u in range(10):
+            if u not in (6, 7):
                 units[u].drain_twin()
             units[u].drain()
         vectors.sender.drain()
@@ -1036,8 +1218,8 @@
     total, width = q.shape
     group = 4 * HEAD
     shapes = [(p.shape[0] // 32, p.shape[1]) for p in parts]
-    outer, inner, output, proj = shapes
-    unit_shapes = [(outer[0] // 4, outer[1])] * 4 + [(inner[0], inner[1] // 4)] * 4 + [output, proj]
+    inner, output, proj = shapes
+    unit_shapes = [(inner[0], inner[1] // 4)] * 4 + [output, proj]
     unit_shapes += [(width // 32, 3 * group)] * 4
     scratch = []
     for shape in unit_shapes:
@@ -1049,7 +1231,7 @@
         return pl.BlockSpec(shape, lambda i: (0,) * len(shape), pipeline_mode=once)
 
     shard = (width // 32, width)
-    outs = [outer, inner, output, proj, shard, shard, shard, vectors.shape]
+    outs = [inner, output, proj, shard, shard, shard, vectors.shape]
     return pl.pallas_call(
         functools.partial(back_body, slot, question),
         grid=(width // group,),
@@ -1059,7 +1241,7 @@
         + [mass_spec(total), kept((total, 2 * HEAD)), kept((total, 2 * HEAD))]
         + [pl.BlockSpec((width, group), lambda i: (0, i), pipeline_mode=once)] * 3
         + [kept((width, total)), kept(vectors.shape)]
-        + [hbm] * 5,
+        + [hbm] * 4,
         out_specs=[hbm, hbm] + [kept(shape) for shape in outs],
         out_shape=[jax.ShapeDtypeStruct((slot, width), f32), jax.ShapeDtypeStruct((total - slot, width), f32)]
         + [jax.ShapeDtypeStruct(shape, f32) for shape in outs],
@@ -1073,9 +1255,9 @@
         ]
         + scratch
         + [
-            pltpu.SemaphoreType.DMA((14, 10)),
-            pltpu.SemaphoreType.DMA((14, 10)),
-            pltpu.SemaphoreType.DMA((14, 4)),
+            pltpu.SemaphoreType.DMA((10, 10)),
+            pltpu.SemaphoreType.DMA((10, 10)),
+            pltpu.SemaphoreType.DMA((10, 4)),
             pltpu.SemaphoreType.DMA((6,)),
             pltpu.SemaphoreType.DMA((6,)),
             pltpu.SemaphoreType.DMA((3,)),
@@ -1083,7 +1265,7 @@
         compiler_params=pltpu.CompilerParams(collective_id=4, has_side_effects=True, vmem_limit_bytes=67043328),
         name="back",
     )(
-        length, q, k, v, mixed, grad, mass, cosine, sine, *weights, tokens.T, vectors, first_grad,
+        length, q, k, v, mixed, grad, mass, cosine, sine, *weights, tokens, vectors, first_grad,
         *[p.reshape((2, 4, 2, 2) + shape) for p, shape in zip(parts, shapes)],
     )
 
@@ -1159,12 +1341,13 @@
     def forward(self, attend, shards, row_vectors, inner_bias):
         tokens = attend[1]
         output_shard, inner_shard, outer_shard, proj_shard = shards
-        outs, (w_output, w_inner) = attend_gather(*attend, [output_shard, inner_shard])
+        slot = attend[-2]
+        outs, turned, (w_output, w_inner) = attend_gather(*attend, [output_shard, inner_shard])
         mixed = outs[3]
-        (normal, inverse, low, activated, slope), (w_outer, w_proj) = inner_forward(
-            tokens, mixed, w_output, w_inner, jnp.stack(row_vectors), inner_bias[None], [outer_shard, proj_shard]
+        (normal, inverse, low, activated, slope, low_turned), (w_outer, w_proj) = inner_forward(
+            tokens, mixed, w_output, w_inner, jnp.stack(row_vectors), inner_bias[None], slot, [outer_shard, proj_shard]
         )
-        return outs, normal, inverse[:, :1], low, activated, slope, (w_output, w_inner, w_outer, w_proj)
+        return outs, normal, inverse[:, :1], (low_turned, turned), activated, slope, (w_output, w_inner, w_outer, w_proj)
 
     def rows(self, rows):
         return gather([rows], 1)[0]
@@ -1176,8 +1359,12 @@
     def row_grads(self, grads):
         return scatter([grads], 3)[0]
 
+    def middle(self, grad, second, low, w_outer, w_inner, slope, part):
+        normed_grad, inner_grad, bias, shard = middle_back(grad, second, low, w_outer, w_inner, slope, part)
+        return normed_grad, inner_grad, bias[0], shard
+
     def back(self, attend, tokens, weights, vectors, inner_bias_grad, first_grad, parts):
-        width = tokens.shape[1]
+        width = tokens.shape[0]
         slot = attend[-2]
         rows = jnp.concatenate([inner_bias_grad.reshape(4, width), jnp.stack(vectors)])
         rows = jnp.pad(rows, ((0, 16 - rows.shape[0]), (0, 0)))
@@ -1208,7 +1395,7 @@
         normal, inverse = normalize_rows(tokens.astype(f32) + dense(outs[3], weights[0]) + bias)
         low = (normal * gain + shift).astype(bf16)
         activated, slope = gelu_both(dense(low, weights[1]) + inner_bias.astype(f32))
-        return outs, normal, inverse, low, activated.astype(bf16), slope.astype(bf16), weights
+        return outs, normal, inverse, (low, tokens), activated.astype(bf16), slope.astype(bf16), weights
 
     def rows(self, rows):
         return self.one(rows)
@@ -1221,6 +1408,10 @@
 
     def spread(self, value):
         return lax.psum_scatter(value.astype(f32), AXES, scatter_dimension=0, tiled=True)
+
+    def middle(self, grad, second, low, w_outer, w_inner, slope, part):
+        hidden = (dense_back(grad, w_outer) * slope.astype(f32)).astype(bf16)
+        return second + dense_back(hidden, w_inner), weight_grad(low, hidden), row_sum(hidden), self.spread(part)
 
     def back(self, attend, tokens, weights, vectors, inner_bias_grad, first_grad, parts):
         slot = attend[-2]
@@ -1287,7 +1478,7 @@
     w_query, w_key, w_value = matrices
     b_output, g_attn, s_attn, b_outer, g_final, s_final = [vectors[i].astype(f32) for i in range(3, 9)]
 
-    outs, first_normal, first_inverse, normed_low, activated, slope, matrices = link.forward(
+    outs, first_normal, first_inverse, (normed_low, tokens_kept), activated, slope, matrices = link.forward(
         (doc_lengths, tokens, w_query, w_key, w_value, vectors[0:8], cosine, sine, slot, question),
         [output_weight, inner_weight, outer_weight, proj_weight],
         [b_output, g_attn, s_attn],
@@ -1360,10 +1551,9 @@
     outer_grad = second_grad.astype(bf16)
     outer_weight_grad = weight_grad(activated, outer_grad)
     outer_bias_grad = row_sum(outer_grad)
-    hidden_grad = (dense_back(outer_grad, w_outer) * slope.astype(f32)).astype(bf16)
-    inner_weight_grad = weight_grad(normed_low, hidden_grad)
-    inner_bias_grad = row_sum(hidden_grad)
-    normed_grad = second_grad + dense_back(hidden_grad, w_inner)
+    normed_grad, inner_weight_grad, inner_bias_grad, outer_shard = link.middle(
+        outer_grad, second_grad, normed_low, w_outer, w_inner, slope, outer_weight_grad
+    )
     attn_gain_grad = row_sum(normed_grad * first_normal)
     attn_shift_grad = row_sum(normed_grad)
     first_grad = norm_back(normed_grad * g_attn, first_normal, first_inverse)
@@ -1376,14 +1566,14 @@
     )
     docs_grad, asked_grad, shards, small, inner_bias_shard = link.back(
         attend,
-        tokens,
+        tokens_kept,
         (w_query, w_key, w_value),
         [outer_bias_grad, final_gain_grad, final_shift_grad, attn_gain_grad, attn_shift_grad, output_bias_grad],
         inner_bias_grad,
         first_grad,
-        [outer_weight_grad, inner_weight_grad, output_weight_grad, proj_weight_grad],
+        [inner_weight_grad, output_weight_grad, proj_weight_grad],
     )
-    outer_shard, inner_shard, output_shard, proj_shard, query_shard, key_shard, value_shard = shards
+    inner_shard, output_shard, proj_shard, query_shard, key_shard, value_shard = shards
     b_outer_shard, gain_shard, shift_shard, attn_gain_shard, attn_shift_shard, b_output_shard, *b_heads = small
     return (
         query_loss,

time: 542 us -> 516 us (0.952); the launches traced: 539 us -> 506 us
  matrix products: 105 us -> 52.6 us
  Pallas kernels: 366 us -> 392 us
  local copies, waits for them, and re-layouts: 40.2 us -> 31.8 us
    pallas_call x1 -> x2, Pallas kernels: 61.7 us -> 123 us  [the longest x1 63.8 us: middle_back(): pl.pallas_call(lambda *refs: middle_body(refs), grid=(8,), in_specs=[kept...]
    dot_general x4 -> x2, matrix products: 42.8 us -> 8 us  [dense_back(): return jnp.einsum('le,de->ld', gradient, matrix, preferred_element_type=f32)]
    pallas_call x1, Pallas kernels: 139 us -> 117 us  [back_close(): pl.pallas_call(functools.partial(back_body, slot, question), grid=(width...]
    dot_general x4 -> x3, matrix products: 38.2 us -> 20.5 us  [weight_grad(): jnp.einsum('ld,le->de', operand, gradient, preferred_element_type=f32)]
    pallas_call x1, Pallas kernels: 75.7 us -> 63.5 us  [attend_gather(): pl.pallas_call(functools.partial(attend_gather_body, slot, question), gri...]
    reduce_sum x2 -> x3, other arithmetic: 8.61 us -> 12.5 us  [row_sum(): return jnp.sum(values.astype(f32), axis=0)]
    unnamed x63 -> x58, local copies, waits for them, and re-layouts: 16.7 us -> 12.8 us
where the time goes in v3:
time: 516 us; the launch traced here: 506 us
  Pallas kernels  392 us (76%)
  matrix products  52.6 us (10%)
  local copies, waits for them, and re-layouts  31.8 us (6%)
  other arithmetic  27.9 us (5%)
    pallas_call x1, Pallas kernels, back_close(): pl.pallas_call(functools.partial(back_body, slot, question), grid=(width...  117 us
    pallas_call x3, Pallas kernels, gather(): pl.pallas_call(functools.partial(gather_body, count), in_specs=[pl.BlockS...  72.6 us
    pallas_call x1, Pallas kernels, middle_back(): pl.pallas_call(lambda *refs: middle_body(refs), grid=(8,), in_specs=[kept...  63.8 us
    pallas_call x1, Pallas kernels, attend_gather(): pl.pallas_call(functools.partial(attend_gather_body, slot, question), gri...  63.5 us
    pallas_call x1, Pallas kernels, inner_forward(): pl.pallas_call(lambda *refs: inner_body(slot, refs), grid=(9,), in_specs=...  59 us
    dot_general x3, matrix products, weight_grad(): jnp.einsum('ld,le->de', operand, gradient, preferred_element_type=f32)  20.5 us
    dot_general x2, matrix products, dense(): return jnp.einsum('ld,de->le', operand, matrix, preferred_element_type=f32)  17.4 us
    pallas_call x1, Pallas kernels, scatter(): pl.pallas_call(functools.partial(scatter_body, count), in_specs=[pl.Block...  15.3 us

profile of v3, /device:TPU:0, one launch (start us, length us, event | category | flops | bytes accessed | tf_op | source)
XLA Modules:
  0.0 506.2 jit_solution(5585550287213197095)
XLA Ops:
  2.0 1.5 stack.65
  4.7 3.2 pad_maximum_fusion.refs_1_.refs_0_
  7.9 41.7 %gather.3 = (bf16[2,4,2,2,32,1024]{5,4,3,2,1,0:T(8,128)(2,1)}, bf16[2,4,2,2,32,1024]{5,4,3,2,1,0:T(8,128)(2,1)}, bf16[2,4,2,2,32,1024]{5,4,3,2,1,0:T(8,128)(2,1)}, bf16[2,4,2,2,16,128]{5,4,3,2,1,0:T(8,128)(2,1)}) custom-call(bf16[32,1024]{1,0:T(8,128)(2,1)} %refs_0_.3, bf16[32,1024]{1,0:T(8,128)(2,1)} %refs_1_.1, bf16[32,1024]{1,0:T(8,128)(2,1)} %refs_2_.1, ...), custom_call_target="tpu_custom_call" | custom-call | tf_op jit(solution)/shard_map/gather/pallas_call | solution.py:373
  50.7 1.5 slice_bitcast_fusion.1.refs_5_
  55.2 63.5 %attend_forward.1 = (bf16[1088,1024]{1,0:T(8,128)(2,1)}, bf16[1088,1024]{1,0:T(8,128)(2,1)}, bf16[1088,1024]{1,0:T(8,128)(2,1)}, bf16[1088,1024]{1,0:T(8,128)(2,...) custom-call(s32[1]{0:T(128)S(6)} %copy.88.refs_0_, ...), custom_call_target="tpu_custom_call" | custom-call | tf_op jit(solution)/shard_map/attend_forward/pallas_call | solution.py:452
  118.6 59.0 %inner_forward.1 = (f32[1088,1024]{1,0:T(8,128)}, f32[1088,128]{1,0:T(8,128)}, bf16[1088,1024]{1,0:T(8,128)(2,1)}, bf16[1088,4096]{1,0:T(8,128)(2,1)}, bf16[1088...) custom-call(bf16[1088,1024]{1,0:T(8,128)(2,1)} %pad_maximum_fusion.r, ...), custom_call_target="tpu_custom_call" | custom-call | tf_op jit(solution)/shard_map/inner_forward/pallas_call | solution.py:564
  177.7 1.3 slice_reduce_fusion
  178.9 16.5 %fusion.25 = (f32[1088]{0:T(1024)S(1)}, f32[1088,1024]{1,0:T(8,128)S(1)}) fusion(f32[1024]{0:T(1024)S(1)} %reshape.310, bf16[1088,4096]{1,0:T(8,128)(2,1)} %get-tuple-element.132, bf16[4096,1024]{1,0:T(8,128)(2,1)} %bitcast.147, f32[1024]{0:T(1024)S(1)} %reshape.309, f32[1088,1024]{1,0:T(8,128)} %get-tuple-element.131, f32[1024]{0:T(1024)S(1)} %reshape.308), kind=kOutput, calls=%fused_computation.101 | convolution fusion | flops 9132375040 | bytes 26231040 | tf_op jit(solution)/shard_map/ld,de->le/dot_general | solution.py:1286
  200.7 16.7 %gather.4 = bf16[2,4,2,2,64,128]{5,4,3,2,1,0:T(8,128)(2,1)S(1)} custom-call(bf16[64,128]{1,0:T(8,128)(2,1)} %slice.131.refs_0_), custom_call_target="tpu_custom_call" | custom-call | tf_op jit(solution)/shard_map/gather/pallas_call | solution.py:373
  217.4 5.0 while.24
  223.3 14.2 %gather.5 = f32[2,4,2,2,8,128]{5,4,3,2,1,0:T(8,128)} custom-call(f32[8,128]{1,0:T(8,128)} %broadcast_in_dim.100.refs_0_), custom_call_target="tpu_custom_call" | custom-call | tf_op jit(solution)/shard_map/gather/pallas_call | solution.py:373
  237.5 1.0 slice_reduce_fusion.2
  239.4 9.4 %while.25 = (s32[]{:T(128)}, f32[1024,128]{1,0:T(8,128)S(1)}, f32[2,1024,128]{2,1,0:T(8,128)}, bf16[2,1024,128]{2,1,0:T(8,128)(2,1)S(1)}, bf16[1024,128]{1,0:T(8...) while((s32[]{:T(128)}, f32[1024,128]{1,0:T(8,128)S(1)}, ...), condition=%wide.region_12.13_spmd.clone, body=%wide.region_11.12_spmd.clone.sunk | while | flops 810813440 | bytes 17328324 | solution.py:1536
  240.1 1.1 multiply_convert_fusion.3
  243.1 1.0 copy-done.9
  244.8 1.1 multiply_convert_fusion.3
  247.8 1.0 copy-done.9
  248.8 15.3 %scatter.1 = f32[64,128]{1,0:T(8,128)} custom-call(f32[2,4,2,2,64,128]{5,4,3,2,1,0:T(8,128)} %bitcast.155), custom_call_target="tpu_custom_call" | custom-call | tf_op jit(solution)/shard_map/scatter/pallas_call | solution.py:699
  264.2 1.2 multiply_reduce_fusion.7
  265.3 1.8 subtract_convert_fusion
  267.2 3.2 convolution_convert_fusion.3
  270.4 1.5 slice_bitcast_fusion
  271.9 1.7 multiply_reduce_fusion.1
  273.6 2.9 convert_reduce_fusion.1
  276.5 13.1 %convolution_convert_fusion = bf16[4096,1024]{1,0:T(8,128)(2,1)} fusion(bf16[1088,4096]{1,0:T(8,128)(2,1)S(1)} %bitcast.191, bf16[1088,1024]{1,0:T(8,128)(2,1)S(1)} %get-tuple-element.241.refs_0_), kind=kOutput, calls=%fused_computation.24 | convolution fusion | flops 9130999808 | bytes 19529728 | tf_op jit(solution)/shard_map/ld,le->de/dot_general | solution.py:1294
  289.7 63.8 %middle.1 = (f32[1088,1024]{1,0:T(8,128)}, bf16[1024,4096]{1,0:T(8,128)(2,1)}, f32[8,4096]{1,0:T(8,128)}, f32[128,1024]{1,0:T(8,128)}) custom-call(bf16[1088,1024]{1,0:T(8,128)(2,1)} %copy-done.6, f32[1088,1024]{1,0:T(8,128)} %get-tuple-element.242.refs_1_, bf16[1024,1088]{1,0:T(8,128)(2,1)} %get-tuple-element.142.refs_2_, bf16[4096,1024]{1,0:T(8,128)(2,1)} %bitcast.148, ...), custom_call_target="tpu_custom_call" | custom-call | tf_op jit(solution)/shard_map/middle/pallas_call | solution.py:1017
  354.4 5.1 %multiply_reduce_fusion = (f32[1024]{0:T(1024)S(1)}, f32[1088]{0:T(1024)S(1)}, f32[1088]{0:T(1024)S(1)}, f32[1024]{0:T(1024)S(1)}) fusion(f32[1088,1024]{1,0:T(8,128)} %get-tuple-element.144, f32[1088,1024]{1,0:T(8,128)} %get-tuple-element.131, f32[1024]{0:T(1024)S(1)} %reshape.308), kind=kLoop, calls=%fused_computation.28 | loop fusion | flops 7794560 | bytes 8933888 | tf_op jit(solution)/shard_map/reduce_sum | solution.py:1298
  359.6 4.5 convert_reduce_fusion
  364.8 6.3 %convolution_convert_fusion.1.refs_5_ = bf16[1088,1024]{1,0:T(8,128)(2,1)} fusion(bf16[1024,1024]{1,0:T(8,128)(2,1)S(1)} %bitcast.152, f32[1088,1024]{1,0:T(8,128)} %get-tuple-element.239.refs_14_), kind=kOutput, calls=%fused_computation.40 | convolution fusion | flops 2283929600 | bytes 8781824 | tf_op jit(solution)/shard_map/le,de->ld/dot_general | solution.py:1290
  371.1 4.2 convolution_convert_fusion.2
  375.3 117.4 %back.1 = (f32[1024,1024]{1,0:T(8,128)}, f32[64,1024]{1,0:T(8,128)}, f32[32,4096]{1,0:T(8,128)}, f32[32,1024]{1,0:T(8,128)}, f32[32,128]{1,0:T(8,128)}, /*index=...) custom-call(s32[1]{0:T(128)S(6)} %copy.88.refs_0_, ...), custom_call_target="tpu_custom_call" | custom-call | tf_op jit(solution)/shard_map/back/pallas_call | solution.py:1235
  495.6 4.9 copy.89
  (138 shorter events, 32.9 us)
Async XLA Ops:
  195.5 2.2 copy-start
  196.1 2.9 copy-start.13
  197.6 1.4 copy-start.1
  241.2 1.2 copy-start.8
  243.1 1.0 copy-start.9
  245.9 1.2 copy-start.8
  247.8 1.0 copy-start.9
  264.2 6.2 %copy-start.2 = (bf16[1088,1024]{1,0:T(8,128)(2,1)S(1)}, bf16[1088,1024]{1,0:T(8,128)(2,1)}, u32[]{:S(2)}) copy-start(bf16[1088,1024]{1,0:T(8,128)(2,1)} %copy-done.1) | copy-start | bytes 6684676
  264.2 7.7 %slice-start = ((s8[4456448]{0:T(1024)(128)(4,1)}), s8[4194304]{0:T(1024)(128)(4,1)S(1)}, s32[]{:S(2)}) async-start(s8[4456448]{0:T(1024)(128)(4,1)} %bitcast.135), calls=%async_computation | async-start | bytes 8388608
  267.1 4.7 slice-start.1
  267.1 4.7 copy-start.14
  271.9 4.6 slice-start.2
  271.9 4.6 slice-start.3
  273.6 2.9 slice-start.4
  276.5 13.2 %copy-start.6 = (bf16[1088,1024]{1,0:T(8,128)(2,1)}, bf16[1088,1024]{1,0:T(8,128)(2,1)S(1)}, u32[]{:S(2)}) copy-start(bf16[1088,1024]{1,0:T(8,128)(2,1)S(1)} %get-tuple-element.241.refs_0_) | copy-start | bytes 6684676
  354.4 5.2 %copy-start.4 = (f32[1088,1024]{1,0:T(8,128)S(1)}, f32[1088,1024]{1,0:T(8,128)}, u32[]{:S(2)}) copy-start(f32[1088,1024]{1,0:T(8,128)} %get-tuple-element.144) | copy-start | bytes 13369348
  359.6 5.2 %copy-start.7 = (bf16[2,4,2,2,32,1024]{5,4,3,2,1,0:T(8,128)(2,1)S(1)}, bf16[2,4,2,2,32,1024]{5,4,3,2,1,0:T(8,128)(2,1)}, u32[]{:S(2)}) copy-start(bf16[2,4,2,2,32,1024]{5,4,3,2,1,0:T(8,128)(2,1)} %get-tuple-element.129) | copy-start | bytes 6291460
  364.8 6.3 %copy-start.3 = (f32[1088,1024]{1,0:T(8,128)S(1)}, f32[1088,1024]{1,0:T(8,128)}, u32[]{:S(2)}) copy-start(f32[1088,1024]{1,0:T(8,128)} %get-tuple-element.239.refs_14_) | copy-start | bytes 13369348
  364.8 6.3 %copy-start.5 = (bf16[1088,1024]{1,0:T(8,128)(2,1)S(1)}, bf16[1088,1024]{1,0:T(8,128)(2,1)}, u32[]{:S(2)}) copy-start(bf16[1088,1024]{1,0:T(8,128)(2,1)} %get-tuple-element.128.refs_1_.refs_4_) | copy-start | bytes 6684676
  492.7 7.8 %copy-start.12 = (f32[64,1024]{1,0:T(8,128)S(1)}, f32[64,1024]{1,0:T(8,128)}, u32[]{:S(2)}) copy-start(f32[64,1024]{1,0:T(8,128)} %get-tuple-element.150) | copy-start | bytes 786436
  495.5 5.7 %copy-start.18 = (f32[32,1024]{1,0:T(8,128)S(1)}, f32[32,1024]{1,0:T(8,128)}, u32[]{:S(2)}) copy-start(f32[32,1024]{1,0:T(8,128)} %get-tuple-element.443) | copy-start | bytes 393220
  495.5 6.3 %copy-start.17 = (f32[32,1024]{1,0:T(8,128)S(1)}, f32[32,1024]{1,0:T(8,128)}, u32[]{:S(2)}) copy-start(f32[32,1024]{1,0:T(8,128)} %get-tuple-element.444) | copy-start | bytes 393220
  495.5 7.0 %copy-start.16 = (f32[32,1024]{1,0:T(8,128)S(1)}, f32[32,1024]{1,0:T(8,128)}, u32[]{:S(2)}) copy-start(f32[32,1024]{1,0:T(8,128)} %get-tuple-element.445) | copy-start | bytes 393220
  495.5 7.6 %copy-start.15 = (f32[32,1024]{1,0:T(8,128)S(1)}, f32[32,1024]{1,0:T(8,128)}, u32[]{:S(2)}) copy-start(f32[32,1024]{1,0:T(8,128)} %get-tuple-element.446) | copy-start | bytes 393220
  495.5 8.3 %copy-start.11 = (f32[32,4096]{1,0:T(8,128)S(1)}, f32[32,4096]{1,0:T(8,128)}, u32[]{:S(2)}) copy-start(f32[32,4096]{1,0:T(8,128)} %get-tuple-element.453) | copy-start | bytes 1572868
  495.5 9.1 %copy-start.10 = (f32[128,1024]{1,0:T(8,128)S(1)}, f32[128,1024]{1,0:T(8,128)}, u32[]{:S(2)}) copy-start(f32[128,1024]{1,0:T(8,128)} %get-tuple-element.455) | copy-start | bytes 1572868
  495.6 9.8 %copy-start.19 = (f32[32,128]{1,0:T(8,128)S(1)}, f32[32,128]{1,0:T(8,128)}, u32[]{:S(2)}) copy-start(f32[32,128]{1,0:T(8,128)} %get-tuple-element.459) | copy-start | bytes 49156

commit v4 on v3

--- a/solution.py
+++ b/solution.py
@@ -22,6 +22,7 @@
 masked_value = -1e30
 score_scale = 0.125 * math.log2(math.e)
 vmem_bytes = 62 * 1024 * 1024
+small_room = 6 * 1024 * 1024
 
 
 def nt(a, b):
@@ -368,7 +369,7 @@
     run.out.drain()
 
 
-def gather(shards, collective_id):
+def gather(shards, collective_id, room=vmem_bytes):
     count = len(shards)
     wholes = pl.pallas_call(
         functools.partial(gather_body, count),
@@ -377,11 +378,55 @@
         out_shape=[spread_shape(a) for a in shards],
         scratch_shapes=gather_sems(count),
         compiler_params=pltpu.CompilerParams(
-            collective_id=collective_id, has_side_effects=True, vmem_limit_bytes=vmem_bytes
+            collective_id=collective_id, has_side_effects=True, vmem_limit_bytes=room
         ),
         name="gather",
     )(*shards)
     return [joined_shards(w) for w in wholes]
+
+
+def exchange_body(block_ref, whole, send_sem, recv_sem, own_sem):
+    place = Place()
+    y, z, x, c = place.y, place.z, place.x, place.c
+    near = []
+    for flip in range(1, 8):
+        there = ((1 - y) if flip & 4 else y, (1 - x) if flip & 2 else x, (1 - c) if flip & 1 else c)
+        near.append((there, (there[0], z * 4 + there[1] * 2 + there[2])))
+    peers = [device for _, device in near] + place.along
+    barrier = pltpu.get_barrier_semaphore()
+    for peer in peers:
+        pl.semaphore_signal(barrier, inc=1, device_id=peer, device_id_type=MESH)
+    pl.semaphore_wait(barrier, len(peers))
+    out = Sender()
+    mine = whole.at[y, z, x, c]
+    for i, (_, device) in enumerate(near):
+        out.go(block_ref, mine, send_sem.at[i], recv_sem.at[i], device)
+    own = pltpu.make_async_copy(block_ref, mine, own_sem.at[0])
+    own.start()
+    own.wait()
+    for i, (there, _) in enumerate(near):
+        arrived(whole.at[there[0], z, there[1], there[2]], recv_sem.at[i])
+    for k, device in enumerate(place.along):
+        out.go(whole.at[:, z], whole.at[:, z], send_sem.at[7 + k], recv_sem.at[7 + k], device)
+    for k in range(3):
+        arrived(whole.at[:, place.ahead[2 - k]], recv_sem.at[7 + k])
+    out.drain()
+
+
+def exchange(block, collective_id):
+    return pl.pallas_call(
+        exchange_body,
+        in_specs=[pl.BlockSpec(memory_space=pltpu.VMEM)],
+        out_specs=pl.BlockSpec(memory_space=pltpu.VMEM),
+        out_shape=spread_shape(block),
+        scratch_shapes=[
+            pltpu.SemaphoreType.DMA((10,)),
+            pltpu.SemaphoreType.DMA((10,)),
+            pltpu.SemaphoreType.DMA((1,)),
+        ],
+        compiler_params=pltpu.CompilerParams(collective_id=collective_id, has_side_effects=True, vmem_limit_bytes=small_room),
+        name="exchange",
+    )(block)
 
 
 attend_plan = {
@@ -708,7 +753,7 @@
             pltpu.SemaphoreType.DMA((count, 4)),
         ],
         compiler_params=pltpu.CompilerParams(
-            collective_id=collective_id, has_side_effects=True, vmem_limit_bytes=vmem_bytes
+            collective_id=collective_id, has_side_effects=True, vmem_limit_bytes=small_room
         ),
         name="scatter",
     )(*[p.reshape((2, 4, 2, 2) + shape) for p, shape in zip(parts, shapes)])
@@ -1350,11 +1395,11 @@
         return outs, normal, inverse[:, :1], (low_turned, turned), activated, slope, (w_output, w_inner, w_outer, w_proj)
 
     def rows(self, rows):
-        return gather([rows], 1)[0]
+        return gather([rows], 1, small_room)[0]
 
     def totals(self, totals):
         block = jnp.broadcast_to(padded(totals[None], 128), (8, 128))
-        return gather([block], 2)[0].reshape(32, 8, 128)[:, 0, : totals.shape[0]]
+        return exchange(block, 2).reshape(32, 8, 128)[:, 0, : totals.shape[0]]
 
     def row_grads(self, grads):
         return scatter([grads], 3)[0]

time: 516 us -> 503 us (0.975)
  Pallas kernels: 392 us -> 386 us
    pallas_call x3 -> x2, Pallas kernels: 72.6 us -> 57.7 us  [gather(): pl.pallas_call(functools.partial(gather_body, count), in_specs=[pl.BlockS...]
    pallas_call x0 -> x1, Pallas kernels: none -> 11 us  [exchange(): pl.pallas_call(exchange_body, in_specs=[pl.BlockSpec(memory_space=pltpu.V...]
    unnamed x58 -> x56, local copies, waits for them, and re-layouts: 12.8 us -> 12.1 us
where the time goes in v4:
time: 503 us; the launch traced here: 494 us
  Pallas kernels  386 us (77%)
  matrix products  53 us (11%)
  local copies, waits for them, and re-layouts  27.2 us (5%)
  other arithmetic  24.8 us (5%)
    pallas_call x1, Pallas kernels, back_close(): pl.pallas_call(functools.partial(back_body, slot, question), grid=(width...  117 us
    pallas_call x1, Pallas kernels, middle_back(): pl.pallas_call(lambda *refs: middle_body(refs), grid=(8,), in_specs=[kept...  63.6 us
    pallas_call x1, Pallas kernels, attend_gather(): pl.pallas_call(functools.partial(attend_gather_body, slot, question), gri...  63.5 us
    pallas_call x1, Pallas kernels, inner_forward(): pl.pallas_call(lambda *refs: inner_body(slot, refs), grid=(9,), in_specs=...  59 us
    pallas_call x2, Pallas kernels, gather(): pl.pallas_call(functools.partial(gather_body, count), in_specs=[pl.BlockS...  57.7 us
    dot_general x3, matrix products, weight_grad(): jnp.einsum('ld,le->de', operand, gradient, preferred_element_type=f32)  20.9 us
    dot_general x2, matrix products, dense(): return jnp.einsum('ld,de->le', operand, matrix, preferred_element_type=f32)  17.4 us
    pallas_call x1, Pallas kernels, scatter(): pl.pallas_call(functools.partial(scatter_body, count), in_specs=[pl.Block...  14.4 us

profile of v4, /device:TPU:0, one launch (start us, length us, event | category | flops | bytes accessed | tf_op | source)
XLA Modules:
  0.0 494.0 jit_solution(1102345802572178063)
XLA Ops:
  2.0 1.5 stack.65
  4.7 3.2 pad_maximum_fusion.refs_1_.refs_0_
  7.9 41.7 %gather.2 = (bf16[2,4,2,2,32,1024]{5,4,3,2,1,0:T(8,128)(2,1)}, bf16[2,4,2,2,32,1024]{5,4,3,2,1,0:T(8,128)(2,1)}, bf16[2,4,2,2,32,1024]{5,4,3,2,1,0:T(8,128)(2,1)}, bf16[2,4,2,2,16,128]{5,4,3,2,1,0:T(8,128)(2,1)}) custom-call(bf16[32,1024]{1,0:T(8,128)(2,1)} %refs_0_.3, bf16[32,1024]{1,0:T(8,128)(2,1)} %refs_1_.1, bf16[32,1024]{1,0:T(8,128)(2,1)} %refs_2_.1, ...), custom_call_target="tpu_custom_call" | custom-call | tf_op jit(solution)/shard_map/gather/pallas_call | solution.py:374
  49.6 0.9 slice.134
  50.7 1.5 slice_bitcast_fusion.1.refs_5_
  52.2 0.9 slice.122
  55.2 63.5 %attend_forward.1 = (bf16[1088,1024]{1,0:T(8,128)(2,1)}, bf16[1088,1024]{1,0:T(8,128)(2,1)}, bf16[1088,1024]{1,0:T(8,128)(2,1)}, bf16[1088,1024]{1,0:T(8,128)(2,...) custom-call(s32[1]{0:T(128)S(6)} %copy.88.refs_0_, ...), custom_call_target="tpu_custom_call" | custom-call | tf_op jit(solution)/shard_map/attend_forward/pallas_call | solution.py:497
  118.6 59.0 %inner_forward.1 = (f32[1088,1024]{1,0:T(8,128)}, f32[1088,128]{1,0:T(8,128)}, bf16[1088,1024]{1,0:T(8,128)(2,1)}, bf16[1088,4096]{1,0:T(8,128)(2,1)}, bf16[1088...) custom-call(bf16[1088,1024]{1,0:T(8,128)(2,1)} %pad_maximum_fusion.r, ...), custom_call_target="tpu_custom_call" | custom-call | tf_op jit(solution)/shard_map/inner_forward/pallas_call | solution.py:609
  177.7 1.3 slice_reduce_fusion
  179.0 16.5 %fusion.25 = (f32[1088]{0:T(1024)S(1)}, f32[1088,1024]{1,0:T(8,128)S(1)}) fusion(f32[1024]{0:T(1024)S(1)} %reshape.314, bf16[1088,4096]{1,0:T(8,128)(2,1)} %get-tuple-element.132, bf16[4096,1024]{1,0:T(8,128)(2,1)} %bitcast.148, f32[1024]{0:T(1024)S(1)} %reshape.313, f32[1088,1024]{1,0:T(8,128)} %get-tuple-element.131, f32[1024]{0:T(1024)S(1)} %reshape.312), kind=kOutput, calls=%fused_computation.101 | convolution fusion | flops 9132375040 | bytes 26231040 | tf_op jit(solution)/shard_map/ld,de->le/dot_general | solution.py:1331
  199.5 16.0 %gather.3 = bf16[2,4,2,2,64,128]{5,4,3,2,1,0:T(8,128)(2,1)S(1)} custom-call(bf16[64,128]{1,0:T(8,128)(2,1)S(1)} %slice.131.refs_0_), custom_call_target="tpu_custom_call" | custom-call | tf_op jit(solution)/shard_map/gather/pallas_call | solution.py:374
  215.5 5.2 %while.24 = (s32[]{:T(128)}, f32[2,1024]{1,0:T(2,128)S(1)}, bf16[2,1024,128]{2,1,0:T(8,128)(2,1)S(1)}, bf16[1024,128]{1,0:T(8,128)(2,1)S(1)}, s32[]{:T(128)}, /*index=5*/s32[]{:T(128)}, s32[]{:T(128)}) while((s32[]{:T(128)}, f32[2,1024]{1,0:T(2,128)S(1)}, bf16[2,1024,128]{2,1,0:T(8,128)(2,1)S(1)}, bf16[1024,128]{1,0:T(8,128)(2,1)S(1)}, ...), condition=%wide.region_6.7_spmd.clone, body=%wide.region_3.6_spmd.clone.sunk | while | flops 275776512 | bytes 8948833 | solution.py:1560
  217.4 0.9 exponential_reduce_fusion.3
  219.8 0.9 exponential_reduce_fusion.3
  221.0 11.0 %exchange.1 = f32[2,4,2,2,8,128]{5,4,3,2,1,0:T(8,128)S(1)} custom-call(f32[8,128]{1,0:T(8,128)S(1)} %broadcast_in_dim.100.block_ref), custom_call_target="tpu_custom_call" | custom-call | tf_op jit(solution)/shard_map/exchange/pallas_call | solution.py:417
  233.0 6.7 %while.25 = (s32[]{:T(128)}, f32[1024,128]{1,0:T(8,128)S(1)}, f32[2,1024,128]{2,1,0:T(8,128)S(1)}, bf16[2,1024,128]{2,1,0:T(8,128)(2,1)S(1)}, bf16[1024,128]{1,0...) while((s32[]{:T(128)}, f32[1024,128]{1,0:T(8,128)S(1)}, ...), condition=%wide.region_12.13_spmd.clone, body=%wide.region_11.12_spmd.clone.sunk | while | flops 810813440 | bytes 8939659 | solution.py:1581
  233.7 1.1 multiply_convert_fusion.3
  237.1 1.1 multiply_convert_fusion.3
  239.7 14.4 %scatter.1 = f32[64,128]{1,0:T(8,128)S(1)} custom-call(f32[2,4,2,2,64,128]{5,4,3,2,1,0:T(8,128)S(1)} %bitcast.156), custom_call_target="tpu_custom_call" | custom-call | tf_op jit(solution)/shard_map/scatter/pallas_call | solution.py:744
  254.9 3.6 convolution_convert_fusion.3
  258.5 1.5 slice_bitcast_fusion
  260.0 1.7 multiply_reduce_fusion.1
  261.8 2.9 convert_reduce_fusion.1
  264.7 13.1 %convolution_convert_fusion = bf16[4096,1024]{1,0:T(8,128)(2,1)} fusion(bf16[1088,4096]{1,0:T(8,128)(2,1)S(1)} %bitcast.191, bf16[1088,1024]{1,0:T(8,128)(2,1)S(1)} %get-tuple-element.241.refs_0_), kind=kOutput, calls=%fused_computation.24 | convolution fusion | flops 9130999808 | bytes 19529728 | tf_op jit(solution)/shard_map/ld,le->de/dot_general | solution.py:1339
  277.8 63.6 %middle.1 = (f32[1088,1024]{1,0:T(8,128)}, bf16[1024,4096]{1,0:T(8,128)(2,1)}, f32[8,4096]{1,0:T(8,128)}, f32[128,1024]{1,0:T(8,128)}) custom-call(bf16[1088,1024]{1,0:T(8,128)(2,1)} %copy-done.6, f32[1088,1024]{1,0:T(8,128)} %get-tuple-element.242.refs_1_, bf16[1024,1088]{1,0:T(8,128)(2,1)} %get-tuple-element.142.refs_2_, bf16[4096,1024]{1,0:T(8,128)(2,1)} %bitcast.149, ...), custom_call_target="tpu_custom_call" | custom-call | tf_op jit(solution)/shard_map/middle/pallas_call | solution.py:1062
  341.4 0.9 slice_reduce_fusion.1
  342.4 5.1 %multiply_reduce_fusion = (f32[1024]{0:T(1024)S(1)}, f32[1088]{0:T(1024)S(1)}, f32[1088]{0:T(1024)S(1)}, f32[1024]{0:T(1024)S(1)}) fusion(f32[1088,1024]{1,0:T(8,128)} %get-tuple-element.144, f32[1088,1024]{1,0:T(8,128)} %get-tuple-element.131, f32[1024]{0:T(1024)S(1)} %reshape.312), kind=kLoop, calls=%fused_computation.28 | loop fusion | flops 7794560 | bytes 8933888 | tf_op jit(solution)/shard_map/reduce_sum | solution.py:1343
  347.6 4.5 convert_reduce_fusion
  352.8 6.3 %convolution_convert_fusion.1.refs_5_ = bf16[1088,1024]{1,0:T(8,128)(2,1)} fusion(bf16[1024,1024]{1,0:T(8,128)(2,1)S(1)} %bitcast.153, f32[1088,1024]{1,0:T(8,128)} %get-tuple-element.239.refs_14_), kind=kOutput, calls=%fused_computation.40 | convolution fusion | flops 2283929600 | bytes 8781824 | tf_op jit(solution)/shard_map/le,de->ld/dot_general | solution.py:1335
  359.1 4.2 convolution_convert_fusion.2
  363.3 117.0 %back.1 = (f32[1024,1024]{1,0:T(8,128)}, f32[64,1024]{1,0:T(8,128)}, f32[32,4096]{1,0:T(8,128)}, f32[32,1024]{1,0:T(8,128)}, f32[32,128]{1,0:T(8,128)}, /*index=...) custom-call(s32[1]{0:T(128)S(6)} %copy.88.refs_0_, ...), custom_call_target="tpu_custom_call" | custom-call | tf_op jit(solution)/shard_map/back/pallas_call | solution.py:1280
  483.2 4.9 copy.89
  (128 shorter events, 26.5 us)
Async XLA Ops:
  195.5 2.2 copy-start
  196.2 2.2 copy-start.11
  197.7 17.8 %copy-start.1 = (bf16[1088,1024]{1,0:T(8,128)(2,1)}, bf16[1088,1024]{1,0:T(8,128)(2,1)S(1)}, u32[]{:S(2)}) copy-start(bf16[1088,1024]{1,0:T(8,128)(2,1)S(1)} %add_convert_fusion) | copy-start | bytes 6684676
  239.7 18.8 %copy-start.2 = (bf16[1088,1024]{1,0:T(8,128)(2,1)S(1)}, bf16[1088,1024]{1,0:T(8,128)(2,1)}, u32[]{:S(2)}) copy-start(bf16[1088,1024]{1,0:T(8,128)(2,1)} %copy-done.1) | copy-start | bytes 6684676
  254.2 5.8 %slice-start = ((s8[4456448]{0:T(1024)(128)(4,1)}), s8[4194304]{0:T(1024)(128)(4,1)S(1)}, s32[]{:S(2)}) async-start(s8[4456448]{0:T(1024)(128)(4,1)} %bitcast.136), calls=%async_computation | async-start | bytes 8388608
  254.9 5.1 %slice-start.1 = ((s8[4456448]{0:T(1024)(128)(4,1)}), s8[262144]{0:T(1024)(128)(4,1)S(1)}, s32[]{:S(2)}) async-start(s8[4456448]{0:T(1024)(128)(4,1)} %bitcast.136), calls=%async_computation.1 | async-start | bytes 524288
  260.0 4.6 slice-start.2
  260.0 4.6 slice-start.3
  261.8 2.9 slice-start.4
  264.6 13.2 %copy-start.6 = (bf16[1088,1024]{1,0:T(8,128)(2,1)}, bf16[1088,1024]{1,0:T(8,128)(2,1)S(1)}, u32[]{:S(2)}) copy-start(bf16[1088,1024]{1,0:T(8,128)(2,1)S(1)} %get-tuple-element.241.refs_0_) | copy-start | bytes 6684676
  342.4 5.2 %copy-start.4 = (f32[1088,1024]{1,0:T(8,128)S(1)}, f32[1088,1024]{1,0:T(8,128)}, u32[]{:S(2)}) copy-start(f32[1088,1024]{1,0:T(8,128)} %get-tuple-element.144) | copy-start | bytes 13369348
  347.6 5.2 %copy-start.7 = (bf16[2,4,2,2,32,1024]{5,4,3,2,1,0:T(8,128)(2,1)S(1)}, bf16[2,4,2,2,32,1024]{5,4,3,2,1,0:T(8,128)(2,1)}, u32[]{:S(2)}) copy-start(bf16[2,4,2,2,32,1024]{5,4,3,2,1,0:T(8,128)(2,1)} %get-tuple-element.129) | copy-start | bytes 6291460
  352.8 6.3 %copy-start.3 = (f32[1088,1024]{1,0:T(8,128)S(1)}, f32[1088,1024]{1,0:T(8,128)}, u32[]{:S(2)}) copy-start(f32[1088,1024]{1,0:T(8,128)} %get-tuple-element.239.refs_14_) | copy-start | bytes 13369348
  352.8 6.3 %copy-start.5 = (bf16[1088,1024]{1,0:T(8,128)(2,1)S(1)}, bf16[1088,1024]{1,0:T(8,128)(2,1)}, u32[]{:S(2)}) copy-start(bf16[1088,1024]{1,0:T(8,128)(2,1)} %get-tuple-element.128.refs_1_.refs_4_) | copy-start | bytes 6684676
  480.3 7.8 %copy-start.10 = (f32[64,1024]{1,0:T(8,128)S(1)}, f32[64,1024]{1,0:T(8,128)}, u32[]{:S(2)}) copy-start(f32[64,1024]{1,0:T(8,128)} %get-tuple-element.150) | copy-start | bytes 786436
  483.2 5.7 %copy-start.15 = (f32[32,1024]{1,0:T(8,128)S(1)}, f32[32,1024]{1,0:T(8,128)}, u32[]{:S(2)}) copy-start(f32[32,1024]{1,0:T(8,128)} %get-tuple-element.443) | copy-start | bytes 393220
  483.2 6.3 %copy-start.14 = (f32[32,1024]{1,0:T(8,128)S(1)}, f32[32,1024]{1,0:T(8,128)}, u32[]{:S(2)}) copy-start(f32[32,1024]{1,0:T(8,128)} %get-tuple-element.444) | copy-start | bytes 393220
  483.2 7.0 %copy-start.13 = (f32[32,1024]{1,0:T(8,128)S(1)}, f32[32,1024]{1,0:T(8,128)}, u32[]{:S(2)}) copy-start(f32[32,1024]{1,0:T(8,128)} %get-tuple-element.445) | copy-start | bytes 393220
  483.2 7.6 %copy-start.12 = (f32[32,1024]{1,0:T(8,128)S(1)}, f32[32,1024]{1,0:T(8,128)}, u32[]{:S(2)}) copy-start(f32[32,1024]{1,0:T(8,128)} %get-tuple-element.446) | copy-start | bytes 393220
  483.2 8.3 %copy-start.9 = (f32[32,4096]{1,0:T(8,128)S(1)}, f32[32,4096]{1,0:T(8,128)}, u32[]{:S(2)}) copy-start(f32[32,4096]{1,0:T(8,128)} %get-tuple-element.453) | copy-start | bytes 1572868
  483.2 9.1 %copy-start.8 = (f32[128,1024]{1,0:T(8,128)S(1)}, f32[128,1024]{1,0:T(8,128)}, u32[]{:S(2)}) copy-start(f32[128,1024]{1,0:T(8,128)} %get-tuple-element.455) | copy-start | bytes 1572868
  483.2 9.8 %copy-start.16 = (f32[32,128]{1,0:T(8,128)S(1)}, f32[32,128]{1,0:T(8,128)}, u32[]{:S(2)}) copy-start(f32[32,128]{1,0:T(8,128)} %get-tuple-element.459) | copy-start | bytes 49156
